TPU v7x, 32 devices: a whole 2x2x4 slice. The times are simulated.
32 devices in a mesh: groups: 2 (over y), seq: 4 (over z), dp: 4 (over x, core).
Axes of the slice: x: 2, y: 2, z: 4, core: 2. Of those that a mesh axis runs over, the one named last changes fastest.
Arguments:
- dna_features: bfloat16 [8, 1024, 384], P(('groups', 'dp'), 'seq'), parts along dimension 0, may hold values from -6 to 6
- filter_weight: bfloat16 [5, 384, 768], P(None, None, 'dp'), may hold values from -0.03125 to 0.03125
- filter_bias: float32 [768], replicated, may hold values from -0.75 to 0.75
- norm_gain: float32 [768], replicated, may hold values from 0.1 to 1.9
- attend_weight: bfloat16 [768, 1280], replicated, may hold values from -5.8456715 to 5.8456715
- output_weight: bfloat16 [768, 768], replicated, may hold values from -0.21875 to 0.21875
- cotangent: bfloat16 [8, 512, 768], P(('groups', 'dp'), 'seq'), parts along dimension 0, may hold values from -0.1875 to 0.1875
Outputs:
- outputs: float32 [8, 512, 768], P(('groups', 'dp'), 'seq'), parts along dimension 0
- grad_attend: float32 [1536, 1280], P(('groups', 'seq')), parts along dimension 0
- grad_output: float32 [1536, 768], P(('groups', 'seq')), parts along dimension 0
- grad_gain: float32 [1536], P(('groups', 'seq')), parts along dimension 0
There are 2 independent parts, one for each index of `groups`. A program takes and returns all parts, laid end to end along the dimension named above; an argument that names none is the same for every part. Nothing has to cross between parts.
All inputs are finite; a program needn't handle non-finite values.
Results may differ from a plain program's by a relative error of at most 0.033.
Values may be sent and summed in bfloat16 or wider, within the bound.
No kernel may reach another device: no remote copies, remote signals or barrier semaphores. Data moves between devices by JAX's collectives and lax.ppermute only.
A program may use at most 64 MiB of HBM per device.

v0:
```python
import jax
import jax.numpy as jnp
from jax import lax
from jax.sharding import PartitionSpec as P

HEADS = 4
KEY_DIM = 64
VAL_DIM = 192


def extended(value, sides, width):
    for axis, dim in sides:
        devices, length = (lax.axis_size(axis), value.shape[dim])
        up = [(i, (i + 1) % devices) for i in range(devices - 1)]
        down = [(j, i) for i, j in up]
        last = lax.slice_in_dim(value, length - width, length, axis=dim)
        first = lax.slice_in_dim(value, 0, width, axis=dim)
        before = lax.ppermute(last, axis, up)
        after = lax.ppermute(first, axis, down)
        value = jnp.concatenate([before, value, after], axis=dim)
    return value


def filter_block(padded, weights, bias_part):
    count = padded.shape[1] - 4
    total = bias_part
    for offset in range(5):
        total = total + jnp.einsum(
            "spc,co->spo",
            padded[:, offset : offset + count],
            weights[offset],
            preferred_element_type=jnp.float32,
        )
    activ = jax.nn.gelu(total, approximate=True)
    activ = activ.reshape(activ.shape[0], count // 2, 2, activ.shape[2])
    return (0.5 * (activ[:, :, 0] + activ[:, :, 1])).astype(jnp.bfloat16)


def per_device(
    dna_features, filter_weight, filter_bias, norm_gain, attend_weight, output_weight, cotangent
):
    padded = extended(dna_features, (("seq", 1),), 2)
    hidden = filter_block(
        padded, lax.all_gather(filter_weight, "dp", axis=2, tiled=True), filter_bias
    )
    hidden = hidden[0]
    widen = hidden.astype(jnp.float32)
    nhat = widen * lax.rsqrt(jnp.mean(widen * widen, axis=-1, keepdims=True) + 1e-06)
    normed = (nhat * norm_gain).astype(jnp.bfloat16)
    tokens = normed.shape[0]
    query_width = HEADS * KEY_DIM
    value_width = HEADS * VAL_DIM
    scale = KEY_DIM ** (-0.5)
    projected = jnp.dot(normed, attend_weight, preferred_element_type=jnp.float32).astype(
        jnp.bfloat16
    )
    queries = projected[:, :query_width]
    keys_local = projected[:, query_width : 2 * query_width]
    values_local = projected[:, 2 * query_width :]
    keys_all, values_all = (
        lax.all_gather(keys_local, "seq", axis=0, tiled=True),
        lax.all_gather(values_local, "seq", axis=0, tiled=True),
    )
    total_len = keys_all.shape[0]
    query_heads = queries.reshape(tokens, HEADS, KEY_DIM)
    key_heads = keys_all.reshape(total_len, HEADS, KEY_DIM)
    value_heads = values_all.reshape(total_len, HEADS, VAL_DIM)
    scores = (
        jnp.einsum("qhd,khd->hqk", query_heads, key_heads, preferred_element_type=jnp.float32)
        * scale
    )
    peak = jnp.max(scores, axis=-1, keepdims=True)
    logsum = peak + jnp.log(jnp.sum(jnp.exp(scores - peak), axis=-1, keepdims=True))
    probs = jnp.exp(scores - logsum)
    probs_b = probs.astype(jnp.bfloat16)
    attended = (
        jnp.einsum("hqk,khd->qhd", probs_b, value_heads, preferred_element_type=jnp.float32)
        .astype(jnp.bfloat16)
        .reshape(tokens, value_width)
    )
    branch = lax.dot_general(
        attended, output_weight, (((1,), (1,)), ((), ())), preferred_element_type=jnp.float32
    )
    outputs = widen + branch
    upstream = cotangent[0]
    output_part = lax.dot_general(
        upstream, attended, (((0,), (0,)), ((), ())), preferred_element_type=jnp.float32
    )
    d_attn = jnp.dot(upstream, output_weight, preferred_element_type=jnp.float32).astype(
        jnp.bfloat16
    )
    d_heads = d_attn.reshape(tokens, HEADS, VAL_DIM)
    attn_heads = attended.reshape(tokens, HEADS, VAL_DIM)
    delta = jnp.sum(d_heads.astype(jnp.float32) * attn_heads.astype(jnp.float32), axis=-1)
    dprob = jnp.einsum("qhd,khd->hqk", d_heads, value_heads, preferred_element_type=jnp.float32)
    dscore = (probs * (dprob - delta.T[:, :, None])).astype(jnp.bfloat16)
    d_query = (
        jnp.einsum("hqk,khd->qhd", dscore, key_heads, preferred_element_type=jnp.float32) * scale
    )
    logsum_rows = logsum[:, :, 0].T
    logsum_all, delta_all = (
        lax.all_gather(logsum_rows, "seq", axis=0, tiled=True),
        lax.all_gather(delta, "seq", axis=0, tiled=True),
    )
    key_heads_local = keys_local.reshape(tokens, HEADS, KEY_DIM)
    value_heads_local = values_local.reshape(tokens, HEADS, VAL_DIM)
    piece_query = lax.all_gather(queries, "seq", axis=0, tiled=True)
    piece_grad = lax.all_gather(d_attn, "seq", axis=0, tiled=True)
    count = piece_query.shape[0]
    piece_qheads = piece_query.reshape(count, HEADS, KEY_DIM)
    piece_gheads = piece_grad.reshape(count, HEADS, VAL_DIM)
    piece_scores = (
        jnp.einsum(
            "qhd,khd->hqk", piece_qheads, key_heads_local, preferred_element_type=jnp.float32
        )
        * scale
    )
    piece_probs = jnp.exp(piece_scores - logsum_all.T[:, :, None])
    piece_probs_b = piece_probs.astype(jnp.bfloat16)
    piece_dprob = jnp.einsum(
        "qhd,khd->hqk", piece_gheads, value_heads_local, preferred_element_type=jnp.float32
    )
    piece_dscore = (piece_probs * (piece_dprob - delta_all.T[:, :, None])).astype(jnp.bfloat16)
    grad_keys = jnp.einsum(
        "hqk,qhd->khd", piece_dscore, piece_qheads, preferred_element_type=jnp.float32
    )
    grad_values = jnp.einsum(
        "hqk,qhd->khd", piece_probs_b, piece_gheads, preferred_element_type=jnp.float32
    )
    grad_keys, grad_values = (grad_keys, grad_values)
    d_proj = jnp.concatenate(
        [
            d_query.reshape(tokens, query_width),
            (grad_keys * scale).reshape(tokens, query_width),
            grad_values.reshape(tokens, value_width),
        ],
        axis=1,
    ).astype(jnp.bfloat16)
    d_normed = lax.dot_general(
        d_proj, attend_weight, (((1,), (1,)), ((), ())), preferred_element_type=jnp.float32
    )
    attend_part = lax.dot_general(
        normed, d_proj, (((0,), (0,)), ((), ())), preferred_element_type=jnp.float32
    )
    gain_part = jnp.sum(d_normed * nhat, axis=0)
    attend_share, output_share, gain_share = (
        lax.psum_scatter(
            attend_part.astype(jnp.bfloat16), "seq", scatter_dimension=0, tiled=True
        ).astype(jnp.float32),
        lax.psum_scatter(
            output_part.astype(jnp.bfloat16), "seq", scatter_dimension=0, tiled=True
        ).astype(jnp.float32),
        lax.psum_scatter(
            gain_part.astype(jnp.bfloat16), "seq", scatter_dimension=0, tiled=True
        ).astype(jnp.float32),
    )
    grad_attend, grad_output, grad_gain = lax.psum((attend_share, output_share, gain_share), "dp")
    return (outputs[None], grad_attend, grad_output, grad_gain)


def solution(mesh):
    return jax.shard_map(
        per_device,
        mesh=mesh,
        in_specs=(
            P(("groups", "dp"), "seq", None),
            P(None, None, "dp"),
            P(),
            P(),
            P(),
            P(),
            P(("groups", "dp"), "seq", None),
        ),
        out_specs=(
            P(("groups", "dp"), "seq", None),
            P(("groups", "seq"), None),
            P(("groups", "seq"), None),
            P(("groups", "seq")),
        ),
        check_vma=False,
    )
```

profile of v0, /device:TPU:0, one launch (start us, length us, event | category | flops | bytes accessed | tf_op | source)
XLA Modules:
  0.0 259.8 jit_solution(10152106171552187702)
XLA Ops:
  8.7 4.9 %collective-permute-start = (bf16[1,2,384]{2,1,0:T(2,128)(2,1)S(1)}, bf16[1,2,384]{2,1,0:T(2,128)(2,1)S(1)}, u32[]{:S(2)}, u32[]{:S(2)}) collective-permute-start(bf16[1,2,384]{2,1,0:T(2,128)(2,1)S(1)} %get-tuple-element.25), channel_id=1, source_target_pairs={{0,4},{4,8},{8,12},{1,5},{5,9},{9,13},{2,6},{6,10},{10,14},{3,7},{... | collective-permute-start | bytes 4616 | tf_op jit(solution)/shard_map/ppermute | solution.py:18
  14.9 1.7 convolution_convert_fusion.4
  16.9 2.2 collective-permute-done.1
  19.1 20.6 %all-gather.2.cloned.1.call-done = bf16[5,384,768]{1,2,0:T(8,128)(2,1)} async-done(((bf16[5,384,192]{1,2,0:T(8,128)(2,1)}), bf16[5,384,768]{1,2,0:T(8,128)(2,1)}) %all-gather.2.cloned.1.call-update) | async-done | bytes 2949136 | tf_op jit(solution)/shard_map/all_gather | solution.py:44
  49.3 13.9 %all_gather.23 = bf16[512,256]{1,0:T(8,128)(2,1)S(1)} all-gather(bf16[128,256]{1,0:T(8,128)(2,1)S(1)} %get-tuple-element.23), channel_id=1, replica_groups=mesh['groups'=2,'seq'=4,'dp'=4] {'seq'}, dimensions={0}, use_global_device_ids=true | all-gather | bytes 327680 | tf_op jit(solution)/shard_map/all_gather | solution.py:61
  66.6 19.3 %all_gather.22 = bf16[512,768]{1,0:T(8,128)(2,1)} all-gather(bf16[128,768]{1,0:T(8,128)(2,1)S(1)} %copy-done.5), channel_id=1, replica_groups=mesh['groups'=2,'seq'=4,'dp'=4] {'seq'}, dimensions={0}, use_global_device_ids=true | all-gather | bytes 983040 | tf_op jit(solution)/shard_map/all_gather | solution.py:62
  85.9 2.3 copy.36
  88.2 1.7 multiply_reduce_fusion
  92.0 2.4 copy.45
  94.5 25.1 %all_gather.26 = bf16[512,768]{1,0:T(8,128)(2,1)} all-gather(bf16[128,768]{1,0:T(8,128)(2,1)} %copy-done.4), channel_id=1, replica_groups=mesh['groups'=2,'seq'=4,'dp'=4] {'seq'}, dimensions={0}, use_global_device_ids=true | all-gather | bytes 983040 | tf_op jit(solution)/shard_map/all_gather | solution.py:108
  119.6 2.3 copy.42
  122.7 1.7 copy.43
  124.4 15.0 %all_gather.24 = bf16[512,256]{1,0:T(8,128)(2,1)} all-gather(bf16[128,256]{1,0:T(8,128)(2,1)S(1)} %get-tuple-element.24), channel_id=1, replica_groups=mesh['groups'=2,'seq'=4,'dp'=4] {'seq'}, dimensions={0}, use_global_device_ids=true | all-gather | bytes 327680 | tf_op jit(solution)/shard_map/all_gather | solution.py:107
  139.4 1.8 copy.40
  141.2 11.9 %all_gather.25 = f32[512,4]{0,1:T(4,128)S(1)} all-gather(f32[128,4]{0,1:T(4,128)S(1)} %bitcast.111), channel_id=1, replica_groups=mesh['groups'=2,'seq'=4,'dp'=4] {'seq'}, dimensions={0}, use_global_device_ids=true | all-gather | bytes 10240 | tf_op jit(solution)/shard_map/all_gather | solution.py:102
  153.1 11.9 %all_gather.27 = f32[512,4]{0,1:T(4,128)S(1)} all-gather(f32[128,4]{0,1:T(4,128)S(1)} %get-tuple-element.29), channel_id=1, replica_groups=mesh['groups'=2,'seq'=4,'dp'=4] {'seq'}, dimensions={0}, use_global_device_ids=true | all-gather | bytes 10240 | tf_op jit(solution)/shard_map/all_gather | solution.py:103
  167.4 2.2 convolution_convert_fusion.3
  169.6 1.8 fusion.16
  171.4 2.5 fusion.15
  174.0 2.1 convolution_convert_fusion
  177.3 1.8 fusion.12
  179.1 9.1 %all-reduce = bf16[768]{0:T(1024)(128)(2,1)S(1)} all-reduce(bf16[768]{0:T(1024)(128)(2,1)S(1)} %fusion.12), channel_id=4, replica_groups=mesh['groups'=2,'seq'=4,'dp'=4] {'seq'}, use_global_device_ids=true, to_apply=%region_9.0.clone | all-reduce | flops 768 | bytes 3072
  190.7 24.5 %reduce-scatter.5.cloned.1.call-done = bf16[192,1280]{1,0:T(8,128)(2,1)} async-done(((bf16[768,1280]{1,0:T(8,128)(2,1)}), bf16[192,1280]{1,0:T(8,128)(2,1)}) %reduce-scatter.5.cloned.1.call-update) | async-done | bytes 491536 | tf_op jit(solution)/shard_map/reduce_scatter | solution.py:147
  215.2 37.0 %all-reduce.3 = (f32[192,1280]{1,0:T(8,128)}, f32[192,768]{0,1:T(8,128)S(1)}, f32[192]{0:T(256)}) all-reduce(bf16[192,1280]{1,0:T(8,128)(2,1)} %reduce-scatter.5.cloned.1.call-done, bf16[192,768]{0,1:T(8,128)(2,1)S(1)} %copy.46, f32[192]{0:T(256)S(1)} %dynamic-slice_convert_fusion), channel_id=1, replica_groups=mesh['groups'=2,'seq'=4,'dp'=4] {'dp'}, use_global_device_ids=true, to_apply=%region_5.0 | all-reduce | flops 393408 | bytes 2360832 | tf_op jit(solution)/shard_map/psum | solution.py:157
  (80 shorter events, 25.3 us)
Async XLA Ops:
  7.2 40.9 %copy-start = (bf16[768,1280]{1,0:T(8,128)(2,1)S(1)}, bf16[768,1280]{1,0:T(8,128)(2,1)}, u32[]{:S(2)}) copy-start(bf16[768,1280]{1,0:T(8,128)(2,1)} %param.11) | copy-start | bytes 5898244
  7.2 9.5 %copy-start.3 = (bf16[1,256,384]{2,1,0:T(8,128)(2,1)S(1)}, bf16[1,256,384]{2,1,0:T(8,128)(2,1)}, u32[]{:S(2)}) copy-start(bf16[1,256,384]{2,1,0:T(8,128)(2,1)} %param.7) | copy-start | bytes 589828
  7.2 32.5 %all-gather.2.cloned.1.call-start = ((), (), s32[]{:S(2)}) async-start(), calls=%async_computation.2 | async-start | bytes 3686400 | tf_op jit(solution)/shard_map/all_gather | solution.py:44
  7.9 181.6 %reduce-scatter.7.cloned.1.call-start = ((), (), s32[]{:S(2)}) async-start(), calls=%async_computation.4 | async-start | bytes 1474560
  8.7 34.3 %collective-permute-start = (bf16[1,2,384]{2,1,0:T(2,128)(2,1)S(1)}, bf16[1,2,384]{2,1,0:T(2,128)(2,1)S(1)}, u32[]{:S(2)}, u32[]{:S(2)}) collective-permute-start(bf16[1,2,384]{2,1,0:T(2,128)(2,1)S(1)} %get-tuple-element.25), channel_id=1, source_target_pairs={{0,4},{4,8},{8,12},{1,5},{5,9},{9,13},{2,6},{6,10},{10,14},{3,7},{... | collective-permute-start | bytes 4616 | tf_op jit(solution)/shard_map/ppermute | solution.py:18
  13.6 5.5 %collective-permute-start.1 = (bf16[1,2,384]{2,1,0:T(2,128)(2,1)S(1)}, bf16[1,2,384]{2,1,0:T(2,128)(2,1)S(1)}, u32[]{:S(2)}, u32[]{:S(2)}) collective-permute-start(bf16[1,2,384]{2,1,0:T(2,128)(2,1)S(1)} %get-tuple-element.26), channel_id=1, source_target_pairs={{4,0},{8,4},{12,8},{5,1},{9,5},{13,9},{6,2},{10,6},{14,10},{7,3},{... | collective-permute-start | bytes 4616 | tf_op jit(solution)/shard_map/ppermute | solution.py:19
  16.6 26.3 %copy-start.4 = (bf16[128,768]{1,0:T(8,128)(2,1)}, bf16[128,768]{1,0:T(8,128)(2,1)S(1)}, u32[]{:S(2)}) copy-start(bf16[128,768]{1,0:T(8,128)(2,1)S(1)} %convolution_convert_fusion.4) | copy-start | bytes 589828
  16.7 26.3 %copy-start.19 = (f32[768]{0:T(1024)S(1)}, f32[768]{0:T(1024)}, u32[]{:S(2)}) copy-start(f32[768]{0:T(1024)} %param.9) | copy-start | bytes 9220
  19.1 20.6 %copy-start.11 = (bf16[1,258,384]{2,1,0:T(8,128)(2,1)}, bf16[1,258,384]{2,1,0:T(8,128)(2,1)S(1)}, u32[]{:S(2)}) copy-start(bf16[1,258,384]{2,1,0:T(8,128)(2,1)S(1)} %constant_dynamic-update-slice_fusion) | copy-start | bytes 594436
  39.7 3.2 %copy-start.8 = (bf16[5,384,768]{1,2,0:T(8,128)(2,1)S(1)}, bf16[5,384,768]{1,2,0:T(8,128)(2,1)}, u32[]{:S(2)}) copy-start(bf16[5,384,768]{1,2,0:T(8,128)(2,1)} %all-gather.2.cloned.1.call-done) | copy-start | bytes 8847364
  45.7 2.4 copy-start.15
  48.1 1.2 copy-start.17
  64.8 1.8 copy-start.5
  88.2 2.3 copy-start.9
  94.4 120.8 %reduce-scatter.5.cloned.1.call-start = ((), (), s32[]{:S(2)}) async-start(), calls=%async_computation.3 | async-start | bytes 2457600 | tf_op jit(solution)/shard_map/reduce_scatter | solution.py:147
  166.4 1.0 copy-start.1
  171.4 4.6 %copy-start.13 = (bf16[4,64,128]{2,1,0:T(8,128)(2,1)}, bf16[4,64,128]{2,1,0:T(8,128)(2,1)S(1)}, u32[]{:S(2)}) copy-start(bf16[4,64,128]{2,1,0:T(8,128)(2,1)S(1)} %fusion.16) | copy-start | bytes 196612
  171.4 2.5 copy-start.10
  171.4 2.5 copy-start.16
  171.4 2.5 copy-start.18
  173.9 2.1 copy-start.14
  173.9 2.1 copy-start.20
  176.1 12.2 %copy-start.2 = (bf16[768,768]{1,0:T(8,128)(2,1)S(1)}, bf16[768,768]{1,0:T(8,128)(2,1)}, u32[]{:S(2)}) copy-start(bf16[768,768]{1,0:T(8,128)(2,1)} %param.12) | copy-start | bytes 3538948
  176.1 12.2 %copy-start.7 = (bf16[4,192,128]{2,1,0:T(8,128)(2,1)S(1)}, bf16[4,192,128]{2,1,0:T(8,128)(2,1)}, u32[]{:S(2)}) copy-start(bf16[4,192,128]{2,1,0:T(8,128)(2,1)} %copy-done.6) | copy-start | bytes 589828
  (2 other events, 1.6 us)
Sparse Core Ops, SparseCore 0:
  9.6 30.1 all-gather.1
  94.5 36.3 reduce-scatter.6
  176.2 38.9 reduce-scatter.4
where the time goes:
time: 261 us; the launch traced here: 260 us
  blocking collectives  143 us (55%)
  waiting for transfers between devices  48.1 us (18%)
  matrix products  25.2 us (10%)
  local copies, waits for them, and re-layouts  21.7 us (8%)
  between operations  14.8 us (6%)
  starting transfers between devices  6.32 us (2%)
    psum x1, blocking collectives, per_device(): lax.psum((attend_share, output_share, gain_share), 'dp')  37 us
    all_gather x1, blocking collectives, per_device(): piece_grad = lax.all_gather(d_attn, 'seq', axis=0, tiled=True)  25.1 us
    reduce_scatter x1, waiting for transfers between devices, per_device(): lax.psum_scatter(attend_part.astype(jnp.bfloat16), 'seq', scatter_dimensi...  24.5 us
    all_gather x1, waiting for transfers between devices, per_device(): lax.all_gather(filter_weight, 'dp', axis=2, tiled=True)  20.6 us
    all_gather x1, blocking collectives, per_device(): lax.all_gather(values_local, 'seq', axis=0, tiled=True)  19.3 us
    all_gather x1, blocking collectives, per_device(): piece_query = lax.all_gather(queries, 'seq', axis=0, tiled=True)  15 us
    all_gather x1, blocking collectives, per_device(): lax.all_gather(keys_local, 'seq', axis=0, tiled=True)  13.9 us
    all_gather x1, blocking collectives, per_device(): lax.all_gather(delta, 'seq', axis=0, tiled=True)  11.9 us
  transfers between devices with their start and end apart: 5, of which 3 were waited for; matrix products, arithmetic and copies ran while one was open for 10% of the time, Pallas kernels for 0%

commit v1 on v0

--- a/solution.py
+++ b/solution.py
@@ -1,6 +1,10 @@
+import functools
+
 import jax
 import jax.numpy as jnp
 from jax import lax
+from jax.experimental import pallas as pl
+from jax.experimental.pallas import tpu as pltpu
 from jax.sharding import PartitionSpec as P
 
 HEADS = 4
@@ -158,9 +162,236 @@
     return (outputs[None], grad_attend, grad_output, grad_gain)
 
 
+F32, BF16 = jnp.float32, jnp.bfloat16
+SEQ, DP = 4, 4
+TOK = 128
+LEN = SEQ * TOK
+CIN, WIDTH = 384, 768
+SHARD = WIDTH // DP
+ROWS = WIDTH // SEQ
+QW, VW = HEADS * KEY_DIM, HEADS * VAL_DIM
+PROJ = 2 * QW + VW
+SCALE = KEY_DIM**-0.5
+NN = (((1,), (0,)), ((), ()))
+NT = (((1,), (1,)), ((), ()))
+TN = (((0,), (0,)), ((), ()))
+
+
+def mm(left, right, dims=NN):
+    return lax.dot_general(left, right, dims, preferred_element_type=F32)
+
+
+def half_gelu(value):
+    inner = 0.7978845608028654 * (value + 0.044715 * value * value * value)
+    return 0.5 * value * (1.0 + jnp.tanh(inner))
+
+
+def ring(value, step):
+    return lax.ppermute(value, "seq", [(i, (i + step) % SEQ) for i in range(SEQ)])
+
+
+def swap(value, bit):
+    return lax.ppermute(value, "dp", [(i, i ^ bit) for i in range(DP)])
+
+
+def put_shards(taps, mine, other, core):
+    for tap in range(5):
+        lanes = slice(tap * CIN, (tap + 1) * CIN)
+        rows = slice(tap * SHARD, (tap + 1) * SHARD)
+        taps[pl.ds(core * SHARD, SHARD), lanes] = mine[rows, :]
+        taps[pl.ds((1 - core) * SHARD, SHARD), lanes] = other[rows, :]
+
+
+def filtered_half(windows, taps, bias):
+    even = mm(windows[:, : 5 * CIN], taps[...], NT) + bias
+    odd = mm(windows[:, CIN:], taps[...], NT) + bias
+    return (0.5 * (half_gelu(even) + half_gelu(odd))).astype(BF16)
+
+
+def near_kernel(f0, fa, fb, fc, w0, w1, bias, windows, hid, positions, taps):
+    z, d = lax.axis_index("seq"), lax.axis_index("dp")
+    chunk = 2 * TOK
+    for g in range(CIN // 128):
+        positions[g, 0:8, :] = jnp.zeros((8, 128), F32)
+        positions[g, 8 + 2 * LEN :, :] = jnp.zeros((8, 128), F32)
+        for ref, off in ((f0, 0), (fa, 3), (fb, 1), (fc, 2)):
+            start = pl.multiple_of(lax.rem(z + off, SEQ) * chunk + 8, 8)
+            positions[g, pl.ds(start, chunk), :] = ref[:, g * 128 : (g + 1) * 128].astype(F32)
+        for k in range(6):
+            at = k * CIN + g * 128
+            windows[:, at : at + 128] = positions[g, pl.ds(6 + k, LEN, stride=2), :].astype(BF16)
+    core = lax.rem(d, 2)
+    put_shards(taps, w0, w1, core)
+    hid[...] = filtered_half(windows, taps, bias[pl.ds(d // 2, 1), :])
+
+
+def forward_kernel(
+    windows, hid_near, w2, w3, bias, gain, aw, ow, outputs, normed_t, proj, probs_t, att_t, taps, hid, normed
+):
+    z, d = lax.axis_index("seq"), lax.axis_index("dp")
+    side, core = d // 2, lax.rem(d, 2)
+    half = WIDTH // 2
+    put_shards(taps, w2, w3, core)
+    hid[side] = hid_near[...]
+    hid[1 - side] = filtered_half(windows, taps, bias[pl.ds(1 - side, 1), :])
+    low, high = hid[0].astype(F32), hid[1].astype(F32)
+    square = jnp.sum(low * low, axis=1, keepdims=True) + jnp.sum(high * high, axis=1, keepdims=True)
+    inv = lax.rsqrt(square * (1.0 / WIDTH) + 1e-06)
+    normed[:, :half] = (low * inv * gain[:, :half]).astype(BF16)
+    normed[:, half:] = (high * inv * gain[:, half:]).astype(BF16)
+    proj[...] = mm(normed[...], aw[...]).astype(BF16)
+    for h in range(HEADS):
+        q = proj[:, h * KEY_DIM : (h + 1) * KEY_DIM]
+        k = proj[:, QW + h * KEY_DIM : QW + (h + 1) * KEY_DIM]
+        v = proj[:, 2 * QW + h * VAL_DIM : 2 * QW + (h + 1) * VAL_DIM]
+        scores = mm(k, q, NT) * SCALE
+        top = jnp.max(scores, axis=0, keepdims=True)
+        weight = jnp.exp(scores - top)
+        total = jnp.sum(weight, axis=0, keepdims=True)
+        probs = (weight * (1.0 / total)).astype(BF16)
+        probs_t[h] = probs
+        att_t[h * VAL_DIM : (h + 1) * VAL_DIM, :] = mm(v, probs, TN).astype(BF16)
+    for at in range(SEQ):
+
+        @pl.when(z == at)
+        def _():
+            rows = slice(at * TOK, (at + 1) * TOK)
+            branch = mm(att_t[:, rows], ow[...], (((0,), (1,)), ((), ())))
+            outputs[:, :half] = branch[:, :half] + hid[0, rows, :].astype(F32)
+            outputs[:, half:] = branch[:, half:] + hid[1, rows, :].astype(F32)
+            normed_t[...] = normed[:, at * ROWS : (at + 1) * ROWS].T
+
+
+def backward_kernel(
+    c0, ca, cb, cc, normed_t, proj, probs_t, att_t, gain, aw, ow, keep, send, cot, cot_t, grad, d_query, d_rest
+):
+    z, d = lax.axis_index("seq"), lax.axis_index("dp")
+    core = lax.rem(d, 2)
+    for ref, off in ((c0, 0), (ca, 3), (cb, 1), (cc, 2)):
+        start = pl.multiple_of(lax.rem(z + off, SEQ) * TOK, TOK)
+        cot[pl.ds(start, TOK), :] = ref[...]
+    for at in range(SEQ):
+
+        @pl.when(z == at)
+        def _():
+            cot_t[...] = cot[:, at * ROWS : (at + 1) * ROWS].T
+
+    grad[...] = mm(cot[...], ow[...]).astype(BF16)
+    out_part = mm(cot_t[...], att_t[...], NT)
+    for h in range(HEADS):
+        q = proj[:, h * KEY_DIM : (h + 1) * KEY_DIM]
+        k = proj[:, QW + h * KEY_DIM : QW + (h + 1) * KEY_DIM]
+        v = proj[:, 2 * QW + h * VAL_DIM : 2 * QW + (h + 1) * VAL_DIM]
+        g = grad[:, h * VAL_DIM : (h + 1) * VAL_DIM]
+        probs = probs_t[h].astype(F32)
+        product = mm(v, g, NT) * probs
+        delta = jnp.sum(product, axis=0, keepdims=True)
+        dscore = (product - probs * delta).astype(BF16)
+        d_query[h * KEY_DIM : (h + 1) * KEY_DIM, :] = (mm(k, dscore, TN) * SCALE).astype(BF16)
+        d_rest[:, h * KEY_DIM : (h + 1) * KEY_DIM] = (mm(dscore, q) * SCALE).astype(BF16)
+        d_rest[:, QW + h * VAL_DIM : QW + (h + 1) * VAL_DIM] = mm(probs_t[h], g).astype(BF16)
+    query_part = mm(normed_t[...], d_query[...], NT)
+    rest_part = mm(normed_t[...], d_rest[...])
+    here = pl.multiple_of(z * ROWS, ROWS)
+    mixed = jnp.sum(query_part * aw[pl.ds(here, ROWS), :QW].astype(F32), axis=1, keepdims=True)
+    mixed = mixed + jnp.sum(rest_part * aw[pl.ds(here, ROWS), QW:].astype(F32), axis=1, keepdims=True)
+    gain_part = jnp.broadcast_to(mixed, (ROWS, 128)).T[0:1, :] / gain[pl.ds(z, 1), :]
+    split = PROJ // 2 - QW
+
+    def write(ref, side):
+        if side == 0:
+            ref[:ROWS, :QW] = query_part.astype(ref.dtype)
+            ref[:ROWS, QW : PROJ // 2] = rest_part[:, :split].astype(ref.dtype)
+        else:
+            ref[:ROWS, : PROJ // 2] = rest_part[:, split:].astype(ref.dtype)
+        ref[:ROWS, PROJ // 2 :] = out_part[:, side * VW // 2 : (side + 1) * VW // 2].astype(ref.dtype)
+        ref[ROWS:, :] = jnp.zeros((16, PROJ // 2 + VW // 2), ref.dtype)
+        ref[ROWS : ROWS + 1, :ROWS] = gain_part.astype(ref.dtype)
+
+    for at in range(2):
+
+        @pl.when(core == at)
+        def _():
+            write(keep, at)
+            write(send, 1 - at)
+
+
+def kernel_call(body, outs, scratch, flops, bytes_accessed, *args):
+    return pl.pallas_call(
+        body,
+        out_shape=[jax.ShapeDtypeStruct(s, t) for s, t in outs],
+        scratch_shapes=[pltpu.VMEM(s, t) for s, t in scratch],
+        compiler_params=pltpu.CompilerParams(vmem_limit_bytes=40 << 20),
+        cost_estimate=pl.CostEstimate(flops=flops, bytes_accessed=bytes_accessed, transcendentals=0),
+    )(*args)
+
+
+def per_device_fast(
+    dna_features, filter_weight, filter_bias, norm_gain, attend_weight, output_weight, cotangent
+):
+    d = lax.axis_index("dp")
+    f0, c0 = dna_features[0], cotangent[0]
+    w0 = filter_weight.transpose(0, 2, 1).reshape(5 * SHARD, CIN)
+    w2 = swap(w0, 2)
+    w1 = swap(w0, 1)
+    fa, fb = ring(f0, 1), ring(f0, SEQ - 1)
+    fc = ring(fa, 1)
+    w2, fa, fb, fc = lax.optimization_barrier((w2, fa, fb, fc))
+    w3 = swap(w2, 1)
+    bias = filter_bias.reshape(2, WIDTH // 2)
+    gain = norm_gain.reshape(1, WIDTH)
+    windows, hid_near = kernel_call(
+        near_kernel,
+        [((LEN, 6 * CIN), BF16), ((LEN, WIDTH // 2), BF16)],
+        [((CIN // 128, 16 + 2 * LEN, 128), F32), ((2 * SHARD, 5 * CIN), BF16)],
+        2 * 2 * LEN * 5 * CIN * WIDTH // 2, 4 << 20,
+        f0, fa, fb, fc, w0, w1, bias,
+    )
+    c0 = lax.optimization_barrier((c0, fc))[0]
+    ca, cb = ring(c0, 1), ring(c0, SEQ - 1)
+    cc = ring(ca, 1)
+    outputs, normed_t, proj, probs_t, att_t = kernel_call(
+        forward_kernel,
+        [
+            ((TOK, WIDTH), F32),
+            ((ROWS, LEN), BF16),
+            ((LEN, PROJ), BF16),
+            ((HEADS, LEN, LEN), BF16),
+            ((VW, LEN), BF16),
+        ],
+        [((2 * SHARD, 5 * CIN), BF16), ((2, LEN, WIDTH // 2), BF16), ((LEN, WIDTH), BF16)],
+        5 << 30, 8 << 20,
+        windows, hid_near, w2, w3, bias, gain, attend_weight, output_weight,
+    )
+    keep, send = kernel_call(
+        backward_kernel,
+        [((ROWS + 16, (PROJ + VW) // 2), F32), ((ROWS + 16, (PROJ + VW) // 2), BF16)],
+        [
+            ((LEN, WIDTH), BF16),
+            ((ROWS, LEN), BF16),
+            ((LEN, VW), BF16),
+            ((QW, LEN), BF16),
+            ((LEN, QW + VW), BF16),
+        ],
+        5 << 30, 8 << 20,
+        c0, ca, cb, cc, normed_t, proj, probs_t, att_t, norm_gain.reshape(SEQ, ROWS), attend_weight, output_weight,
+    )
+    part = (keep + swap(send, 1).astype(F32)).astype(BF16)
+    whole = (part.astype(F32) + swap(part, 2).astype(F32)).astype(BF16)
+    other = swap(whole, 1)
+    first = lax.rem(d, 2) == 0
+    low = jnp.where(first, whole, other).astype(F32)
+    high = jnp.where(first, other, whole).astype(F32)
+    cut = PROJ // 2
+    grad_attend = jnp.concatenate([low[:ROWS, :cut], high[:ROWS, :cut]], axis=1)
+    grad_output = jnp.concatenate([low[:ROWS, cut:], high[:ROWS, cut:]], axis=1)
+    return outputs[None], grad_attend, grad_output, low[ROWS, :ROWS]
+
+
 def solution(mesh):
+    small = mesh.shape["seq"] == SEQ and mesh.shape["dp"] == DP
     return jax.shard_map(
-        per_device,
+        per_device_fast if small else per_device,
         mesh=mesh,
         in_specs=(
             P(("groups", "dp"), "seq", None),

time: 261 us -> 64.4 us (0.25)
  blocking collectives: 143 us -> 0 us
  matrix products: 25.2 us -> 0 us
  waiting for transfers between devices: 48.1 us -> 28.8 us
  local copies, waits for them, and re-layouts: 21.7 us -> 4.9 us
  Pallas kernels: 0 us -> 15.3 us
  between operations: 14.8 us -> 0.78 us
  starting transfers between devices: 6.32 us -> 12.1 us
    all_gather x6 -> x0, blocking collectives: 97.1 us -> none  [the longest x1 25.1 us: per_device(): piece_grad = lax.all_gather(d_attn, 'seq', axis=0, tiled=True)]
    psum x1 -> x0, blocking collectives: 37 us -> none  [per_device(): lax.psum((attend_share, output_share, gain_share), 'dp')]
    ppermute x2 -> x12, waiting for transfers between devices: 2.23 us -> 28.8 us  [the longest x6 14.5 us: ring(): lax.ppermute(value, 'seq', [(i, (i + step) % SEQ) for i in range(SEQ)])]
    dot_general x17 -> x0, matrix products: 25.2 us -> none  [the longest x5 5.35 us: filter_block(): jnp.einsum('spc,co->spo', padded[:, offset:offset + count], weights[offse...]
    reduce_scatter x1 -> x0, waiting for transfers between devices: 24.5 us -> none  [per_device(): lax.psum_scatter(attend_part.astype(jnp.bfloat16), 'seq', scatter_dimensi...]
    all_gather x1 -> x0, waiting for transfers between devices: 20.6 us -> none  [per_device(): lax.all_gather(filter_weight, 'dp', axis=2, tiled=True)]
    pallas_call x0 -> x3, Pallas kernels: none -> 15.3 us  [kernel_call(): pl.pallas_call(body, out_shape=[jax.ShapeDtypeStruct(s, t) for s, t in ou...]
    unnamed x1 -> x0, blocking collectives: 9.08 us -> none
  transfers between devices with their start and end apart: 5 -> 12, of which waited for: 3 -> 7; matrix products, arithmetic and copies ran while one was open for 10% -> 3% of each run, Pallas kernels for 0% -> 16%
where the time goes in v1:
time: 64.4 us; the launch traced here: 64.1 us
  waiting for transfers between devices  28.8 us (45%)
  Pallas kernels  15.3 us (24%)
  starting transfers between devices  12.1 us (19%)
  local copies, waits for them, and re-layouts  4.9 us (8%)
  other arithmetic  2.23 us (3%)
  between operations  0.78 us (1%)
    pallas_call x3, Pallas kernels, kernel_call(): pl.pallas_call(body, out_shape=[jax.ShapeDtypeStruct(s, t) for s, t in ou...  15.3 us
    ppermute x6, waiting for transfers between devices, ring(): lax.ppermute(value, 'seq', [(i, (i + step) % SEQ) for i in range(SEQ)])  14.5 us
    ppermute x6, waiting for transfers between devices, swap(): return lax.ppermute(value, 'dp', [(i, i ^ bit) for i in range(DP)])  14.2 us
    ppermute x6, starting transfers between devices, ring(): lax.ppermute(value, 'seq', [(i, (i + step) % SEQ) for i in range(SEQ)])  7.71 us
    ppermute x6, starting transfers between devices, swap(): return lax.ppermute(value, 'dp', [(i, i ^ bit) for i in range(DP)])  4.36 us
    unnamed x10, local copies, waits for them, and re-layouts  2.06 us
  transfers between devices with their start and end apart: 12, of which 7 were waited for; matrix products, arithmetic and copies ran while one was open for 3% of the time, Pallas kernels for 16%

profile of v1, /device:TPU:0, one launch (start us, length us, event | category | flops | bytes accessed | tf_op | source)
XLA Modules:
  0.0 64.1 jit_solution(10059544623953741006)
XLA Ops:
  0.6 3.0 %collective-permute-start = (bf16[960,384]{1,0:T(8,128)(2,1)}, bf16[960,384]{1,0:T(8,128)(2,1)S(1)}, u32[]{:S(2)}, u32[]{:S(2)}) collective-permute-start(bf16[960,384]{1,0:T(8,128)(2,1)} %bitcast.7), channel_id=1, source_target_pairs={{0,2},{1,3},{2,0},{3,1},{4,6},{5,7},{6,4},{7,5},{8,10},{9,11},{10,... | collective-permute-start | bytes 2211848 | tf_op jit(solution)/shard_map/ppermute | solution.py:194
  3.6 1.6 %collective-permute-start.1 = (bf16[256,384]{1,0:T(8,128)(2,1)}, bf16[256,384]{1,0:T(8,128)(2,1)S(1)}, u32[]{:S(2)}, u32[]{:S(2)}) collective-permute-start(bf16[256,384]{1,0:T(8,128)(2,1)} %bitcast.10), channel_id=1, source_target_pairs={{0,4},{4,8},{8,12},{12,0},{1,5},{5,9},{9,13},{13,1},{2,6},{6,10},{... | collective-permute-start | bytes 589832 | tf_op jit(solution)/shard_map/ppermute | solution.py:190
  5.2 2.2 %collective-permute-start.2 = (bf16[256,384]{1,0:T(8,128)(2,1)}, bf16[256,384]{1,0:T(8,128)(2,1)S(1)}, u32[]{:S(2)}, u32[]{:S(2)}) collective-permute-start(bf16[256,384]{1,0:T(8,128)(2,1)} %bitcast.11), channel_id=1, source_target_pairs={{0,12},{4,0},{8,4},{12,8},{1,13},{5,1},{9,5},{13,9},{2,14},{6,2},{... | collective-permute-start | bytes 589832 | tf_op jit(solution)/shard_map/ppermute | solution.py:190
  7.5 6.1 %collective-permute-done.1.fa = bf16[256,384]{1,0:T(8,128)(2,1)S(1)} collective-permute-done((bf16[256,384]{1,0:T(8,128)(2,1)}, bf16[256,384]{1,0:T(8,128)(2,1)S(1)}, u32[]{:S(2)}, u32[]{:S(2)}) %collective-permute-start.1) | collective-permute-done | bytes 196640 | tf_op jit(solution)/shard_map/ppermute | solution.py:190
  13.5 2.6 %collective-permute-done.2.fb = bf16[256,384]{1,0:T(8,128)(2,1)S(1)} collective-permute-done((bf16[256,384]{1,0:T(8,128)(2,1)}, bf16[256,384]{1,0:T(8,128)(2,1)S(1)}, u32[]{:S(2)}, u32[]{:S(2)}) %collective-permute-start.2) | collective-permute-done | bytes 196640 | tf_op jit(solution)/shard_map/ppermute | solution.py:190
  16.1 4.8 %collective-permute-done.3.fc = bf16[256,384]{1,0:T(8,128)(2,1)S(1)} collective-permute-done((bf16[256,384]{1,0:T(8,128)(2,1)S(1)}, bf16[256,384]{1,0:T(8,128)(2,1)S(1)}, u32[]{:S(2)}, u32[]{:S(2)}) %collective-permute-start.3) | collective-permute-done | bytes 196640 | tf_op jit(solution)/shard_map/ppermute | solution.py:190
  21.0 1.2 %collective-permute-start.6 = (bf16[128,768]{1,0:T(8,128)(2,1)}, bf16[128,768]{1,0:T(8,128)(2,1)S(1)}, u32[]{:S(2)}, u32[]{:S(2)}) collective-permute-start(bf16[128,768]{1,0:T(8,128)(2,1)} %bitcast.13), channel_id=1, source_target_pairs={{0,4},{4,8},{8,12},{12,0},{1,5},{5,9},{9,13},{13,1},{2,6},{6,10},{... | collective-permute-start | bytes 589832 | tf_op jit(solution)/shard_map/ppermute | solution.py:190
  22.2 0.7 %reshape.22.gain = f32[1,768]{1,0:T(1,128)S(1)} reshape(f32[768]{0:T(1024)} %param.10) | data formatting | bytes 6144 | tf_op jit(solution)/shard_map/reshape | solution.py:342
  22.9 0.8 %reshape.23.gain = f32[4,192]{1,0:T(4,128)S(1)} reshape(f32[768]{0:T(1024)} %param.10) | data formatting | bytes 6144 | tf_op jit(solution)/shard_map/reshape | solution.py:377
  23.6 0.7 %reshape.21.bias = f32[2,384]{1,0:T(2,128)S(1)} reshape(f32[768]{0:T(1024)} %param.9) | data formatting | bytes 6144 | tf_op jit(solution)/shard_map/reshape | solution.py:341
  24.3 2.6 %collective-permute-start.7 = (bf16[128,768]{1,0:T(8,128)(2,1)}, bf16[128,768]{1,0:T(8,128)(2,1)S(1)}, u32[]{:S(2)}, u32[]{:S(2)}) collective-permute-start(bf16[128,768]{1,0:T(8,128)(2,1)} %bitcast.14), channel_id=1, source_target_pairs={{0,12},{4,0},{8,4},{12,8},{1,13},{5,1},{9,5},{13,9},{2,14},{6,2},{... | collective-permute-start | bytes 589832 | tf_op jit(solution)/shard_map/ppermute | solution.py:190
  27.0 1.1 %copy-done.2 = bf16[5,384,192]{1,2,0:T(8,128)(2,1)S(1)} copy-done((bf16[5,384,192]{1,2,0:T(8,128)(2,1)S(1)}, bf16[5,384,192]{1,2,0:T(8,128)(2,1)}, u32[]{:S(2)}) %copy-start.2) | copy-done | bytes 737304
  28.1 0.9 %copy-done.3 = bf16[1,256,384]{2,1,0:T(8,128)(2,1)S(1)} copy-done((bf16[1,256,384]{2,1,0:T(8,128)(2,1)S(1)}, bf16[1,256,384]{2,1,0:T(8,128)(2,1)}, u32[]{:S(2)}) %copy-start.3) | copy-done | bytes 196632
  29.0 2.9 %shard_map.102 = (bf16[512,2304]{1,0:T(8,128)(2,1)S(1)}, bf16[512,384]{1,0:T(8,128)(2,1)S(1)}) custom-call(bf16[256,384]{1,0:T(8,128)(2,1)S(1)} %bitcast.12, bf16[256,384]{1,0:T(8,128)(2,1)S(1)} %collective-permute-done.1.fa, bf16[256,384]{1,0:T(8,128)(2,1)S(1)} %collective-permute-done.2.fb, bf16[256,384]{1,0:T(8,128)(2,1)S(1)} %collective-permute-done.3.fc, ...), custom_call_target="tpu_custom_call" | custom-call | flops 1509949440 | bytes 4194304 | tf_op jit(solution)/shard_map/pallas_call | solution.py:320
  32.1 7.4 %shard_map.103 = (f32[128,768]{1,0:T(8,128)}, bf16[192,512]{1,0:T(8,128)(2,1)S(1)}, bf16[512,1280]{1,0:T(8,128)(2,1)S(1)}, bf16[4,512,512]{2,1,0:T(8,128)(2,1)S(1)}, bf16[768,512]{1,0:T(8,128)(2,1)S(1)}) custom-call(bf16[512,2304]{1,0:T(8,128)(2,1)S(1)} %get-tuple-element.21.windows, bf16[512,384]{1,0:T(8,128)(2,1)S(1)} %get-tuple-element.22.hid_near, ...), custom_call_target="tpu_custom_call" | custom-call | flops 5368709120 | bytes 8388608 | tf_op jit(solution)/shard_map/pallas_call | solution.py:320
  39.5 1.0 %collective-permute-done.8.cc = bf16[128,768]{1,0:T(8,128)(2,1)S(1)} collective-permute-done((bf16[128,768]{1,0:T(8,128)(2,1)S(1)}, bf16[128,768]{1,0:T(8,128)(2,1)S(1)}, u32[]{:S(2)}, u32[]{:S(2)}) %collective-permute-start.8) | collective-permute-done | bytes 196640 | tf_op jit(solution)/shard_map/ppermute | solution.py:190
  40.5 5.0 %shard_map.104 = (f32[208,1024]{1,0:T(8,128)S(1)}, bf16[208,1024]{1,0:T(8,128)(2,1)S(1)}) custom-call(bf16[128,768]{1,0:T(8,128)(2,1)S(1)} %bitcast.15, bf16[128,768]{1,0:T(8,128)(2,1)S(1)} %collective-permute-done.6.ca, bf16[128,768]{1,0:T(8,128)(2,1)S(1)} %collective-permute-done.7.cb, bf16[128,768]{1,0:T(8,128)(2,1)S(1)} %collective-permute-done.8.cc, ...), custom_call_target="tpu_custom_call" | custom-call | flops 5368709120 | bytes 8388608 | tf_op jit(solution)/shard_map/pallas_call | solution.py:320
  45.6 1.8 %collective-permute-done.9 = bf16[208,1024]{1,0:T(8,128)(2,1)S(1)} collective-permute-done((bf16[208,1024]{1,0:T(8,128)(2,1)S(1)}, bf16[208,1024]{1,0:T(8,128)(2,1)S(1)}, u32[]{:S(2)}, u32[]{:S(2)}) %collective-permute-start.9) | collective-permute-done | bytes 426016 | tf_op jit(solution)/shard_map/ppermute | solution.py:194
  47.5 1.2 %collective-permute-start.10 = (bf16[208,1024]{1,0:T(8,128)(2,1)S(1)}, bf16[208,1024]{1,0:T(8,128)(2,1)S(1)}, u32[]{:S(2)}, u32[]{:S(2)}) collective-permute-start(bf16[208,1024]{1,0:T(8,128)(2,1)S(1)} %add_convert_fusion.1), channel_id=1, source_target_pairs={{0,2},{1,3},{2,0},{3,1},{4,6},{5,7},{6,4},{7,5},{8,10},{9,11},{10,... | collective-permute-start | bytes 1277960 | tf_op jit(solution)/shard_map/ppermute | solution.py:194
  48.7 10.7 %collective-permute-done.10 = bf16[208,1024]{1,0:T(8,128)(2,1)S(1)} collective-permute-done((bf16[208,1024]{1,0:T(8,128)(2,1)S(1)}, bf16[208,1024]{1,0:T(8,128)(2,1)S(1)}, u32[]{:S(2)}, u32[]{:S(2)}) %collective-permute-start.10) | collective-permute-done | bytes 426016 | tf_op jit(solution)/shard_map/ppermute | solution.py:194
  59.6 1.8 %collective-permute-done.11 = bf16[208,1024]{1,0:T(8,128)(2,1)S(1)} collective-permute-done((bf16[208,1024]{1,0:T(8,128)(2,1)S(1)}, bf16[208,1024]{1,0:T(8,128)(2,1)S(1)}, u32[]{:S(2)}, u32[]{:S(2)}) %collective-permute-start.11) | collective-permute-done | bytes 426016 | tf_op jit(solution)/shard_map/ppermute | solution.py:194
  61.7 0.6 slice.24
  62.2 0.9 %pad_maximum_fusion.1 = f32[192,768]{1,0:T(8,128)} fusion(f32[192,384]{1,0:T(8,128)S(1)} %slice.23, f32[192,384]{1,0:T(8,128)S(1)} %slice.22), kind=kLoop, calls=%fused_computation.3 | loop fusion | flops 147456 | bytes 1179648 | tf_op jit(solution)/shard_map/concatenate | solution.py:387
  63.1 1.0 %pad_maximum_fusion = f32[192,1280]{1,0:T(8,128)} fusion(f32[192,640]{1,0:T(8,128)S(1)} %slice.21, f32[192,640]{1,0:T(8,128)S(1)} %slice.20), kind=kLoop, calls=%fused_computation | loop fusion | flops 245760 | bytes 1966080 | tf_op jit(solution)/shard_map/concatenate | solution.py:386
  (26 shorter events, 0.7 us)
Async XLA Ops:
  0.6 20.4 %collective-permute-start = (bf16[960,384]{1,0:T(8,128)(2,1)}, bf16[960,384]{1,0:T(8,128)(2,1)S(1)}, u32[]{:S(2)}, u32[]{:S(2)}) collective-permute-start(bf16[960,384]{1,0:T(8,128)(2,1)} %bitcast.7), channel_id=1, source_target_pairs={{0,2},{1,3},{2,0},{3,1},{4,6},{5,7},{6,4},{7,5},{8,10},{9,11},{10,... | collective-permute-start | bytes 2211848 | tf_op jit(solution)/shard_map/ppermute | solution.py:194
  3.6 9.9 %collective-permute-start.1 = (bf16[256,384]{1,0:T(8,128)(2,1)}, bf16[256,384]{1,0:T(8,128)(2,1)S(1)}, u32[]{:S(2)}, u32[]{:S(2)}) collective-permute-start(bf16[256,384]{1,0:T(8,128)(2,1)} %bitcast.10), channel_id=1, source_target_pairs={{0,4},{4,8},{8,12},{12,0},{1,5},{5,9},{9,13},{13,1},{2,6},{6,10},{... | collective-permute-start | bytes 589832 | tf_op jit(solution)/shard_map/ppermute | solution.py:190
  5.2 10.9 %collective-permute-start.2 = (bf16[256,384]{1,0:T(8,128)(2,1)}, bf16[256,384]{1,0:T(8,128)(2,1)S(1)}, u32[]{:S(2)}, u32[]{:S(2)}) collective-permute-start(bf16[256,384]{1,0:T(8,128)(2,1)} %bitcast.11), channel_id=1, source_target_pairs={{0,12},{4,0},{8,4},{12,8},{1,13},{5,1},{9,5},{13,9},{2,14},{6,2},{... | collective-permute-start | bytes 589832 | tf_op jit(solution)/shard_map/ppermute | solution.py:190
  13.5 7.5 %collective-permute-start.3 = (bf16[256,384]{1,0:T(8,128)(2,1)S(1)}, bf16[256,384]{1,0:T(8,128)(2,1)S(1)}, u32[]{:S(2)}, u32[]{:S(2)}) collective-permute-start(bf16[256,384]{1,0:T(8,128)(2,1)S(1)} %collective-permute-done.1.fa), channel_id=1, source_target_pairs={{0,4},{4,8},{8,12},{12,0},{1,5},{5,9},{9,13},{13,1},{2,6},{6,10},{... | collective-permute-start | bytes 589832 | tf_op jit(solution)/shard_map/ppermute | solution.py:190
  13.5 13.5 %collective-permute-start.4 = (bf16[960,384]{1,0:T(8,128)(2,1)}, bf16[960,384]{1,0:T(8,128)(2,1)S(1)}, u32[]{:S(2)}, u32[]{:S(2)}) collective-permute-start(bf16[960,384]{1,0:T(8,128)(2,1)} %bitcast.8), channel_id=1, source_target_pairs={{0,1},{1,0},{2,3},{3,2},{4,5},{5,4},{6,7},{7,6},{8,9},{9,8},{10,11... | collective-permute-start | bytes 2211848 | tf_op jit(solution)/shard_map/ppermute | solution.py:194
  21.0 11.1 %collective-permute-start.5 = (bf16[960,384]{1,0:T(8,128)(2,1)S(1)}, bf16[960,384]{1,0:T(8,128)(2,1)S(1)}, u32[]{:S(2)}, u32[]{:S(2)}) collective-permute-start(bf16[960,384]{1,0:T(8,128)(2,1)S(1)} %collective-permute-done.w2), channel_id=1, source_target_pairs={{0,1},{1,0},{2,3},{3,2},{4,5},{5,4},{6,7},{7,6},{8,9},{9,8},{10,11... | collective-permute-start | bytes 2211848 | tf_op jit(solution)/shard_map/ppermute | solution.py:194
  21.0 11.0 %collective-permute-start.6 = (bf16[128,768]{1,0:T(8,128)(2,1)}, bf16[128,768]{1,0:T(8,128)(2,1)S(1)}, u32[]{:S(2)}, u32[]{:S(2)}) collective-permute-start(bf16[128,768]{1,0:T(8,128)(2,1)} %bitcast.13), channel_id=1, source_target_pairs={{0,4},{4,8},{8,12},{12,0},{1,5},{5,9},{9,13},{13,1},{2,6},{6,10},{... | collective-permute-start | bytes 589832 | tf_op jit(solution)/shard_map/ppermute | solution.py:190
  24.3 7.7 %copy-start = (bf16[768,1280]{1,0:T(8,128)(2,1)S(1)}, bf16[768,1280]{1,0:T(8,128)(2,1)}, u32[]{:S(2)}) copy-start(bf16[768,1280]{1,0:T(8,128)(2,1)} %aw.3) | copy-start | bytes 5898244
  24.3 7.7 %copy-start.1 = (bf16[768,768]{1,0:T(8,128)(2,1)S(1)}, bf16[768,768]{1,0:T(8,128)(2,1)}, u32[]{:S(2)}) copy-start(bf16[768,768]{1,0:T(8,128)(2,1)} %ow.3) | copy-start | bytes 3538948
  24.3 15.2 %collective-permute-start.7 = (bf16[128,768]{1,0:T(8,128)(2,1)}, bf16[128,768]{1,0:T(8,128)(2,1)S(1)}, u32[]{:S(2)}, u32[]{:S(2)}) collective-permute-start(bf16[128,768]{1,0:T(8,128)(2,1)} %bitcast.14), channel_id=1, source_target_pairs={{0,12},{4,0},{8,4},{12,8},{1,13},{5,1},{9,5},{13,9},{2,14},{6,2},{... | collective-permute-start | bytes 589832 | tf_op jit(solution)/shard_map/ppermute | solution.py:190
  27.0 1.1 %copy-start.2 = (bf16[5,384,192]{1,2,0:T(8,128)(2,1)S(1)}, bf16[5,384,192]{1,2,0:T(8,128)(2,1)}, u32[]{:S(2)}) copy-start(bf16[5,384,192]{1,2,0:T(8,128)(2,1)} %param.8) | copy-start | bytes 2211844
  28.1 0.9 %copy-start.3 = (bf16[1,256,384]{2,1,0:T(8,128)(2,1)S(1)}, bf16[1,256,384]{2,1,0:T(8,128)(2,1)}, u32[]{:S(2)}) copy-start(bf16[1,256,384]{2,1,0:T(8,128)(2,1)} %param.7) | copy-start | bytes 589828
  32.0 8.6 %collective-permute-start.8 = (bf16[128,768]{1,0:T(8,128)(2,1)S(1)}, bf16[128,768]{1,0:T(8,128)(2,1)S(1)}, u32[]{:S(2)}, u32[]{:S(2)}) collective-permute-start(bf16[128,768]{1,0:T(8,128)(2,1)S(1)} %collective-permute-done.6.ca), channel_id=1, source_target_pairs={{0,4},{4,8},{8,12},{12,0},{1,5},{5,9},{9,13},{13,1},{2,6},{6,10},{... | collective-permute-start | bytes 589832 | tf_op jit(solution)/shard_map/ppermute | solution.py:190
  32.1 8.5 %copy-start.4 = (bf16[1,128,768]{2,1,0:T(8,128)(2,1)S(1)}, bf16[1,128,768]{2,1,0:T(8,128)(2,1)}, u32[]{:S(2)}) copy-start(bf16[1,128,768]{2,1,0:T(8,128)(2,1)} %param.13) | copy-start | bytes 589828
  45.5 1.8 %collective-permute-start.9 = (bf16[208,1024]{1,0:T(8,128)(2,1)S(1)}, bf16[208,1024]{1,0:T(8,128)(2,1)S(1)}, u32[]{:S(2)}, u32[]{:S(2)}) collective-permute-start(bf16[208,1024]{1,0:T(8,128)(2,1)S(1)} %get-tuple-element.31), channel_id=1, source_target_pairs={{0,1},{1,0},{2,3},{3,2},{4,5},{5,4},{6,7},{7,6},{8,9},{9,8},{10,11... | collective-permute-start | bytes 1277960 | tf_op jit(solution)/shard_map/ppermute | solution.py:194
  47.5 11.9 %collective-permute-start.10 = (bf16[208,1024]{1,0:T(8,128)(2,1)S(1)}, bf16[208,1024]{1,0:T(8,128)(2,1)S(1)}, u32[]{:S(2)}, u32[]{:S(2)}) collective-permute-start(bf16[208,1024]{1,0:T(8,128)(2,1)S(1)} %add_convert_fusion.1), channel_id=1, source_target_pairs={{0,2},{1,3},{2,0},{3,1},{4,6},{5,7},{6,4},{7,5},{8,10},{9,11},{10,... | collective-permute-start | bytes 1277960 | tf_op jit(solution)/shard_map/ppermute | solution.py:194
  59.6 1.8 %collective-permute-start.11 = (bf16[208,1024]{1,0:T(8,128)(2,1)S(1)}, bf16[208,1024]{1,0:T(8,128)(2,1)S(1)}, u32[]{:S(2)}, u32[]{:S(2)}) collective-permute-start(bf16[208,1024]{1,0:T(8,128)(2,1)S(1)} %add_convert_fusion), channel_id=1, source_target_pairs={{0,1},{1,0},{2,3},{3,2},{4,5},{5,4},{6,7},{7,6},{8,9},{9,8},{10,11... | collective-permute-start | bytes 1277960 | tf_op jit(solution)/shard_map/ppermute | solution.py:194

commit v2 on v1

--- a/solution.py
+++ b/solution.py
@@ -202,13 +202,25 @@
         taps[pl.ds((1 - core) * SHARD, SHARD), lanes] = other[rows, :]
 
 
+def half_of(bias, side):
+    both = bias[...].reshape(1, WIDTH)
+    return jnp.where(side == 0, both[:, : WIDTH // 2], both[:, WIDTH // 2 :])
+
+
 def filtered_half(windows, taps, bias):
     even = mm(windows[:, : 5 * CIN], taps[...], NT) + bias
     odd = mm(windows[:, CIN:], taps[...], NT) + bias
     return (0.5 * (half_gelu(even) + half_gelu(odd))).astype(BF16)
 
 
-def near_kernel(f0, fa, fb, fc, w0, w1, bias, windows, hid, positions, taps):
+def taps_kernel(w0_far, w1, taps, w0, sems):
+    load = pltpu.make_async_copy(w0_far, w0, sems.at[0])
+    load.start()
+    load.wait()
+    put_shards(taps, w0, w1, lax.rem(lax.axis_index("dp"), 2))
+
+
+def near_kernel(f0, fa, fb, fc, taps, bias, windows, hid, positions):
     z, d = lax.axis_index("seq"), lax.axis_index("dp")
     chunk = 2 * TOK
     for g in range(CIN // 128):
@@ -220,30 +232,44 @@
         for k in range(6):
             at = k * CIN + g * 128
             windows[:, at : at + 128] = positions[g, pl.ds(6 + k, LEN, stride=2), :].astype(BF16)
-    core = lax.rem(d, 2)
-    put_shards(taps, w0, w1, core)
-    hid[...] = filtered_half(windows, taps, bias[pl.ds(d // 2, 1), :])
-
-
-def forward_kernel(
-    windows, hid_near, w2, w3, bias, gain, aw, ow, outputs, normed_t, proj, probs_t, att_t, taps, hid, normed
-):
+    hid[...] = filtered_half(windows[: LEN // 2, :], taps, half_of(bias, d // 2))
+
+
+def rest_kernel(windows, taps, bias, hid):
+    hid[...] = filtered_half(windows[LEN // 2 :, :], taps, half_of(bias, lax.axis_index("dp") // 2))
+
+
+def project_kernel(windows, hid_near, hid_rest, w2, w3, bias, gain, aw, hid, normed, proj, normed_t, taps):
     z, d = lax.axis_index("seq"), lax.axis_index("dp")
-    side, core = d // 2, lax.rem(d, 2)
-    half = WIDTH // 2
-    put_shards(taps, w2, w3, core)
-    hid[side] = hid_near[...]
-    hid[1 - side] = filtered_half(windows, taps, bias[pl.ds(1 - side, 1), :])
+    side, half = d // 2, WIDTH // 2
+    put_shards(taps, w2, w3, lax.rem(d, 2))
+    hid[side, : LEN // 2, :] = hid_near[...]
+    hid[side, LEN // 2 :, :] = hid_rest[...]
+    hid[1 - side] = filtered_half(windows, taps, half_of(bias, 1 - side))
     low, high = hid[0].astype(F32), hid[1].astype(F32)
     square = jnp.sum(low * low, axis=1, keepdims=True) + jnp.sum(high * high, axis=1, keepdims=True)
     inv = lax.rsqrt(square * (1.0 / WIDTH) + 1e-06)
-    normed[:, :half] = (low * inv * gain[:, :half]).astype(BF16)
-    normed[:, half:] = (high * inv * gain[:, half:]).astype(BF16)
+    scales = gain[...].reshape(1, WIDTH)
+    normed[:, :half] = (low * inv * scales[:, :half]).astype(BF16)
+    normed[:, half:] = (high * inv * scales[:, half:]).astype(BF16)
     proj[...] = mm(normed[...], aw[...]).astype(BF16)
+    for at in range(SEQ):
+
+        @pl.when(z == at)
+        def _():
+            normed_t[...] = normed[:, at * ROWS : (at + 1) * ROWS].T
+
+
+def heads_of(proj, h):
+    q = proj[:, h * KEY_DIM : (h + 1) * KEY_DIM]
+    k = proj[:, QW + h * KEY_DIM : QW + (h + 1) * KEY_DIM]
+    v = proj[:, 2 * QW + h * VAL_DIM : 2 * QW + (h + 1) * VAL_DIM]
+    return q, k, v
+
+
+def attend_kernel(proj, probs_t, att_t):
     for h in range(HEADS):
-        q = proj[:, h * KEY_DIM : (h + 1) * KEY_DIM]
-        k = proj[:, QW + h * KEY_DIM : QW + (h + 1) * KEY_DIM]
-        v = proj[:, 2 * QW + h * VAL_DIM : 2 * QW + (h + 1) * VAL_DIM]
+        q, k, v = heads_of(proj, h)
         scores = mm(k, q, NT) * SCALE
         top = jnp.max(scores, axis=0, keepdims=True)
         weight = jnp.exp(scores - top)
@@ -251,6 +277,11 @@
         probs = (weight * (1.0 / total)).astype(BF16)
         probs_t[h] = probs
         att_t[h * VAL_DIM : (h + 1) * VAL_DIM, :] = mm(v, probs, TN).astype(BF16)
+
+
+def outputs_kernel(hid, att_t, ow, outputs):
+    z = lax.axis_index("seq")
+    half = WIDTH // 2
     for at in range(SEQ):
 
         @pl.when(z == at)
@@ -259,14 +290,19 @@
             branch = mm(att_t[:, rows], ow[...], (((0,), (1,)), ((), ())))
             outputs[:, :half] = branch[:, :half] + hid[0, rows, :].astype(F32)
             outputs[:, half:] = branch[:, half:] + hid[1, rows, :].astype(F32)
-            normed_t[...] = normed[:, at * ROWS : (at + 1) * ROWS].T
-
-
-def backward_kernel(
-    c0, ca, cb, cc, normed_t, proj, probs_t, att_t, gain, aw, ow, keep, send, cot, cot_t, grad, d_query, d_rest
-):
+
+
+def both_ways(write, keep, send, core):
+    for at in range(2):
+
+        @pl.when(core == at)
+        def _():
+            write(keep, at)
+            write(send, 1 - at)
+
+
+def value_kernel(c0, ca, cb, cc, normed_t, probs_t, att_t, aw, ow, grad, keep, send, mixed, cot, cot_t, d_value):
     z, d = lax.axis_index("seq"), lax.axis_index("dp")
-    core = lax.rem(d, 2)
     for ref, off in ((c0, 0), (ca, 3), (cb, 1), (cc, 2)):
         start = pl.multiple_of(lax.rem(z + off, SEQ) * TOK, TOK)
         cot[pl.ds(start, TOK), :] = ref[...]
@@ -279,113 +315,195 @@
     grad[...] = mm(cot[...], ow[...]).astype(BF16)
     out_part = mm(cot_t[...], att_t[...], NT)
     for h in range(HEADS):
-        q = proj[:, h * KEY_DIM : (h + 1) * KEY_DIM]
-        k = proj[:, QW + h * KEY_DIM : QW + (h + 1) * KEY_DIM]
-        v = proj[:, 2 * QW + h * VAL_DIM : 2 * QW + (h + 1) * VAL_DIM]
-        g = grad[:, h * VAL_DIM : (h + 1) * VAL_DIM]
+        lanes = slice(h * VAL_DIM, (h + 1) * VAL_DIM)
+        d_value[:, lanes] = mm(probs_t[h], grad[:, lanes]).astype(BF16)
+    value_part = mm(normed_t[...], d_value[...])
+    here = pl.multiple_of(z * ROWS, ROWS)
+    total = jnp.sum(value_part * aw[pl.ds(here, ROWS), 2 * QW :].astype(F32), axis=1, keepdims=True)
+    mixed[...] = jnp.broadcast_to(total, (ROWS, 128))
+    half = VW // 2
+
+    def write(ref, side):
+        lanes = slice(side * half, (side + 1) * half)
+        ref[:, :half] = value_part[:, lanes].astype(ref.dtype)
+        ref[:, half:] = out_part[:, lanes].astype(ref.dtype)
+
+    both_ways(write, keep, send, lax.rem(d, 2))
+
+
+def score_grads(grad, proj, probs_t, d_query, d_key, first):
+    for h in range(first, first + HEADS // 2):
+        q, k, v = heads_of(proj, h)
         probs = probs_t[h].astype(F32)
-        product = mm(v, g, NT) * probs
+        product = mm(v, grad[:, h * VAL_DIM : (h + 1) * VAL_DIM], NT) * probs
         delta = jnp.sum(product, axis=0, keepdims=True)
         dscore = (product - probs * delta).astype(BF16)
-        d_query[h * KEY_DIM : (h + 1) * KEY_DIM, :] = (mm(k, dscore, TN) * SCALE).astype(BF16)
-        d_rest[:, h * KEY_DIM : (h + 1) * KEY_DIM] = (mm(dscore, q) * SCALE).astype(BF16)
-        d_rest[:, QW + h * VAL_DIM : QW + (h + 1) * VAL_DIM] = mm(probs_t[h], g).astype(BF16)
-    query_part = mm(normed_t[...], d_query[...], NT)
-    rest_part = mm(normed_t[...], d_rest[...])
+        lanes = slice((h - first) * KEY_DIM, (h - first + 1) * KEY_DIM)
+        d_query[lanes, :] = (mm(k, dscore, TN) * SCALE).astype(BF16)
+        d_key[:, lanes] = (mm(dscore, q) * SCALE).astype(BF16)
+
+
+def early_key_kernel(grad, proj, probs_t, d_query, d_key):
+    score_grads(grad, proj, probs_t, d_query, d_key, 0)
+
+
+def late_key_kernel(
+    grad, proj, probs_t, query_early, key_early, normed_t, mixed, gain, aw, keep, send, d_query, d_key
+):
+    z, d = lax.axis_index("seq"), lax.axis_index("dp")
+    score_grads(grad, proj, probs_t, d_query, d_key, HEADS // 2)
+    left = normed_t[...]
+    query_part = jnp.concatenate([mm(left, query_early[...], NT), mm(left, d_query[...], NT)], axis=1)
+    key_part = jnp.concatenate([mm(left, key_early[...]), mm(left, d_key[...])], axis=1)
     here = pl.multiple_of(z * ROWS, ROWS)
-    mixed = jnp.sum(query_part * aw[pl.ds(here, ROWS), :QW].astype(F32), axis=1, keepdims=True)
-    mixed = mixed + jnp.sum(rest_part * aw[pl.ds(here, ROWS), QW:].astype(F32), axis=1, keepdims=True)
-    gain_part = jnp.broadcast_to(mixed, (ROWS, 128)).T[0:1, :] / gain[pl.ds(z, 1), :]
-    split = PROJ // 2 - QW
+    total = query_part * aw[pl.ds(here, ROWS), :QW].astype(F32)
+    total = total + key_part * aw[pl.ds(here, ROWS), QW : 2 * QW].astype(F32)
+    total = mixed[...] + jnp.sum(total, axis=1, keepdims=True)
+    scales = gain[...].reshape(1, WIDTH)
+    mine = scales[:, :ROWS]
+    for at in range(1, SEQ):
+        mine = jnp.where(z == at, scales[:, at * ROWS : (at + 1) * ROWS], mine)
+    gain_part = total.T[0:1, :] / mine
 
     def write(ref, side):
-        if side == 0:
-            ref[:ROWS, :QW] = query_part.astype(ref.dtype)
-            ref[:ROWS, QW : PROJ // 2] = rest_part[:, :split].astype(ref.dtype)
-        else:
-            ref[:ROWS, : PROJ // 2] = rest_part[:, split:].astype(ref.dtype)
-        ref[:ROWS, PROJ // 2 :] = out_part[:, side * VW // 2 : (side + 1) * VW // 2].astype(ref.dtype)
-        ref[ROWS:, :] = jnp.zeros((16, PROJ // 2 + VW // 2), ref.dtype)
+        ref[:ROWS, :] = (key_part if side else query_part).astype(ref.dtype)
+        ref[ROWS:, :] = jnp.zeros((16, QW), ref.dtype)
         ref[ROWS : ROWS + 1, :ROWS] = gain_part.astype(ref.dtype)
 
+    both_ways(write, keep, send, lax.rem(d, 2))
+
+
+def finish_kernel(whole_v, whole_k, top_v, rest_v, other_k, grad_attend, grad_output, grad_gain):
+    half = VW // 2
+
+    def place(source, rows, side):
+        lanes = slice(side * half, (side + 1) * half)
+        grad_attend[rows, 2 * QW + side * half : 2 * QW + (side + 1) * half] = source[:, :half].astype(F32)
+        grad_output[rows, lanes] = source[:, half:].astype(F32)
+
     for at in range(2):
 
-        @pl.when(core == at)
+        @pl.when(lax.rem(lax.axis_index("dp"), 2) == at)
         def _():
-            write(keep, at)
-            write(send, 1 - at)
-
-
-def kernel_call(body, outs, scratch, flops, bytes_accessed, *args):
+            place(whole_v, slice(0, ROWS), at)
+            place(top_v, slice(0, ROWS // 2), 1 - at)
+            place(rest_v, slice(ROWS // 2, ROWS), 1 - at)
+            low, high = (whole_k, other_k) if at == 0 else (other_k, whole_k)
+            grad_attend[:, :QW] = low[:ROWS, :].astype(F32)
+            grad_attend[:, QW : 2 * QW] = high[:ROWS, :].astype(F32)
+            grad_gain[...] = low[ROWS : ROWS + 8, :ROWS].astype(F32)[0]
+
+
+def kernel_call(body, outs, scratch, flops, *args, far=()):
+    whole = pl.BlockSpec(memory_space=pltpu.VMEM)
+    away = pl.BlockSpec(memory_space=pltpu.HBM)
+    sems = [pltpu.SemaphoreType.DMA((len(far),))] if far else []
     return pl.pallas_call(
         body,
+        in_specs=[away if i in far else whole for i in range(len(args))],
         out_shape=[jax.ShapeDtypeStruct(s, t) for s, t in outs],
-        scratch_shapes=[pltpu.VMEM(s, t) for s, t in scratch],
+        scratch_shapes=[pltpu.VMEM(s, t) for s, t in scratch] + sems,
         compiler_params=pltpu.CompilerParams(vmem_limit_bytes=40 << 20),
-        cost_estimate=pl.CostEstimate(flops=flops, bytes_accessed=bytes_accessed, transcendentals=0),
+        cost_estimate=pl.CostEstimate(flops=flops, bytes_accessed=1 << 16, transcendentals=0),
     )(*args)
+
+
+def combined(keep, arrived):
+    return (keep.astype(F32) + arrived.astype(F32)).astype(BF16)
 
 
 def per_device_fast(
     dna_features, filter_weight, filter_bias, norm_gain, attend_weight, output_weight, cotangent
 ):
-    d = lax.axis_index("dp")
     f0, c0 = dna_features[0], cotangent[0]
     w0 = filter_weight.transpose(0, 2, 1).reshape(5 * SHARD, CIN)
+    half = WIDTH // 2
     w2 = swap(w0, 2)
     w1 = swap(w0, 1)
     fa, fb = ring(f0, 1), ring(f0, SEQ - 1)
-    fc = ring(fa, 1)
-    w2, fa, fb, fc = lax.optimization_barrier((w2, fa, fb, fc))
-    w3 = swap(w2, 1)
-    bias = filter_bias.reshape(2, WIDTH // 2)
-    gain = norm_gain.reshape(1, WIDTH)
+    (taps,) = kernel_call(
+        taps_kernel,
+        [((2 * SHARD, 5 * CIN), BF16)],
+        [((5 * SHARD, CIN), BF16)],
+        1 << 31,
+        pltpu.with_memory_space_constraint(w0, pltpu.HBM), w1,
+        far=(0,),
+    )
+    ca = ring(c0, 1)
+    far_a, taps = lax.optimization_barrier((fa, taps))
+    to_left, far_a, fb = lax.optimization_barrier((c0, far_a, fb))
+    fc = ring(far_a, 1)
+    cb, cc = ring(to_left, SEQ - 1), ring(ca, 1)
+    fc, ca = lax.optimization_barrier((fc, ca))
     windows, hid_near = kernel_call(
         near_kernel,
-        [((LEN, 6 * CIN), BF16), ((LEN, WIDTH // 2), BF16)],
-        [((CIN // 128, 16 + 2 * LEN, 128), F32), ((2 * SHARD, 5 * CIN), BF16)],
-        2 * 2 * LEN * 5 * CIN * WIDTH // 2, 4 << 20,
-        f0, fa, fb, fc, w0, w1, bias,
-    )
-    c0 = lax.optimization_barrier((c0, fc))[0]
-    ca, cb = ring(c0, 1), ring(c0, SEQ - 1)
-    cc = ring(ca, 1)
-    outputs, normed_t, proj, probs_t, att_t = kernel_call(
-        forward_kernel,
-        [
-            ((TOK, WIDTH), F32),
-            ((ROWS, LEN), BF16),
-            ((LEN, PROJ), BF16),
-            ((HEADS, LEN, LEN), BF16),
-            ((VW, LEN), BF16),
-        ],
-        [((2 * SHARD, 5 * CIN), BF16), ((2, LEN, WIDTH // 2), BF16), ((LEN, WIDTH), BF16)],
-        5 << 30, 8 << 20,
-        windows, hid_near, w2, w3, bias, gain, attend_weight, output_weight,
-    )
-    keep, send = kernel_call(
-        backward_kernel,
-        [((ROWS + 16, (PROJ + VW) // 2), F32), ((ROWS + 16, (PROJ + VW) // 2), BF16)],
-        [
-            ((LEN, WIDTH), BF16),
-            ((ROWS, LEN), BF16),
-            ((LEN, VW), BF16),
-            ((QW, LEN), BF16),
-            ((LEN, QW + VW), BF16),
-        ],
-        5 << 30, 8 << 20,
-        c0, ca, cb, cc, normed_t, proj, probs_t, att_t, norm_gain.reshape(SEQ, ROWS), attend_weight, output_weight,
-    )
-    part = (keep + swap(send, 1).astype(F32)).astype(BF16)
-    whole = (part.astype(F32) + swap(part, 2).astype(F32)).astype(BF16)
-    other = swap(whole, 1)
-    first = lax.rem(d, 2) == 0
-    low = jnp.where(first, whole, other).astype(F32)
-    high = jnp.where(first, other, whole).astype(F32)
-    cut = PROJ // 2
-    grad_attend = jnp.concatenate([low[:ROWS, :cut], high[:ROWS, :cut]], axis=1)
-    grad_output = jnp.concatenate([low[:ROWS, cut:], high[:ROWS, cut:]], axis=1)
-    return outputs[None], grad_attend, grad_output, low[ROWS, :ROWS]
+        [((LEN, 6 * CIN), BF16), ((LEN // 2, half), BF16)],
+        [((CIN // 128, 16 + 2 * LEN, 128), F32)],
+        1 << 16,
+        f0, fa, fb, fc, taps, filter_bias,
+    )
+    w2, windows = lax.optimization_barrier((w2, windows))
+    w3 = swap(w2, 1)
+    (hid_rest,) = kernel_call(
+        rest_kernel, [((LEN // 2, half), BF16)], [], 1 << 33, windows, taps, filter_bias
+    )
+    hid, normed, proj, normed_t = kernel_call(
+        project_kernel,
+        [((2, LEN, half), BF16), ((LEN, WIDTH), BF16), ((LEN, PROJ), BF16), ((ROWS, LEN), BF16)],
+        [((2 * SHARD, 5 * CIN), BF16)],
+        1 << 24,
+        windows, hid_near, hid_rest, w2, w3, filter_bias, norm_gain, attend_weight,
+    )
+    probs_t, att_t = kernel_call(
+        attend_kernel,
+        [((HEADS, LEN, LEN), BF16), ((VW, LEN), BF16)],
+        [],
+        1 << 31,
+        proj,
+    )
+    (outputs,) = kernel_call(
+        outputs_kernel, [((TOK, WIDTH), F32)], [], 1 << 31, hid, att_t, output_weight
+    )
+    grad, keep_v, send_v, mixed = kernel_call(
+        value_kernel,
+        [((LEN, VW), BF16), ((ROWS, VW), F32), ((ROWS, VW), BF16), ((ROWS, 128), F32)],
+        [((LEN, WIDTH), BF16), ((ROWS, LEN), BF16), ((LEN, VW), BF16)],
+        1 << 33,
+        c0, ca, cb, cc, normed_t, probs_t, att_t, attend_weight, output_weight,
+    )
+    query_early, key_early = kernel_call(
+        early_key_kernel,
+        [((QW // 2, LEN), BF16), ((LEN, QW // 2), BF16)],
+        [],
+        1 << 24,
+        grad, proj, probs_t,
+    )
+    part_v = combined(keep_v, swap(send_v, 1))
+    part_v, query_early = lax.optimization_barrier((part_v, query_early))
+    keep_k, send_k = kernel_call(
+        late_key_kernel,
+        [((ROWS + 16, QW), F32), ((ROWS + 16, QW), BF16)],
+        [((QW // 2, LEN), BF16), ((LEN, QW // 2), BF16)],
+        1 << 29,
+        grad, proj, probs_t, query_early, key_early, normed_t, mixed, norm_gain, attend_weight,
+    )
+    arrived_v = swap(part_v, 2)
+    part_k = combined(keep_k, swap(send_k, 1))
+    arrived_k = swap(part_k, 2)
+    arrived_v = lax.optimization_barrier((arrived_v, part_k))[0]
+    whole_v, whole_k = combined(part_v, arrived_v), combined(part_k, arrived_k)
+    other_k = swap(whole_k, 1)
+    top = swap(whole_v[: ROWS // 2], 1)
+    rest, top = lax.optimization_barrier((whole_v[ROWS // 2 :], top))
+    other_v = (top, swap(rest, 1))
+    grad_attend, grad_output, grad_gain = kernel_call(
+        finish_kernel,
+        [((ROWS, PROJ), F32), ((ROWS, WIDTH), F32), ((ROWS,), F32)],
+        [],
+        1 << 24,
+        whole_v, whole_k, *other_v, other_k,
+    )
+    return outputs[None], grad_attend, grad_output, grad_gain
 
 
 def solution(mesh):

time: 64.4 us -> 59.1 us (0.918)
  waiting for transfers between devices: 28.8 us -> 22 us
  Pallas kernels: 15.3 us -> 20.7 us
  local copies, waits for them, and re-layouts: 4.9 us -> 0.05 us
  starting transfers between devices: 12.1 us -> 15.2 us
  other arithmetic: 2.23 us -> 0.19 us
    pallas_call x3 -> x10, Pallas kernels: 15.3 us -> 20.7 us  [kernel_call(): pl.pallas_call(body, in_specs=[away if i in far else whole for i in range...]
    ppermute x6 -> x10, waiting for transfers between devices: 14.2 us -> 10.5 us  [swap(): return lax.ppermute(value, 'dp', [(i, i ^ bit) for i in range(DP)])]
    ppermute x6, waiting for transfers between devices: 14.5 us -> 11.5 us  [ring(): lax.ppermute(value, 'seq', [(i, (i + step) % SEQ) for i in range(SEQ)])]
    reshape x3 -> x0, local copies, waits for them, and re-layouts: 2.15 us -> none  [the longest x1 0.76 us: per_device_fast(): norm_gain.reshape(SEQ, ROWS)]
    unnamed x10 -> x12, local copies, waits for them, and re-layouts: 2.06 us -> 0.03 us
    concatenate x2 -> x0, other arithmetic: 1.86 us -> none  [the longest x1 1.01 us: per_device_fast(): grad_attend = jnp.concatenate([low[:ROWS, :cut], high[:ROWS, :cut]], axis=1)]
    ppermute x6, starting transfers between devices: 7.71 us -> 9.34 us  [ring(): lax.ppermute(value, 'seq', [(i, (i + step) % SEQ) for i in range(SEQ)])]
    ppermute x6 -> x10, starting transfers between devices: 4.36 us -> 5.9 us  [swap(): return lax.ppermute(value, 'dp', [(i, i ^ bit) for i in range(DP)])]
  transfers between devices with their start and end apart: 12 -> 16, of which waited for: 7 -> 8; matrix products, arithmetic and copies ran while one was open for 3% -> 0% of each run, Pallas kernels for 16% -> 26%
where the time goes in v2:
time: 59.1 us; the launch traced here: 59 us
  waiting for transfers between devices  22 us (37%)
  Pallas kernels  20.7 us (35%)
  starting transfers between devices  15.2 us (26%)
  between operations  0.81 us (1%)
    pallas_call x10, Pallas kernels, kernel_call(): pl.pallas_call(body, in_specs=[away if i in far else whole for i in range...  20.7 us
    ppermute x6, waiting for transfers between devices, ring(): lax.ppermute(value, 'seq', [(i, (i + step) % SEQ) for i in range(SEQ)])  11.5 us
    ppermute x10, waiting for transfers between devices, swap(): return lax.ppermute(value, 'dp', [(i, i ^ bit) for i in range(DP)])  10.5 us
    ppermute x6, starting transfers between devices, ring(): lax.ppermute(value, 'seq', [(i, (i + step) % SEQ) for i in range(SEQ)])  9.34 us
    ppermute x10, starting transfers between devices, swap(): return lax.ppermute(value, 'dp', [(i, i ^ bit) for i in range(DP)])  5.9 us
  transfers between devices with their start and end apart: 16, of which 8 were waited for; matrix products, arithmetic and copies ran while one was open for 0% of the time, Pallas kernels for 26%

profile of v2, /device:TPU:0, one launch (start us, length us, event | category | flops | bytes accessed | tf_op | source)
XLA Modules:
  0.0 59.0 jit_solution(5266585884909143448)
XLA Ops:
  0.6 0.5 collective-permute-start.2
  1.1 2.6 %collective-permute-start = (bf16[960,384]{1,0:T(8,128)(2,1)}, bf16[960,384]{1,0:T(8,128)(2,1)S(1)}, u32[]{:S(2)}, u32[]{:S(2)}) collective-permute-start(bf16[960,384]{1,0:T(8,128)(2,1)} %bitcast.13), channel_id=1, source_target_pairs={{0,2},{1,3},{2,0},{3,1},{4,6},{5,7},{6,4},{7,5},{8,10},{9,11},{10,... | collective-permute-start | bytes 2211848 | tf_op jit(solution)/shard_map/ppermute | solution.py:194
  3.7 1.6 %collective-permute-start.1 = (bf16[256,384]{1,0:T(8,128)(2,1)}, bf16[256,384]{1,0:T(8,128)(2,1)S(1)}, u32[]{:S(2)}, u32[]{:S(2)}) collective-permute-start(bf16[256,384]{1,0:T(8,128)(2,1)} %bitcast.6), channel_id=1, source_target_pairs={{0,4},{4,8},{8,12},{12,0},{1,5},{5,9},{9,13},{13,1},{2,6},{6,10},{... | collective-permute-start | bytes 589832 | tf_op jit(solution)/shard_map/ppermute | solution.py:190
  5.3 2.2 %collective-permute-start.3 = (bf16[256,384]{1,0:T(8,128)(2,1)}, bf16[256,384]{1,0:T(8,128)(2,1)S(1)}, u32[]{:S(2)}, u32[]{:S(2)}) collective-permute-start(bf16[256,384]{1,0:T(8,128)(2,1)} %bitcast.7), channel_id=1, source_target_pairs={{0,12},{4,0},{8,4},{12,8},{1,13},{5,1},{9,5},{13,9},{2,14},{6,2},{... | collective-permute-start | bytes 589832 | tf_op jit(solution)/shard_map/ppermute | solution.py:190
  7.6 1.3 %shard_map.102.taps = bf16[384,1920]{1,0:T(8,128)(2,1)S(1)} custom-call(bf16[960,384]{1,0:T(8,128)(2,1)} %bitcast.14, bf16[960,384]{1,0:T(8,128)(2,1)S(1)} %collective-permute-done.2.w1), custom_call_target="tpu_custom_call" | custom-call | flops 2147483648 | bytes 65536 | tf_op jit(solution)/shard_map/pallas_call | solution.py:401
  8.9 4.6 %collective-permute-done.1.fa = bf16[256,384]{1,0:T(8,128)(2,1)S(1)} collective-permute-done((bf16[256,384]{1,0:T(8,128)(2,1)}, bf16[256,384]{1,0:T(8,128)(2,1)S(1)}, u32[]{:S(2)}, u32[]{:S(2)}) %collective-permute-start.1) | collective-permute-done | bytes 196640 | tf_op jit(solution)/shard_map/ppermute | solution.py:190
  13.5 3.0 %collective-permute-done.3.fb = bf16[256,384]{1,0:T(8,128)(2,1)S(1)} collective-permute-done((bf16[256,384]{1,0:T(8,128)(2,1)}, bf16[256,384]{1,0:T(8,128)(2,1)S(1)}, u32[]{:S(2)}, u32[]{:S(2)}) %collective-permute-start.3) | collective-permute-done | bytes 196640 | tf_op jit(solution)/shard_map/ppermute | solution.py:190
  16.5 1.7 %collective-permute-start.4 = (bf16[256,384]{1,0:T(8,128)(2,1)S(1)}, bf16[256,384]{1,0:T(8,128)(2,1)S(1)}, u32[]{:S(2)}, u32[]{:S(2)}) collective-permute-start(bf16[256,384]{1,0:T(8,128)(2,1)S(1)} %collective-permute-done.1.fa), channel_id=1, source_target_pairs={{0,4},{4,8},{8,12},{12,0},{1,5},{5,9},{9,13},{13,1},{2,6},{6,10},{... | collective-permute-start | bytes 589832 | tf_op jit(solution)/shard_map/ppermute | solution.py:190
  18.2 3.7 %collective-permute-done.5.ca = bf16[128,768]{1,0:T(8,128)(2,1)S(1)} collective-permute-done((bf16[128,768]{1,0:T(8,128)(2,1)}, bf16[128,768]{1,0:T(8,128)(2,1)S(1)}, u32[]{:S(2)}, u32[]{:S(2)}) %collective-permute-start.5) | collective-permute-done | bytes 196640 | tf_op jit(solution)/shard_map/ppermute | solution.py:190
  21.9 3.8 %collective-permute-start.7 = (bf16[128,768]{1,0:T(8,128)(2,1)S(1)}, bf16[128,768]{1,0:T(8,128)(2,1)S(1)}, u32[]{:S(2)}, u32[]{:S(2)}) collective-permute-start(bf16[128,768]{1,0:T(8,128)(2,1)S(1)} %bitcast.10), channel_id=1, source_target_pairs={{0,12},{4,0},{8,4},{12,8},{1,13},{5,1},{9,5},{13,9},{2,14},{6,2},{... | collective-permute-start | bytes 589832 | tf_op jit(solution)/shard_map/ppermute | solution.py:190
  25.9 1.8 %shard_map.103 = (bf16[512,2304]{1,0:T(8,128)(2,1)S(1)}, bf16[256,384]{1,0:T(8,128)(2,1)S(1)}) custom-call(bf16[256,384]{1,0:T(8,128)(2,1)S(1)} %bitcast.8, bf16[256,384]{1,0:T(8,128)(2,1)S(1)} %collective-permute-done.1.fa, bf16[256,384]{1,0:T(8,128)(2,1)S(1)} %collective-permute-done.3.fb, bf16[256,384]{1,0:T(8,128)(2,1)S(1)} %collective-permute-done.4.fc, ...), custom_call_target="tpu_custom_call" | custom-call | flops 65536 | bytes 65536 | tf_op jit(solution)/shard_map/pallas_call | solution.py:401
  27.9 1.4 %shard_map.104.hid_rest = bf16[256,384]{1,0:T(8,128)(2,1)S(1)} custom-call(bf16[512,2304]{1,0:T(8,128)(2,1)S(1)} %get-tuple-element.42.windows, bf16[384,1920]{1,0:T(8,128)(2,1)S(1)} %shard_map.102.taps, f32[768]{0:T(1024)S(1)} %copy-done.2), custom_call_target="tpu_custom_call" | custom-call | flops 8589934592 | bytes 65536 | tf_op jit(solution)/shard_map/pallas_call | solution.py:401
  29.2 0.8 %collective-permute-done.6.w3 = bf16[960,384]{1,0:T(8,128)(2,1)S(1)} collective-permute-done((bf16[960,384]{1,0:T(8,128)(2,1)S(1)}, bf16[960,384]{1,0:T(8,128)(2,1)S(1)}, u32[]{:S(2)}, u32[]{:S(2)}) %collective-permute-start.6) | collective-permute-done | bytes 737312 | tf_op jit(solution)/shard_map/ppermute | solution.py:194
  30.1 5.1 %shard_map.105 = (bf16[2,512,384]{2,1,0:T(8,128)(2,1)S(1)}, bf16[512,768]{1,0:T(8,128)(2,1)}, bf16[512,1280]{1,0:T(8,128)(2,1)S(1)}, bf16[192,512]{1,0:T(8,128)(2,1)S(1)}) custom-call(bf16[512,2304]{1,0:T(8,128)(2,1)S(1)} %get-tuple-element.42.windows, bf16[256,384]{1,0:T(8,128)(2,1)S(1)} %get-tuple-element.43.hid_near, ...), custom_call_target="tpu_custom_call" | custom-call | flops 16777216 | bytes 65536 | tf_op jit(solution)/shard_map/pallas_call | solution.py:401
  35.2 2.7 %shard_map.106 = (bf16[4,512,512]{2,1,0:T(8,128)(2,1)S(1)}, bf16[768,512]{1,0:T(8,128)(2,1)S(1)}) custom-call(bf16[512,1280]{1,0:T(8,128)(2,1)S(1)} %get-tuple-element.46.proj), custom_call_target="tpu_custom_call" | custom-call | flops 2147483648 | bytes 65536 | tf_op jit(solution)/shard_map/pallas_call | solution.py:401
  37.9 2.4 %shard_map.108 = (bf16[512,768]{1,0:T(8,128)(2,1)S(1)}, f32[192,768]{1,0:T(8,128)S(1)}, bf16[192,768]{1,0:T(8,128)(2,1)S(1)}, f32[192,128]{1,0:T(8,128)S(1)}) custom-call(bf16[128,768]{1,0:T(8,128)(2,1)S(1)} %bitcast.11, bf16[128,768]{1,0:T(8,128)(2,1)S(1)} %collective-permute-done.5.ca, bf16[128,768]{1,0:T(8,128)(2,1)S(1)} %collective-permute-done.7.cb, ...), custom_call_target="tpu_custom_call" | custom-call | flops 8589934592 | bytes 65536 | tf_op jit(solution)/shard_map/pallas_call | solution.py:401
  40.6 1.6 %shard_map.109 = (bf16[128,512]{1,0:T(8,128)(2,1)S(1)}, bf16[512,128]{1,0:T(8,128)(2,1)S(1)}) custom-call(bf16[512,768]{1,0:T(8,128)(2,1)S(1)} %get-tuple-element.54.grad, bf16[512,1280]{1,0:T(8,128)(2,1)S(1)} %get-tuple-element.46.proj, bf16[4,512,512]{2,1,0:T(8,128)(2,1)S(1)} %get-tuple-element.51.probs_t), custom_call_target="tpu_custom_call" | custom-call | flops 16777216 | bytes 65536 | tf_op jit(solution)/shard_map/pallas_call | solution.py:401
  42.3 1.8 %shard_map.110 = (f32[208,256]{1,0:T(8,128)S(1)}, bf16[208,256]{1,0:T(8,128)(2,1)S(1)}) custom-call(bf16[512,768]{1,0:T(8,128)(2,1)S(1)} %get-tuple-element.54.grad, bf16[512,1280]{1,0:T(8,128)(2,1)S(1)} %get-tuple-element.46.proj, bf16[4,512,512]{2,1,0:T(8,128)(2,1)S(1)} %get-tuple-element.51.probs_t, bf16[128,512]{1,0:T(8,128)(2,1)S(1)} %get-tuple-element.57.query_early, ...), custom_call_target="tpu_custom_call" | custom-call | flops 536870912 | bytes 65536 | tf_op jit(solution)/shard_map/pallas_call | solution.py:401
  44.8 0.6 %collective-permute-done.11 = bf16[208,256]{1,0:T(8,128)(2,1)S(1)} collective-permute-done((bf16[208,256]{1,0:T(8,128)(2,1)S(1)}, bf16[208,256]{1,0:T(8,128)(2,1)S(1)}, u32[]{:S(2)}, u32[]{:S(2)}) %collective-permute-start.11) | collective-permute-done | bytes 106528 | tf_op jit(solution)/shard_map/ppermute | solution.py:194
  45.5 1.1 %collective-permute-start.12 = (bf16[208,256]{1,0:T(8,128)(2,1)S(1)}, bf16[208,256]{1,0:T(8,128)(2,1)S(1)}, u32[]{:S(2)}, u32[]{:S(2)}) collective-permute-start(bf16[208,256]{1,0:T(8,128)(2,1)S(1)} %add_convert_fusion.3), channel_id=1, source_target_pairs={{0,2},{1,3},{2,0},{3,1},{4,6},{5,7},{6,4},{7,5},{8,10},{9,11},{10,... | collective-permute-start | bytes 319496 | tf_op jit(solution)/shard_map/ppermute | solution.py:194
  46.7 7.7 %collective-permute-done.10 = bf16[192,768]{1,0:T(8,128)(2,1)S(1)} collective-permute-done((bf16[192,768]{1,0:T(8,128)(2,1)S(1)}, bf16[192,768]{1,0:T(8,128)(2,1)S(1)}, u32[]{:S(2)}, u32[]{:S(2)}) %collective-permute-start.10) | collective-permute-done | bytes 294944 | tf_op jit(solution)/shard_map/ppermute | solution.py:194
  54.6 1.3 %collective-permute-done.12 = bf16[208,256]{1,0:T(8,128)(2,1)S(1)} collective-permute-done((bf16[208,256]{1,0:T(8,128)(2,1)S(1)}, bf16[208,256]{1,0:T(8,128)(2,1)S(1)}, u32[]{:S(2)}, u32[]{:S(2)}) %collective-permute-start.12) | collective-permute-done | bytes 106528 | tf_op jit(solution)/shard_map/ppermute | solution.py:194
  56.4 1.3 %shard_map.107 = f32[128,768]{1,0:T(8,128)} custom-call(bf16[2,512,384]{2,1,0:T(8,128)(2,1)S(1)} %get-tuple-element.45.hid, bf16[768,512]{1,0:T(8,128)(2,1)S(1)} %get-tuple-element.47.att_t, bf16[768,768]{1,0:T(8,128)(2,1)S(1)} %copy-done.4), custom_call_target="tpu_custom_call" | custom-call | flops 2147483648 | bytes 65536 | tf_op jit(solution)/shard_map/pallas_call | solution.py:401
  57.7 1.2 %shard_map.111 = (f32[192,1280]{1,0:T(8,128)}, f32[192,768]{1,0:T(8,128)}, f32[192]{0:T(256)}) custom-call(bf16[192,768]{1,0:T(8,128)(2,1)S(1)} %add_convert_fusion.whole_v, bf16[208,256]{1,0:T(8,128)(2,1)S(1)} %add_convert_fusion.2.whole_k, bf16[96,768]{1,0:T(8,128)(2,1)S(1)} %collective-permute-done.13.top_v, ...), custom_call_target="tpu_custom_call" | custom-call | flops 16777216 | bytes 65536 | tf_op jit(solution)/shard_map/pallas_call | solution.py:401
  (35 shorter events, 2.1 us)
Async XLA Ops:
  0.6 6.9 %collective-permute-start.2 = (bf16[960,384]{1,0:T(8,128)(2,1)}, bf16[960,384]{1,0:T(8,128)(2,1)S(1)}, u32[]{:S(2)}, u32[]{:S(2)}) collective-permute-start(bf16[960,384]{1,0:T(8,128)(2,1)} %bitcast.12), channel_id=1, source_target_pairs={{0,1},{1,0},{2,3},{3,2},{4,5},{5,4},{6,7},{7,6},{8,9},{9,8},{10,11... | collective-permute-start | bytes 2211848 | tf_op jit(solution)/shard_map/ppermute | solution.py:194
  1.1 26.6 %collective-permute-start = (bf16[960,384]{1,0:T(8,128)(2,1)}, bf16[960,384]{1,0:T(8,128)(2,1)S(1)}, u32[]{:S(2)}, u32[]{:S(2)}) collective-permute-start(bf16[960,384]{1,0:T(8,128)(2,1)} %bitcast.13), channel_id=1, source_target_pairs={{0,2},{1,3},{2,0},{3,1},{4,6},{5,7},{6,4},{7,5},{8,10},{9,11},{10,... | collective-permute-start | bytes 2211848 | tf_op jit(solution)/shard_map/ppermute | solution.py:194
  3.7 9.8 %collective-permute-start.1 = (bf16[256,384]{1,0:T(8,128)(2,1)}, bf16[256,384]{1,0:T(8,128)(2,1)S(1)}, u32[]{:S(2)}, u32[]{:S(2)}) collective-permute-start(bf16[256,384]{1,0:T(8,128)(2,1)} %bitcast.6), channel_id=1, source_target_pairs={{0,4},{4,8},{8,12},{12,0},{1,5},{5,9},{9,13},{13,1},{2,6},{6,10},{... | collective-permute-start | bytes 589832 | tf_op jit(solution)/shard_map/ppermute | solution.py:190
  5.3 11.2 %collective-permute-start.3 = (bf16[256,384]{1,0:T(8,128)(2,1)}, bf16[256,384]{1,0:T(8,128)(2,1)S(1)}, u32[]{:S(2)}, u32[]{:S(2)}) collective-permute-start(bf16[256,384]{1,0:T(8,128)(2,1)} %bitcast.7), channel_id=1, source_target_pairs={{0,12},{4,0},{8,4},{12,8},{1,13},{5,1},{9,5},{13,9},{2,14},{6,2},{... | collective-permute-start | bytes 589832 | tf_op jit(solution)/shard_map/ppermute | solution.py:190
  7.5 14.4 %copy-start.5 = (bf16[1,128,768]{2,1,0:T(8,128)(2,1)S(1)}, bf16[1,128,768]{2,1,0:T(8,128)(2,1)}, u32[]{:S(2)}) copy-start(bf16[1,128,768]{2,1,0:T(8,128)(2,1)} %param.13) | copy-start | bytes 589828
  7.5 18.4 %copy-start.1 = (bf16[1,256,384]{2,1,0:T(8,128)(2,1)S(1)}, bf16[1,256,384]{2,1,0:T(8,128)(2,1)}, u32[]{:S(2)}) copy-start(bf16[1,256,384]{2,1,0:T(8,128)(2,1)} %param.7) | copy-start | bytes 589828
  7.5 18.4 %copy-start.2 = (f32[768]{0:T(1024)S(1)}, f32[768]{0:T(1024)}, u32[]{:S(2)}) copy-start(f32[768]{0:T(1024)} %bias.5) | copy-start | bytes 9220
  7.5 14.4 %collective-permute-start.5 = (bf16[128,768]{1,0:T(8,128)(2,1)}, bf16[128,768]{1,0:T(8,128)(2,1)S(1)}, u32[]{:S(2)}, u32[]{:S(2)}) collective-permute-start(bf16[128,768]{1,0:T(8,128)(2,1)} %bitcast.9), channel_id=1, source_target_pairs={{0,4},{4,8},{8,12},{12,0},{1,5},{5,9},{9,13},{13,1},{2,6},{6,10},{... | collective-permute-start | bytes 589832 | tf_op jit(solution)/shard_map/ppermute | solution.py:190
  16.5 9.4 %collective-permute-start.4 = (bf16[256,384]{1,0:T(8,128)(2,1)S(1)}, bf16[256,384]{1,0:T(8,128)(2,1)S(1)}, u32[]{:S(2)}, u32[]{:S(2)}) collective-permute-start(bf16[256,384]{1,0:T(8,128)(2,1)S(1)} %collective-permute-done.1.fa), channel_id=1, source_target_pairs={{0,4},{4,8},{8,12},{12,0},{1,5},{5,9},{9,13},{13,1},{2,6},{6,10},{... | collective-permute-start | bytes 589832 | tf_op jit(solution)/shard_map/ppermute | solution.py:190
  21.9 16.0 %collective-permute-start.8 = (bf16[128,768]{1,0:T(8,128)(2,1)S(1)}, bf16[128,768]{1,0:T(8,128)(2,1)S(1)}, u32[]{:S(2)}, u32[]{:S(2)}) collective-permute-start(bf16[128,768]{1,0:T(8,128)(2,1)S(1)} %collective-permute-done.5.ca), channel_id=1, source_target_pairs={{0,4},{4,8},{8,12},{12,0},{1,5},{5,9},{9,13},{13,1},{2,6},{6,10},{... | collective-permute-start | bytes 589832 | tf_op jit(solution)/shard_map/ppermute | solution.py:190
  21.9 16.0 %collective-permute-start.7 = (bf16[128,768]{1,0:T(8,128)(2,1)S(1)}, bf16[128,768]{1,0:T(8,128)(2,1)S(1)}, u32[]{:S(2)}, u32[]{:S(2)}) collective-permute-start(bf16[128,768]{1,0:T(8,128)(2,1)S(1)} %bitcast.10), channel_id=1, source_target_pairs={{0,12},{4,0},{8,4},{12,8},{1,13},{5,1},{9,5},{13,9},{2,14},{6,2},{... | collective-permute-start | bytes 589832 | tf_op jit(solution)/shard_map/ppermute | solution.py:190
  27.8 2.3 %copy-start = (bf16[768,1280]{1,0:T(8,128)(2,1)S(1)}, bf16[768,1280]{1,0:T(8,128)(2,1)}, u32[]{:S(2)}) copy-start(bf16[768,1280]{1,0:T(8,128)(2,1)} %aw.5) | copy-start | bytes 5898244
  27.8 2.3 %copy-start.3 = (f32[768]{0:T(1024)S(1)}, f32[768]{0:T(1024)}, u32[]{:S(2)}) copy-start(f32[768]{0:T(1024)} %gain.3) | copy-start | bytes 9220
  27.8 2.3 %collective-permute-start.6 = (bf16[960,384]{1,0:T(8,128)(2,1)S(1)}, bf16[960,384]{1,0:T(8,128)(2,1)S(1)}, u32[]{:S(2)}, u32[]{:S(2)}) collective-permute-start(bf16[960,384]{1,0:T(8,128)(2,1)S(1)} %collective-permute-done.w2), channel_id=1, source_target_pairs={{0,1},{1,0},{2,3},{3,2},{4,5},{5,4},{6,7},{7,6},{8,9},{9,8},{10,11... | collective-permute-start | bytes 2211848 | tf_op jit(solution)/shard_map/ppermute | solution.py:194
  35.2 2.8 %copy-start.4 = (bf16[768,768]{1,0:T(8,128)(2,1)S(1)}, bf16[768,768]{1,0:T(8,128)(2,1)}, u32[]{:S(2)}) copy-start(bf16[768,768]{1,0:T(8,128)(2,1)} %ow.3) | copy-start | bytes 3538948
  40.4 1.8 %collective-permute-start.9 = (bf16[192,768]{1,0:T(8,128)(2,1)S(1)}, bf16[192,768]{1,0:T(8,128)(2,1)S(1)}, u32[]{:S(2)}, u32[]{:S(2)}) collective-permute-start(bf16[192,768]{1,0:T(8,128)(2,1)S(1)} %get-tuple-element.53), channel_id=1, source_target_pairs={{0,1},{1,0},{2,3},{3,2},{4,5},{5,4},{6,7},{7,6},{8,9},{9,8},{10,11... | collective-permute-start | bytes 884744 | tf_op jit(solution)/shard_map/ppermute | solution.py:194
  44.1 1.4 %collective-permute-start.11 = (bf16[208,256]{1,0:T(8,128)(2,1)S(1)}, bf16[208,256]{1,0:T(8,128)(2,1)S(1)}, u32[]{:S(2)}, u32[]{:S(2)}) collective-permute-start(bf16[208,256]{1,0:T(8,128)(2,1)S(1)} %get-tuple-element.61), channel_id=1, source_target_pairs={{0,1},{1,0},{2,3},{3,2},{4,5},{5,4},{6,7},{7,6},{8,9},{9,8},{10,11... | collective-permute-start | bytes 319496 | tf_op jit(solution)/shard_map/ppermute | solution.py:194
  44.5 9.9 %collective-permute-start.10 = (bf16[192,768]{1,0:T(8,128)(2,1)S(1)}, bf16[192,768]{1,0:T(8,128)(2,1)S(1)}, u32[]{:S(2)}, u32[]{:S(2)}) collective-permute-start(bf16[192,768]{1,0:T(8,128)(2,1)S(1)} %add_convert_fusion.1), channel_id=1, source_target_pairs={{0,2},{1,3},{2,0},{3,1},{4,6},{5,7},{6,4},{7,5},{8,10},{9,11},{10,... | collective-permute-start | bytes 884744 | tf_op jit(solution)/shard_map/ppermute | solution.py:194
  45.5 10.3 %collective-permute-start.12 = (bf16[208,256]{1,0:T(8,128)(2,1)S(1)}, bf16[208,256]{1,0:T(8,128)(2,1)S(1)}, u32[]{:S(2)}, u32[]{:S(2)}) collective-permute-start(bf16[208,256]{1,0:T(8,128)(2,1)S(1)} %add_convert_fusion.3), channel_id=1, source_target_pairs={{0,2},{1,3},{2,0},{3,1},{4,6},{5,7},{6,4},{7,5},{8,10},{9,11},{10,... | collective-permute-start | bytes 319496 | tf_op jit(solution)/shard_map/ppermute | solution.py:194
  54.5 1.5 %collective-permute-start.13 = (bf16[96,768]{1,0:T(8,128)(2,1)S(1)}, bf16[96,768]{1,0:T(8,128)(2,1)S(1)}, u32[]{:S(2)}, u32[]{:S(2)}) collective-permute-start(bf16[96,768]{1,0:T(8,128)(2,1)S(1)} %get-tuple-element.68), channel_id=1, source_target_pairs={{0,1},{1,0},{2,3},{3,2},{4,5},{5,4},{6,7},{7,6},{8,9},{9,8},{10,11... | collective-permute-start | bytes 442376 | tf_op jit(solution)/shard_map/ppermute | solution.py:194
  55.9 1.9 %collective-permute-start.15 = (bf16[208,256]{1,0:T(8,128)(2,1)S(1)}, bf16[208,256]{1,0:T(8,128)(2,1)S(1)}, u32[]{:S(2)}, u32[]{:S(2)}) collective-permute-start(bf16[208,256]{1,0:T(8,128)(2,1)S(1)} %add_convert_fusion.2.whole_k), channel_id=1, source_target_pairs={{0,1},{1,0},{2,3},{3,2},{4,5},{5,4},{6,7},{7,6},{8,9},{9,8},{10,11... | collective-permute-start | bytes 319496 | tf_op jit(solution)/shard_map/ppermute | solution.py:194
  56.0 1.8 %collective-permute-start.14 = (bf16[96,768]{1,0:T(8,128)(2,1)S(1)}, bf16[96,768]{1,0:T(8,128)(2,1)S(1)}, u32[]{:S(2)}, u32[]{:S(2)}) collective-permute-start(bf16[96,768]{1,0:T(8,128)(2,1)S(1)} %get-tuple-element.64), channel_id=1, source_target_pairs={{0,1},{1,0},{2,3},{3,2},{4,5},{5,4},{6,7},{7,6},{8,9},{9,8},{10,11... | collective-permute-start | bytes 442376 | tf_op jit(solution)/shard_map/ppermute | solution.py:194

commit v3 on v2

--- a/solution.py
+++ b/solution.py
@@ -165,6 +165,7 @@
 F32, BF16 = jnp.float32, jnp.bfloat16
 SEQ, DP = 4, 4
 TOK = 128
+EDGE = 16
 LEN = SEQ * TOK
 CIN, WIDTH = 384, 768
 SHARD = WIDTH // DP
@@ -220,31 +221,56 @@
     put_shards(taps, w0, w1, lax.rem(lax.axis_index("dp"), 2))
 
 
-def near_kernel(f0, fa, fb, fc, taps, bias, windows, hid, positions):
-    z, d = lax.axis_index("seq"), lax.axis_index("dp")
+def fill_positions(positions, z, parts):
     chunk = 2 * TOK
     for g in range(CIN // 128):
         positions[g, 0:8, :] = jnp.zeros((8, 128), F32)
         positions[g, 8 + 2 * LEN :, :] = jnp.zeros((8, 128), F32)
-        for ref, off in ((f0, 0), (fa, 3), (fb, 1), (fc, 2)):
+        for ref, off in parts:
             start = pl.multiple_of(lax.rem(z + off, SEQ) * chunk + 8, 8)
-            positions[g, pl.ds(start, chunk), :] = ref[:, g * 128 : (g + 1) * 128].astype(F32)
+            if ref is None:
+                positions[g, pl.ds(start, chunk), :] = jnp.zeros((chunk, 128), F32)
+            else:
+                positions[g, pl.ds(start, chunk), :] = ref[:, g * 128 : (g + 1) * 128].astype(F32)
+
+
+def near_kernel(f0, fa, fb, taps, bias, windows, hid, positions):
+    z, d = lax.axis_index("seq"), lax.axis_index("dp")
+    fill_positions(positions, z, ((f0, 0), (fa, 3), (fb, 1), (None, 2)))
+    for g in range(CIN // 128):
         for k in range(6):
             at = k * CIN + g * 128
             windows[:, at : at + 128] = positions[g, pl.ds(6 + k, LEN, stride=2), :].astype(BF16)
-    hid[...] = filtered_half(windows[: LEN // 2, :], taps, half_of(bias, d // 2))
-
-
-def rest_kernel(windows, taps, bias, hid):
-    hid[...] = filtered_half(windows[LEN // 2 :, :], taps, half_of(bias, lax.axis_index("dp") // 2))
-
-
-def project_kernel(windows, hid_near, hid_rest, w2, w3, bias, gain, aw, hid, normed, proj, normed_t, taps):
+    hid[...] = filtered_half(windows, taps, half_of(bias, d // 2))
+
+
+def row_picker(z):
+    row = lax.broadcasted_iota(jnp.int32, (ROWS, WIDTH), 0)
+    lane = lax.broadcasted_iota(jnp.int32, (ROWS, WIDTH), 1)
+    return jnp.where(lane == row + z * ROWS, 1.0, 0.0).astype(BF16)
+
+
+def mend_kernel(fa, fb, fc, windows_in, hid_in, taps, bias, windows, hid, positions):
+    z, d = lax.axis_index("seq"), lax.axis_index("dp")
+    fill_positions(positions, z, ((fa, 3), (fb, 1), (fc, 2)))
+    windows[...] = windows_in[...]
+    hid[...] = hid_in[...]
+    first = jnp.clip(lax.rem(z + 2, SEQ) * TOK - EDGE, 0, LEN - TOK - 2 * EDGE)
+    first = pl.multiple_of(first, EDGE)
+    fresh = pl.ds(first, TOK + 2 * EDGE)
+    for g in range(CIN // 128):
+        for k in range(6):
+            at = k * CIN + g * 128
+            spots = pl.ds(2 * first + (6 + k), TOK + 2 * EDGE, stride=2)
+            windows[fresh, at : at + 128] = positions[g, spots, :].astype(BF16)
+    hid[fresh, :] = filtered_half(windows[fresh, :], taps, half_of(bias, d // 2))
+
+
+def project_kernel(windows, hid_near, w2, w3, bias, gain, aw, hid, normed, proj, normed_t, taps):
     z, d = lax.axis_index("seq"), lax.axis_index("dp")
     side, half = d // 2, WIDTH // 2
     put_shards(taps, w2, w3, lax.rem(d, 2))
-    hid[side, : LEN // 2, :] = hid_near[...]
-    hid[side, LEN // 2 :, :] = hid_rest[...]
+    hid[side] = hid_near[...]
     hid[1 - side] = filtered_half(windows, taps, half_of(bias, 1 - side))
     low, high = hid[0].astype(F32), hid[1].astype(F32)
     square = jnp.sum(low * low, axis=1, keepdims=True) + jnp.sum(high * high, axis=1, keepdims=True)
@@ -253,11 +279,7 @@
     normed[:, :half] = (low * inv * scales[:, :half]).astype(BF16)
     normed[:, half:] = (high * inv * scales[:, half:]).astype(BF16)
     proj[...] = mm(normed[...], aw[...]).astype(BF16)
-    for at in range(SEQ):
-
-        @pl.when(z == at)
-        def _():
-            normed_t[...] = normed[:, at * ROWS : (at + 1) * ROWS].T
+    normed_t[...] = mm(row_picker(z), normed[...], NT).astype(BF16)
 
 
 def heads_of(proj, h):
@@ -306,12 +328,7 @@
     for ref, off in ((c0, 0), (ca, 3), (cb, 1), (cc, 2)):
         start = pl.multiple_of(lax.rem(z + off, SEQ) * TOK, TOK)
         cot[pl.ds(start, TOK), :] = ref[...]
-    for at in range(SEQ):
-
-        @pl.when(z == at)
-        def _():
-            cot_t[...] = cot[:, at * ROWS : (at + 1) * ROWS].T
-
+    cot_t[...] = mm(row_picker(z), cot[...], NT).astype(BF16)
     grad[...] = mm(cot[...], ow[...]).astype(BF16)
     out_part = mm(cot_t[...], att_t[...], NT)
     for h in range(HEADS):
@@ -373,21 +390,20 @@
     both_ways(write, keep, send, lax.rem(d, 2))
 
 
-def finish_kernel(whole_v, whole_k, top_v, rest_v, other_k, grad_attend, grad_output, grad_gain):
+def finish_kernel(whole_v, whole_k, other_v, other_k, grad_attend, grad_output, grad_gain):
     half = VW // 2
 
-    def place(source, rows, side):
+    def place(source, side):
         lanes = slice(side * half, (side + 1) * half)
-        grad_attend[rows, 2 * QW + side * half : 2 * QW + (side + 1) * half] = source[:, :half].astype(F32)
-        grad_output[rows, lanes] = source[:, half:].astype(F32)
+        grad_attend[:, 2 * QW + side * half : 2 * QW + (side + 1) * half] = source[:, :half].astype(F32)
+        grad_output[:, lanes] = source[:, half:].astype(F32)
 
     for at in range(2):
 
         @pl.when(lax.rem(lax.axis_index("dp"), 2) == at)
         def _():
-            place(whole_v, slice(0, ROWS), at)
-            place(top_v, slice(0, ROWS // 2), 1 - at)
-            place(rest_v, slice(ROWS // 2, ROWS), 1 - at)
+            place(whole_v, at)
+            place(other_v, 1 - at)
             low, high = (whole_k, other_k) if at == 0 else (other_k, whole_k)
             grad_attend[:, :QW] = low[:ROWS, :].astype(F32)
             grad_attend[:, QW : 2 * QW] = high[:ROWS, :].astype(F32)
@@ -433,42 +449,46 @@
     far_a, taps = lax.optimization_barrier((fa, taps))
     to_left, far_a, fb = lax.optimization_barrier((c0, far_a, fb))
     fc = ring(far_a, 1)
-    cb, cc = ring(to_left, SEQ - 1), ring(ca, 1)
-    fc, ca = lax.optimization_barrier((fc, ca))
     windows, hid_near = kernel_call(
         near_kernel,
-        [((LEN, 6 * CIN), BF16), ((LEN // 2, half), BF16)],
+        [((LEN, 6 * CIN), BF16), ((LEN, half), BF16)],
         [((CIN // 128, 16 + 2 * LEN, 128), F32)],
-        1 << 16,
-        f0, fa, fb, fc, taps, filter_bias,
-    )
-    w2, windows = lax.optimization_barrier((w2, windows))
+        1 << 24,
+        f0, fa, fb, taps, filter_bias,
+    )
+    ca, windows = lax.optimization_barrier((ca, windows))
+    cb, cc = ring(to_left, SEQ - 1), ring(ca, 1)
+    w2, fc, windows = lax.optimization_barrier((w2, fc, windows))
     w3 = swap(w2, 1)
-    (hid_rest,) = kernel_call(
-        rest_kernel, [((LEN // 2, half), BF16)], [], 1 << 33, windows, taps, filter_bias
+    windows, hid_near = kernel_call(
+        mend_kernel,
+        [((LEN, 6 * CIN), BF16), ((LEN, half), BF16)],
+        [((CIN // 128, 16 + 2 * LEN, 128), F32)],
+        1 << 33,
+        fa, fb, fc, windows, hid_near, taps, filter_bias,
     )
     hid, normed, proj, normed_t = kernel_call(
         project_kernel,
         [((2, LEN, half), BF16), ((LEN, WIDTH), BF16), ((LEN, PROJ), BF16), ((ROWS, LEN), BF16)],
         [((2 * SHARD, 5 * CIN), BF16)],
-        1 << 24,
-        windows, hid_near, hid_rest, w2, w3, filter_bias, norm_gain, attend_weight,
+        1 << 33,
+        windows, hid_near, w2, w3, filter_bias, norm_gain, attend_weight,
     )
     probs_t, att_t = kernel_call(
         attend_kernel,
         [((HEADS, LEN, LEN), BF16), ((VW, LEN), BF16)],
         [],
-        1 << 31,
+        1 << 33,
         proj,
     )
     (outputs,) = kernel_call(
-        outputs_kernel, [((TOK, WIDTH), F32)], [], 1 << 31, hid, att_t, output_weight
+        outputs_kernel, [((TOK, WIDTH), F32)], [], 1 << 16, hid, att_t, output_weight
     )
     grad, keep_v, send_v, mixed = kernel_call(
         value_kernel,
         [((LEN, VW), BF16), ((ROWS, VW), F32), ((ROWS, VW), BF16), ((ROWS, 128), F32)],
         [((LEN, WIDTH), BF16), ((ROWS, LEN), BF16), ((LEN, VW), BF16)],
-        1 << 33,
+        1 << 29,
         c0, ca, cb, cc, normed_t, probs_t, att_t, attend_weight, output_weight,
     )
     query_early, key_early = kernel_call(
@@ -484,24 +504,20 @@
         late_key_kernel,
         [((ROWS + 16, QW), F32), ((ROWS + 16, QW), BF16)],
         [((QW // 2, LEN), BF16), ((LEN, QW // 2), BF16)],
-        1 << 29,
+        1 << 33,
         grad, proj, probs_t, query_early, key_early, normed_t, mixed, norm_gain, attend_weight,
     )
     arrived_v = swap(part_v, 2)
     part_k = combined(keep_k, swap(send_k, 1))
     arrived_k = swap(part_k, 2)
-    arrived_v = lax.optimization_barrier((arrived_v, part_k))[0]
     whole_v, whole_k = combined(part_v, arrived_v), combined(part_k, arrived_k)
-    other_k = swap(whole_k, 1)
-    top = swap(whole_v[: ROWS // 2], 1)
-    rest, top = lax.optimization_barrier((whole_v[ROWS // 2 :], top))
-    other_v = (top, swap(rest, 1))
+    other_v, other_k = swap(whole_v, 1), swap(whole_k, 1)
     grad_attend, grad_output, grad_gain = kernel_call(
         finish_kernel,
         [((ROWS, PROJ), F32), ((ROWS, WIDTH), F32), ((ROWS,), F32)],
         [],
-        1 << 24,
-        whole_v, whole_k, *other_v, other_k,
+        1 << 31,
+        whole_v, whole_k, other_v, other_k,
     )
     return outputs[None], grad_attend, grad_output, grad_gain
 

time: 59.1 us -> 56 us (0.948)
  waiting for transfers between devices: 22 us -> 19.3 us
    ppermute x6, waiting for transfers between devices: 11.5 us -> 8.89 us  [ring(): lax.ppermute(value, 'seq', [(i, (i + step) % SEQ) for i in range(SEQ)])]
    ppermute x10 -> x9, starting transfers between devices: 5.9 us -> 5.32 us  [swap(): return lax.ppermute(value, 'dp', [(i, i ^ bit) for i in range(DP)])]
    ppermute x10 -> x9, waiting for transfers between devices: 10.5 us -> 10.5 us  [swap(): return lax.ppermute(value, 'dp', [(i, i ^ bit) for i in range(DP)])]
  transfers between devices with their start and end apart: 16 -> 15, of which waited for: 8 -> 8; matrix products, arithmetic and copies ran while one was open for 0% -> 0% of each run, Pallas kernels for 26% -> 28%
where the time goes in v3:
time: 56 us; the launch traced here: 55.8 us
  Pallas kernels  20.9 us (37%)
  waiting for transfers between devices  19.3 us (34%)
  starting transfers between devices  14.7 us (26%)
  between operations  0.76 us (1%)
    pallas_call x10, Pallas kernels, kernel_call(): pl.pallas_call(body, in_specs=[away if i in far else whole for i in range...  20.9 us
    ppermute x9, waiting for transfers between devices, swap(): return lax.ppermute(value, 'dp', [(i, i ^ bit) for i in range(DP)])  10.5 us
    ppermute x6, starting transfers between devices, ring(): lax.ppermute(value, 'seq', [(i, (i + step) % SEQ) for i in range(SEQ)])  9.34 us
    ppermute x6, waiting for transfers between devices, ring(): lax.ppermute(value, 'seq', [(i, (i + step) % SEQ) for i in range(SEQ)])  8.89 us
    ppermute x9, starting transfers between devices, swap(): return lax.ppermute(value, 'dp', [(i, i ^ bit) for i in range(DP)])  5.32 us
  transfers between devices with their start and end apart: 15, of which 8 were waited for; matrix products, arithmetic and copies ran while one was open for 0% of the time, Pallas kernels for 28%

profile of v3, /device:TPU:0, one launch (start us, length us, event | category | flops | bytes accessed | tf_op | source)
XLA Modules:
  0.0 55.8 jit_solution(2661180656410392700)
XLA Ops:
  0.6 0.5 collective-permute-start.1
  1.1 2.6 %collective-permute-start.3 = (bf16[960,384]{1,0:T(8,128)(2,1)}, bf16[960,384]{1,0:T(8,128)(2,1)S(1)}, u32[]{:S(2)}, u32[]{:S(2)}) collective-permute-start(bf16[960,384]{1,0:T(8,128)(2,1)} %bitcast.14), channel_id=1, source_target_pairs={{0,2},{1,3},{2,0},{3,1},{4,6},{5,7},{6,4},{7,5},{8,10},{9,11},{10,... | collective-permute-start | bytes 2211848 | tf_op jit(solution)/shard_map/ppermute | solution.py:195
  3.7 1.6 %collective-permute-start = (bf16[256,384]{1,0:T(8,128)(2,1)}, bf16[256,384]{1,0:T(8,128)(2,1)S(1)}, u32[]{:S(2)}, u32[]{:S(2)}) collective-permute-start(bf16[256,384]{1,0:T(8,128)(2,1)} %bitcast.9), channel_id=1, source_target_pairs={{0,4},{4,8},{8,12},{12,0},{1,5},{5,9},{9,13},{13,1},{2,6},{6,10},{... | collective-permute-start | bytes 589832 | tf_op jit(solution)/shard_map/ppermute | solution.py:191
  5.3 2.2 %collective-permute-start.2 = (bf16[256,384]{1,0:T(8,128)(2,1)}, bf16[256,384]{1,0:T(8,128)(2,1)S(1)}, u32[]{:S(2)}, u32[]{:S(2)}) collective-permute-start(bf16[256,384]{1,0:T(8,128)(2,1)} %bitcast.10), channel_id=1, source_target_pairs={{0,12},{4,0},{8,4},{12,8},{1,13},{5,1},{9,5},{13,9},{2,14},{6,2},{... | collective-permute-start | bytes 589832 | tf_op jit(solution)/shard_map/ppermute | solution.py:191
  7.6 1.3 %shard_map.102.taps = bf16[384,1920]{1,0:T(8,128)(2,1)S(1)} custom-call(bf16[960,384]{1,0:T(8,128)(2,1)} %bitcast.15, bf16[960,384]{1,0:T(8,128)(2,1)S(1)} %collective-permute-done.1.w1), custom_call_target="tpu_custom_call" | custom-call | flops 2147483648 | bytes 65536 | tf_op jit(solution)/shard_map/pallas_call | solution.py:417
  8.9 4.6 %collective-permute-done.fa = bf16[256,384]{1,0:T(8,128)(2,1)S(1)} collective-permute-done((bf16[256,384]{1,0:T(8,128)(2,1)}, bf16[256,384]{1,0:T(8,128)(2,1)S(1)}, u32[]{:S(2)}, u32[]{:S(2)}) %collective-permute-start) | collective-permute-done | bytes 196640 | tf_op jit(solution)/shard_map/ppermute | solution.py:191
  13.5 3.0 %collective-permute-done.2.fb = bf16[256,384]{1,0:T(8,128)(2,1)S(1)} collective-permute-done((bf16[256,384]{1,0:T(8,128)(2,1)}, bf16[256,384]{1,0:T(8,128)(2,1)S(1)}, u32[]{:S(2)}, u32[]{:S(2)}) %collective-permute-start.2) | collective-permute-done | bytes 196640 | tf_op jit(solution)/shard_map/ppermute | solution.py:191
  16.5 1.7 %collective-permute-start.4 = (bf16[256,384]{1,0:T(8,128)(2,1)S(1)}, bf16[256,384]{1,0:T(8,128)(2,1)S(1)}, u32[]{:S(2)}, u32[]{:S(2)}) collective-permute-start(bf16[256,384]{1,0:T(8,128)(2,1)S(1)} %collective-permute-done.fa), channel_id=1, source_target_pairs={{0,4},{4,8},{8,12},{12,0},{1,5},{5,9},{9,13},{13,1},{2,6},{6,10},{... | collective-permute-start | bytes 589832 | tf_op jit(solution)/shard_map/ppermute | solution.py:191
  18.2 2.6 %shard_map.103 = (bf16[512,2304]{1,0:T(8,128)(2,1)S(1)}, bf16[512,384]{1,0:T(8,128)(2,1)S(1)}) custom-call(bf16[256,384]{1,0:T(8,128)(2,1)S(1)} %bitcast.11, bf16[256,384]{1,0:T(8,128)(2,1)S(1)} %collective-permute-done.fa, bf16[256,384]{1,0:T(8,128)(2,1)S(1)} %collective-permute-done.2.fb, bf16[384,1920]{1,0:T(8,128)(2,1)S(1)} %shard_map.102.taps, ...), custom_call_target="tpu_custom_call" | custom-call | flops 16777216 | bytes 65536 | tf_op jit(solution)/shard_map/pallas_call | solution.py:417
  20.8 1.1 %collective-permute-done.5.ca = bf16[128,768]{1,0:T(8,128)(2,1)S(1)} collective-permute-done((bf16[128,768]{1,0:T(8,128)(2,1)}, bf16[128,768]{1,0:T(8,128)(2,1)S(1)}, u32[]{:S(2)}, u32[]{:S(2)}) %collective-permute-start.5) | collective-permute-done | bytes 196640 | tf_op jit(solution)/shard_map/ppermute | solution.py:191
  21.9 3.8 %collective-permute-start.7 = (bf16[128,768]{1,0:T(8,128)(2,1)S(1)}, bf16[128,768]{1,0:T(8,128)(2,1)S(1)}, u32[]{:S(2)}, u32[]{:S(2)}) collective-permute-start(bf16[128,768]{1,0:T(8,128)(2,1)S(1)} %bitcast.7), channel_id=1, source_target_pairs={{0,12},{4,0},{8,4},{12,8},{1,13},{5,1},{9,5},{13,9},{2,14},{6,2},{... | collective-permute-start | bytes 589832 | tf_op jit(solution)/shard_map/ppermute | solution.py:191
  25.9 1.4 %shard_map.104 = (bf16[512,2304]{1,0:T(8,128)(2,1)S(1)}, bf16[512,384]{1,0:T(8,128)(2,1)S(1)}) custom-call(bf16[256,384]{1,0:T(8,128)(2,1)S(1)} %collective-permute-done.fa, bf16[256,384]{1,0:T(8,128)(2,1)S(1)} %collective-permute-done.2.fb, bf16[256,384]{1,0:T(8,128)(2,1)S(1)} %collective-permute-done.4.fc, ...), custom_call_target="tpu_custom_call" | custom-call | flops 8589934592 | bytes 65536 | tf_op jit(solution)/shard_map/pallas_call | solution.py:417
  27.4 0.8 %collective-permute-done.6.w3 = bf16[960,384]{1,0:T(8,128)(2,1)S(1)} collective-permute-done((bf16[960,384]{1,0:T(8,128)(2,1)S(1)}, bf16[960,384]{1,0:T(8,128)(2,1)S(1)}, u32[]{:S(2)}, u32[]{:S(2)}) %collective-permute-start.6) | collective-permute-done | bytes 737312 | tf_op jit(solution)/shard_map/ppermute | solution.py:195
  28.2 4.4 %shard_map.105 = (bf16[2,512,384]{2,1,0:T(8,128)(2,1)S(1)}, bf16[512,768]{1,0:T(8,128)(2,1)}, bf16[512,1280]{1,0:T(8,128)(2,1)S(1)}, bf16[192,512]{1,0:T(8,128)(2,1)S(1)}) custom-call(bf16[512,2304]{1,0:T(8,128)(2,1)S(1)} %get-tuple-element.45.windows, bf16[512,384]{1,0:T(8,128)(2,1)S(1)} %get-tuple-element.46.hid_near, ...), custom_call_target="tpu_custom_call" | custom-call | flops 8589934592 | bytes 65536 | tf_op jit(solution)/shard_map/pallas_call | solution.py:417
  32.6 2.7 %shard_map.106 = (bf16[4,512,512]{2,1,0:T(8,128)(2,1)S(1)}, bf16[768,512]{1,0:T(8,128)(2,1)S(1)}) custom-call(bf16[512,1280]{1,0:T(8,128)(2,1)S(1)} %get-tuple-element.49.proj), custom_call_target="tpu_custom_call" | custom-call | flops 8589934592 | bytes 65536 | tf_op jit(solution)/shard_map/pallas_call | solution.py:417
  35.3 2.4 %shard_map.108 = (bf16[512,768]{1,0:T(8,128)(2,1)S(1)}, f32[192,768]{1,0:T(8,128)S(1)}, bf16[192,768]{1,0:T(8,128)(2,1)S(1)}, f32[192,128]{1,0:T(8,128)S(1)}) custom-call(bf16[128,768]{1,0:T(8,128)(2,1)S(1)} %bitcast.8, bf16[128,768]{1,0:T(8,128)(2,1)S(1)} %collective-permute-done.5.ca, bf16[128,768]{1,0:T(8,128)(2,1)S(1)} %collective-permute-done.7.cb, ...), custom_call_target="tpu_custom_call" | custom-call | flops 536870912 | bytes 65536 | tf_op jit(solution)/shard_map/pallas_call | solution.py:417
  37.9 1.6 %shard_map.109 = (bf16[128,512]{1,0:T(8,128)(2,1)S(1)}, bf16[512,128]{1,0:T(8,128)(2,1)S(1)}) custom-call(bf16[512,768]{1,0:T(8,128)(2,1)S(1)} %get-tuple-element.57.grad, bf16[512,1280]{1,0:T(8,128)(2,1)S(1)} %get-tuple-element.49.proj, bf16[4,512,512]{2,1,0:T(8,128)(2,1)S(1)} %get-tuple-element.54.probs_t), custom_call_target="tpu_custom_call" | custom-call | flops 16777216 | bytes 65536 | tf_op jit(solution)/shard_map/pallas_call | solution.py:417
  39.6 1.8 %shard_map.110 = (f32[208,256]{1,0:T(8,128)S(1)}, bf16[208,256]{1,0:T(8,128)(2,1)S(1)}) custom-call(bf16[512,768]{1,0:T(8,128)(2,1)S(1)} %get-tuple-element.57.grad, bf16[512,1280]{1,0:T(8,128)(2,1)S(1)} %get-tuple-element.49.proj, bf16[4,512,512]{2,1,0:T(8,128)(2,1)S(1)} %get-tuple-element.54.probs_t, bf16[128,512]{1,0:T(8,128)(2,1)S(1)} %get-tuple-element.60.query_early, ...), custom_call_target="tpu_custom_call" | custom-call | flops 8589934592 | bytes 65536 | tf_op jit(solution)/shard_map/pallas_call | solution.py:417
  42.2 0.7 %collective-permute-done.11 = bf16[208,256]{1,0:T(8,128)(2,1)S(1)} collective-permute-done((bf16[208,256]{1,0:T(8,128)(2,1)S(1)}, bf16[208,256]{1,0:T(8,128)(2,1)S(1)}, u32[]{:S(2)}, u32[]{:S(2)}) %collective-permute-start.11) | collective-permute-done | bytes 106528 | tf_op jit(solution)/shard_map/ppermute | solution.py:195
  42.9 1.1 %collective-permute-start.12 = (bf16[208,256]{1,0:T(8,128)(2,1)S(1)}, bf16[208,256]{1,0:T(8,128)(2,1)S(1)}, u32[]{:S(2)}, u32[]{:S(2)}) collective-permute-start(bf16[208,256]{1,0:T(8,128)(2,1)S(1)} %add_convert_fusion.3), channel_id=1, source_target_pairs={{0,2},{1,3},{2,0},{3,1},{4,6},{5,7},{6,4},{7,5},{8,10},{9,11},{10,... | collective-permute-start | bytes 319496 | tf_op jit(solution)/shard_map/ppermute | solution.py:195
  44.0 7.7 %collective-permute-done.10 = bf16[192,768]{1,0:T(8,128)(2,1)S(1)} collective-permute-done((bf16[192,768]{1,0:T(8,128)(2,1)S(1)}, bf16[192,768]{1,0:T(8,128)(2,1)S(1)}, u32[]{:S(2)}, u32[]{:S(2)}) %collective-permute-start.10) | collective-permute-done | bytes 294944 | tf_op jit(solution)/shard_map/ppermute | solution.py:195
  51.9 1.3 %collective-permute-done.12 = bf16[208,256]{1,0:T(8,128)(2,1)S(1)} collective-permute-done((bf16[208,256]{1,0:T(8,128)(2,1)S(1)}, bf16[208,256]{1,0:T(8,128)(2,1)S(1)}, u32[]{:S(2)}, u32[]{:S(2)}) %collective-permute-start.12) | collective-permute-done | bytes 106528 | tf_op jit(solution)/shard_map/ppermute | solution.py:195
  53.3 1.3 %shard_map.107 = f32[128,768]{1,0:T(8,128)} custom-call(bf16[2,512,384]{2,1,0:T(8,128)(2,1)S(1)} %get-tuple-element.48.hid, bf16[768,512]{1,0:T(8,128)(2,1)S(1)} %get-tuple-element.50.att_t, bf16[768,768]{1,0:T(8,128)(2,1)S(1)} %copy-done), custom_call_target="tpu_custom_call" | custom-call | flops 65536 | bytes 65536 | tf_op jit(solution)/shard_map/pallas_call | solution.py:417
  54.6 1.2 %shard_map.111 = (f32[192,1280]{1,0:T(8,128)}, f32[192,768]{1,0:T(8,128)}, f32[192]{0:T(256)}) custom-call(bf16[192,768]{1,0:T(8,128)(2,1)S(1)} %add_convert_fusion.whole_v, bf16[208,256]{1,0:T(8,128)(2,1)S(1)} %add_convert_fusion.2.whole_k, bf16[192,768]{1,0:T(8,128)(2,1)S(1)} %collective-permute-done.13.other_v, ...), custom_call_target="tpu_custom_call" | custom-call | flops 2147483648 | bytes 65536 | tf_op jit(solution)/shard_map/pallas_call | solution.py:417
  (32 shorter events, 1.5 us)
Async XLA Ops:
  0.6 6.9 %collective-permute-start.1 = (bf16[960,384]{1,0:T(8,128)(2,1)}, bf16[960,384]{1,0:T(8,128)(2,1)S(1)}, u32[]{:S(2)}, u32[]{:S(2)}) collective-permute-start(bf16[960,384]{1,0:T(8,128)(2,1)} %bitcast.13), channel_id=1, source_target_pairs={{0,1},{1,0},{2,3},{3,2},{4,5},{5,4},{6,7},{7,6},{8,9},{9,8},{10,11... | collective-permute-start | bytes 2211848 | tf_op jit(solution)/shard_map/ppermute | solution.py:195
  1.1 24.6 %collective-permute-start.3 = (bf16[960,384]{1,0:T(8,128)(2,1)}, bf16[960,384]{1,0:T(8,128)(2,1)S(1)}, u32[]{:S(2)}, u32[]{:S(2)}) collective-permute-start(bf16[960,384]{1,0:T(8,128)(2,1)} %bitcast.14), channel_id=1, source_target_pairs={{0,2},{1,3},{2,0},{3,1},{4,6},{5,7},{6,4},{7,5},{8,10},{9,11},{10,... | collective-permute-start | bytes 2211848 | tf_op jit(solution)/shard_map/ppermute | solution.py:195
  3.7 9.8 %collective-permute-start = (bf16[256,384]{1,0:T(8,128)(2,1)}, bf16[256,384]{1,0:T(8,128)(2,1)S(1)}, u32[]{:S(2)}, u32[]{:S(2)}) collective-permute-start(bf16[256,384]{1,0:T(8,128)(2,1)} %bitcast.9), channel_id=1, source_target_pairs={{0,4},{4,8},{8,12},{12,0},{1,5},{5,9},{9,13},{13,1},{2,6},{6,10},{... | collective-permute-start | bytes 589832 | tf_op jit(solution)/shard_map/ppermute | solution.py:191
  5.3 11.2 %collective-permute-start.2 = (bf16[256,384]{1,0:T(8,128)(2,1)}, bf16[256,384]{1,0:T(8,128)(2,1)S(1)}, u32[]{:S(2)}, u32[]{:S(2)}) collective-permute-start(bf16[256,384]{1,0:T(8,128)(2,1)} %bitcast.10), channel_id=1, source_target_pairs={{0,12},{4,0},{8,4},{12,8},{1,13},{5,1},{9,5},{13,9},{2,14},{6,2},{... | collective-permute-start | bytes 589832 | tf_op jit(solution)/shard_map/ppermute | solution.py:191
  7.5 10.7 %copy-start.3 = (bf16[1,256,384]{2,1,0:T(8,128)(2,1)S(1)}, bf16[1,256,384]{2,1,0:T(8,128)(2,1)}, u32[]{:S(2)}) copy-start(bf16[1,256,384]{2,1,0:T(8,128)(2,1)} %param.7) | copy-start | bytes 589828
  7.5 10.7 %copy-start.4 = (f32[768]{0:T(1024)S(1)}, f32[768]{0:T(1024)}, u32[]{:S(2)}) copy-start(f32[768]{0:T(1024)} %bias.5) | copy-start | bytes 9220
  7.5 14.4 %collective-permute-start.5 = (bf16[128,768]{1,0:T(8,128)(2,1)}, bf16[128,768]{1,0:T(8,128)(2,1)S(1)}, u32[]{:S(2)}, u32[]{:S(2)}) collective-permute-start(bf16[128,768]{1,0:T(8,128)(2,1)} %bitcast.6), channel_id=1, source_target_pairs={{0,4},{4,8},{8,12},{12,0},{1,5},{5,9},{9,13},{13,1},{2,6},{6,10},{... | collective-permute-start | bytes 589832 | tf_op jit(solution)/shard_map/ppermute | solution.py:191
  8.9 13.1 %copy-start.2 = (bf16[1,128,768]{2,1,0:T(8,128)(2,1)S(1)}, bf16[1,128,768]{2,1,0:T(8,128)(2,1)}, u32[]{:S(2)}) copy-start(bf16[1,128,768]{2,1,0:T(8,128)(2,1)} %param.13) | copy-start | bytes 589828
  16.5 9.4 %collective-permute-start.4 = (bf16[256,384]{1,0:T(8,128)(2,1)S(1)}, bf16[256,384]{1,0:T(8,128)(2,1)S(1)}, u32[]{:S(2)}, u32[]{:S(2)}) collective-permute-start(bf16[256,384]{1,0:T(8,128)(2,1)S(1)} %collective-permute-done.fa), channel_id=1, source_target_pairs={{0,4},{4,8},{8,12},{12,0},{1,5},{5,9},{9,13},{13,1},{2,6},{6,10},{... | collective-permute-start | bytes 589832 | tf_op jit(solution)/shard_map/ppermute | solution.py:191
  21.9 13.4 %collective-permute-start.8 = (bf16[128,768]{1,0:T(8,128)(2,1)S(1)}, bf16[128,768]{1,0:T(8,128)(2,1)S(1)}, u32[]{:S(2)}, u32[]{:S(2)}) collective-permute-start(bf16[128,768]{1,0:T(8,128)(2,1)S(1)} %collective-permute-done.5.ca), channel_id=1, source_target_pairs={{0,4},{4,8},{8,12},{12,0},{1,5},{5,9},{9,13},{13,1},{2,6},{6,10},{... | collective-permute-start | bytes 589832 | tf_op jit(solution)/shard_map/ppermute | solution.py:191
  21.9 13.4 %collective-permute-start.7 = (bf16[128,768]{1,0:T(8,128)(2,1)S(1)}, bf16[128,768]{1,0:T(8,128)(2,1)S(1)}, u32[]{:S(2)}, u32[]{:S(2)}) collective-permute-start(bf16[128,768]{1,0:T(8,128)(2,1)S(1)} %bitcast.7), channel_id=1, source_target_pairs={{0,12},{4,0},{8,4},{12,8},{1,13},{5,1},{9,5},{13,9},{2,14},{6,2},{... | collective-permute-start | bytes 589832 | tf_op jit(solution)/shard_map/ppermute | solution.py:191
  25.9 2.2 %collective-permute-start.6 = (bf16[960,384]{1,0:T(8,128)(2,1)S(1)}, bf16[960,384]{1,0:T(8,128)(2,1)S(1)}, u32[]{:S(2)}, u32[]{:S(2)}) collective-permute-start(bf16[960,384]{1,0:T(8,128)(2,1)S(1)} %collective-permute-done.3.w2), channel_id=1, source_target_pairs={{0,1},{1,0},{2,3},{3,2},{4,5},{5,4},{6,7},{7,6},{8,9},{9,8},{10,11... | collective-permute-start | bytes 2211848 | tf_op jit(solution)/shard_map/ppermute | solution.py:195
  25.9 2.2 %copy-start.1 = (bf16[768,1280]{1,0:T(8,128)(2,1)S(1)}, bf16[768,1280]{1,0:T(8,128)(2,1)}, u32[]{:S(2)}) copy-start(bf16[768,1280]{1,0:T(8,128)(2,1)} %aw.5) | copy-start | bytes 5898244
  25.9 2.2 %copy-start.5 = (f32[768]{0:T(1024)S(1)}, f32[768]{0:T(1024)}, u32[]{:S(2)}) copy-start(f32[768]{0:T(1024)} %gain.3) | copy-start | bytes 9220
  32.6 2.8 %copy-start = (bf16[768,768]{1,0:T(8,128)(2,1)S(1)}, bf16[768,768]{1,0:T(8,128)(2,1)}, u32[]{:S(2)}) copy-start(bf16[768,768]{1,0:T(8,128)(2,1)} %ow.3) | copy-start | bytes 3538948
  37.7 1.8 %collective-permute-start.9 = (bf16[192,768]{1,0:T(8,128)(2,1)S(1)}, bf16[192,768]{1,0:T(8,128)(2,1)S(1)}, u32[]{:S(2)}, u32[]{:S(2)}) collective-permute-start(bf16[192,768]{1,0:T(8,128)(2,1)S(1)} %get-tuple-element.56), channel_id=1, source_target_pairs={{0,1},{1,0},{2,3},{3,2},{4,5},{5,4},{6,7},{7,6},{8,9},{9,8},{10,11... | collective-permute-start | bytes 884744 | tf_op jit(solution)/shard_map/ppermute | solution.py:195
  41.4 1.4 %collective-permute-start.11 = (bf16[208,256]{1,0:T(8,128)(2,1)S(1)}, bf16[208,256]{1,0:T(8,128)(2,1)S(1)}, u32[]{:S(2)}, u32[]{:S(2)}) collective-permute-start(bf16[208,256]{1,0:T(8,128)(2,1)S(1)} %get-tuple-element.64), channel_id=1, source_target_pairs={{0,1},{1,0},{2,3},{3,2},{4,5},{5,4},{6,7},{7,6},{8,9},{9,8},{10,11... | collective-permute-start | bytes 319496 | tf_op jit(solution)/shard_map/ppermute | solution.py:195
  41.9 9.9 %collective-permute-start.10 = (bf16[192,768]{1,0:T(8,128)(2,1)S(1)}, bf16[192,768]{1,0:T(8,128)(2,1)S(1)}, u32[]{:S(2)}, u32[]{:S(2)}) collective-permute-start(bf16[192,768]{1,0:T(8,128)(2,1)S(1)} %add_convert_fusion.1), channel_id=1, source_target_pairs={{0,2},{1,3},{2,0},{3,1},{4,6},{5,7},{6,4},{7,5},{8,10},{9,11},{10,... | collective-permute-start | bytes 884744 | tf_op jit(solution)/shard_map/ppermute | solution.py:195
  42.9 10.3 %collective-permute-start.12 = (bf16[208,256]{1,0:T(8,128)(2,1)S(1)}, bf16[208,256]{1,0:T(8,128)(2,1)S(1)}, u32[]{:S(2)}, u32[]{:S(2)}) collective-permute-start(bf16[208,256]{1,0:T(8,128)(2,1)S(1)} %add_convert_fusion.3), channel_id=1, source_target_pairs={{0,2},{1,3},{2,0},{3,1},{4,6},{5,7},{6,4},{7,5},{8,10},{9,11},{10,... | collective-permute-start | bytes 319496 | tf_op jit(solution)/shard_map/ppermute | solution.py:195
  51.8 2.7 %collective-permute-start.13 = (bf16[192,768]{1,0:T(8,128)(2,1)S(1)}, bf16[192,768]{1,0:T(8,128)(2,1)S(1)}, u32[]{:S(2)}, u32[]{:S(2)}) collective-permute-start(bf16[192,768]{1,0:T(8,128)(2,1)S(1)} %add_convert_fusion.whole_v), channel_id=1, source_target_pairs={{0,1},{1,0},{2,3},{3,2},{4,5},{5,4},{6,7},{7,6},{8,9},{9,8},{10,11... | collective-permute-start | bytes 884744 | tf_op jit(solution)/shard_map/ppermute | solution.py:195
  53.2 1.4 %collective-permute-start.14 = (bf16[208,256]{1,0:T(8,128)(2,1)S(1)}, bf16[208,256]{1,0:T(8,128)(2,1)S(1)}, u32[]{:S(2)}, u32[]{:S(2)}) collective-permute-start(bf16[208,256]{1,0:T(8,128)(2,1)S(1)} %add_convert_fusion.2.whole_k), channel_id=1, source_target_pairs={{0,1},{1,0},{2,3},{3,2},{4,5},{5,4},{6,7},{7,6},{8,9},{9,8},{10,11... | collective-permute-start | bytes 319496 | tf_op jit(solution)/shard_map/ppermute | solution.py:195

commit v4 on v3

--- a/solution.py
+++ b/solution.py
@@ -365,7 +365,7 @@
 
 
 def late_key_kernel(
-    grad, proj, probs_t, query_early, key_early, normed_t, mixed, gain, aw, keep, send, d_query, d_key
+    grad, proj, probs_t, query_early, key_early, normed_t, mixed, gain, aw, keep, top, rest, d_query, d_key
 ):
     z, d = lax.axis_index("seq"), lax.axis_index("dp")
     score_grads(grad, proj, probs_t, d_query, d_key, HEADS // 2)
@@ -382,12 +382,23 @@
         mine = jnp.where(z == at, scales[:, at * ROWS : (at + 1) * ROWS], mine)
     gain_part = total.T[0:1, :] / mine
 
-    def write(ref, side):
-        ref[:ROWS, :] = (key_part if side else query_part).astype(ref.dtype)
-        ref[ROWS:, :] = jnp.zeros((16, QW), ref.dtype)
-        ref[ROWS : ROWS + 1, :ROWS] = gain_part.astype(ref.dtype)
-
-    both_ways(write, keep, send, lax.rem(d, 2))
+    gain_rows = jnp.concatenate([gain_part, jnp.zeros((15, ROWS), F32)], axis=0)
+    cut = ROWS // 2
+
+    def part(side, rows):
+        return (key_part if side else query_part)[rows, :]
+
+    for at in range(2):
+
+        @pl.when(lax.rem(d, 2) == at)
+        def _():
+            keep[:ROWS, :] = part(at, slice(0, ROWS))
+            keep[ROWS:, :] = jnp.zeros((16, QW), F32)
+            keep[ROWS:, :ROWS] = gain_rows
+            top[...] = part(1 - at, slice(0, cut)).astype(BF16)
+            rest[:cut, :] = part(1 - at, slice(cut, ROWS)).astype(BF16)
+            rest[cut:, :] = jnp.zeros((16, QW), BF16)
+            rest[cut:, :ROWS] = gain_rows.astype(BF16)
 
 
 def finish_kernel(whole_v, whole_k, other_v, other_k, grad_attend, grad_output, grad_gain):
@@ -500,15 +511,16 @@
     )
     part_v = combined(keep_v, swap(send_v, 1))
     part_v, query_early = lax.optimization_barrier((part_v, query_early))
-    keep_k, send_k = kernel_call(
+    keep_k, top_k, rest_k = kernel_call(
         late_key_kernel,
-        [((ROWS + 16, QW), F32), ((ROWS + 16, QW), BF16)],
+        [((ROWS + 16, QW), F32), ((ROWS // 2, QW), BF16), ((ROWS // 2 + 16, QW), BF16)],
         [((QW // 2, LEN), BF16), ((LEN, QW // 2), BF16)],
         1 << 33,
         grad, proj, probs_t, query_early, key_early, normed_t, mixed, norm_gain, attend_weight,
     )
     arrived_v = swap(part_v, 2)
-    part_k = combined(keep_k, swap(send_k, 1))
+    arrived_v, outputs = lax.optimization_barrier((arrived_v, outputs))
+    part_k = combined(keep_k, jnp.concatenate([swap(top_k, 1), swap(rest_k, 1)]))
     arrived_k = swap(part_k, 2)
     whole_v, whole_k = combined(part_v, arrived_v), combined(part_k, arrived_k)
     other_v, other_k = swap(whole_v, 1), swap(whole_k, 1)

time: 56 us -> 54 us (0.964)
  waiting for transfers between devices: 19.3 us -> 16.6 us
  starting transfers between devices: 14.7 us -> 15.5 us
    ppermute x9 -> x10, waiting for transfers between devices: 10.5 us -> 7.71 us  [swap(): return lax.ppermute(value, 'dp', [(i, i ^ bit) for i in range(DP)])]
    ppermute x9 -> x10, starting transfers between devices: 5.32 us -> 6.14 us  [swap(): return lax.ppermute(value, 'dp', [(i, i ^ bit) for i in range(DP)])]
  transfers between devices with their start and end apart: 15 -> 16, of which waited for: 8 -> 8; matrix products, arithmetic and copies ran while one was open for 0% -> 0% of each run, Pallas kernels for 28% -> 32%
where the time goes in v4:
time: 54 us; the launch traced here: 53.9 us
  Pallas kernels  20.8 us (39%)
  waiting for transfers between devices  16.6 us (31%)
  starting transfers between devices  15.5 us (29%)
  between operations  0.76 us (1%)
    pallas_call x10, Pallas kernels, kernel_call(): pl.pallas_call(body, in_specs=[away if i in far else whole for i in range...  20.8 us
    ppermute x6, starting transfers between devices, ring(): lax.ppermute(value, 'seq', [(i, (i + step) % SEQ) for i in range(SEQ)])  9.34 us
    ppermute x6, waiting for transfers between devices, ring(): lax.ppermute(value, 'seq', [(i, (i + step) % SEQ) for i in range(SEQ)])  8.89 us
    ppermute x10, waiting for transfers between devices, swap(): return lax.ppermute(value, 'dp', [(i, i ^ bit) for i in range(DP)])  7.71 us
    ppermute x10, starting transfers between devices, swap(): return lax.ppermute(value, 'dp', [(i, i ^ bit) for i in range(DP)])  6.14 us
  transfers between devices with their start and end apart: 16, of which 8 were waited for; matrix products, arithmetic and copies ran while one was open for 0% of the time, Pallas kernels for 32%

profile of v4, /device:TPU:0, one launch (start us, length us, event | category | flops | bytes accessed | tf_op | source)
XLA Modules:
  0.0 53.9 jit_solution(15311965703981231605)
XLA Ops:
  0.6 0.5 collective-permute-start.2
  1.1 2.6 %collective-permute-start.6 = (bf16[960,384]{1,0:T(8,128)(2,1)}, bf16[960,384]{1,0:T(8,128)(2,1)S(1)}, u32[]{:S(2)}, u32[]{:S(2)}) collective-permute-start(bf16[960,384]{1,0:T(8,128)(2,1)} %bitcast.14), channel_id=1, source_target_pairs={{0,2},{1,3},{2,0},{3,1},{4,6},{5,7},{6,4},{7,5},{8,10},{9,11},{10,... | collective-permute-start | bytes 2211848 | tf_op jit(solution)/shard_map/ppermute | solution.py:195
  3.7 1.6 %collective-permute-start.1 = (bf16[256,384]{1,0:T(8,128)(2,1)}, bf16[256,384]{1,0:T(8,128)(2,1)S(1)}, u32[]{:S(2)}, u32[]{:S(2)}) collective-permute-start(bf16[256,384]{1,0:T(8,128)(2,1)} %bitcast.9), channel_id=1, source_target_pairs={{0,4},{4,8},{8,12},{12,0},{1,5},{5,9},{9,13},{13,1},{2,6},{6,10},{... | collective-permute-start | bytes 589832 | tf_op jit(solution)/shard_map/ppermute | solution.py:191
  5.3 2.2 %collective-permute-start.3 = (bf16[256,384]{1,0:T(8,128)(2,1)}, bf16[256,384]{1,0:T(8,128)(2,1)S(1)}, u32[]{:S(2)}, u32[]{:S(2)}) collective-permute-start(bf16[256,384]{1,0:T(8,128)(2,1)} %bitcast.10), channel_id=1, source_target_pairs={{0,12},{4,0},{8,4},{12,8},{1,13},{5,1},{9,5},{13,9},{2,14},{6,2},{... | collective-permute-start | bytes 589832 | tf_op jit(solution)/shard_map/ppermute | solution.py:191
  7.6 1.3 %shard_map.102.taps = bf16[384,1920]{1,0:T(8,128)(2,1)S(1)} custom-call(bf16[960,384]{1,0:T(8,128)(2,1)} %bitcast.15, bf16[960,384]{1,0:T(8,128)(2,1)S(1)} %collective-permute-done.2.w1), custom_call_target="tpu_custom_call" | custom-call | flops 2147483648 | bytes 65536 | tf_op jit(solution)/shard_map/pallas_call | solution.py:428
  8.9 4.6 %collective-permute-done.1.fa = bf16[256,384]{1,0:T(8,128)(2,1)S(1)} collective-permute-done((bf16[256,384]{1,0:T(8,128)(2,1)}, bf16[256,384]{1,0:T(8,128)(2,1)S(1)}, u32[]{:S(2)}, u32[]{:S(2)}) %collective-permute-start.1) | collective-permute-done | bytes 196640 | tf_op jit(solution)/shard_map/ppermute | solution.py:191
  13.5 3.0 %collective-permute-done.3.fb = bf16[256,384]{1,0:T(8,128)(2,1)S(1)} collective-permute-done((bf16[256,384]{1,0:T(8,128)(2,1)}, bf16[256,384]{1,0:T(8,128)(2,1)S(1)}, u32[]{:S(2)}, u32[]{:S(2)}) %collective-permute-start.3) | collective-permute-done | bytes 196640 | tf_op jit(solution)/shard_map/ppermute | solution.py:191
  16.5 1.7 %collective-permute-start.7 = (bf16[256,384]{1,0:T(8,128)(2,1)S(1)}, bf16[256,384]{1,0:T(8,128)(2,1)S(1)}, u32[]{:S(2)}, u32[]{:S(2)}) collective-permute-start(bf16[256,384]{1,0:T(8,128)(2,1)S(1)} %collective-permute-done.1.fa), channel_id=1, source_target_pairs={{0,4},{4,8},{8,12},{12,0},{1,5},{5,9},{9,13},{13,1},{2,6},{6,10},{... | collective-permute-start | bytes 589832 | tf_op jit(solution)/shard_map/ppermute | solution.py:191
  18.2 2.6 %shard_map.103 = (bf16[512,2304]{1,0:T(8,128)(2,1)S(1)}, bf16[512,384]{1,0:T(8,128)(2,1)S(1)}) custom-call(bf16[256,384]{1,0:T(8,128)(2,1)S(1)} %bitcast.11, bf16[256,384]{1,0:T(8,128)(2,1)S(1)} %collective-permute-done.1.fa, bf16[256,384]{1,0:T(8,128)(2,1)S(1)} %collective-permute-done.3.fb, bf16[384,1920]{1,0:T(8,128)(2,1)S(1)} %shard_map.102.taps, ...), custom_call_target="tpu_custom_call" | custom-call | flops 16777216 | bytes 65536 | tf_op jit(solution)/shard_map/pallas_call | solution.py:428
  20.8 1.1 %collective-permute-done.ca = bf16[128,768]{1,0:T(8,128)(2,1)S(1)} collective-permute-done((bf16[128,768]{1,0:T(8,128)(2,1)}, bf16[128,768]{1,0:T(8,128)(2,1)S(1)}, u32[]{:S(2)}, u32[]{:S(2)}) %collective-permute-start) | collective-permute-done | bytes 196640 | tf_op jit(solution)/shard_map/ppermute | solution.py:191
  21.9 3.8 %collective-permute-start.4 = (bf16[128,768]{1,0:T(8,128)(2,1)S(1)}, bf16[128,768]{1,0:T(8,128)(2,1)S(1)}, u32[]{:S(2)}, u32[]{:S(2)}) collective-permute-start(bf16[128,768]{1,0:T(8,128)(2,1)S(1)} %bitcast.7), channel_id=1, source_target_pairs={{0,12},{4,0},{8,4},{12,8},{1,13},{5,1},{9,5},{13,9},{2,14},{6,2},{... | collective-permute-start | bytes 589832 | tf_op jit(solution)/shard_map/ppermute | solution.py:191
  25.9 1.4 %shard_map.104 = (bf16[512,2304]{1,0:T(8,128)(2,1)S(1)}, bf16[512,384]{1,0:T(8,128)(2,1)S(1)}) custom-call(bf16[256,384]{1,0:T(8,128)(2,1)S(1)} %collective-permute-done.1.fa, bf16[256,384]{1,0:T(8,128)(2,1)S(1)} %collective-permute-done.3.fb, bf16[256,384]{1,0:T(8,128)(2,1)S(1)} %collective-permute-done.7.fc, ...), custom_call_target="tpu_custom_call" | custom-call | flops 8589934592 | bytes 65536 | tf_op jit(solution)/shard_map/pallas_call | solution.py:428
  27.4 0.8 %collective-permute-done.8.w3 = bf16[960,384]{1,0:T(8,128)(2,1)S(1)} collective-permute-done((bf16[960,384]{1,0:T(8,128)(2,1)S(1)}, bf16[960,384]{1,0:T(8,128)(2,1)S(1)}, u32[]{:S(2)}, u32[]{:S(2)}) %collective-permute-start.8) | collective-permute-done | bytes 737312 | tf_op jit(solution)/shard_map/ppermute | solution.py:195
  28.2 4.4 %shard_map.105 = (bf16[2,512,384]{2,1,0:T(8,128)(2,1)S(1)}, bf16[512,768]{1,0:T(8,128)(2,1)}, bf16[512,1280]{1,0:T(8,128)(2,1)S(1)}, bf16[192,512]{1,0:T(8,128)(2,1)S(1)}) custom-call(bf16[512,2304]{1,0:T(8,128)(2,1)S(1)} %get-tuple-element.50.windows, bf16[512,384]{1,0:T(8,128)(2,1)S(1)} %get-tuple-element.51.hid_near, ...), custom_call_target="tpu_custom_call" | custom-call | flops 8589934592 | bytes 65536 | tf_op jit(solution)/shard_map/pallas_call | solution.py:428
  32.6 2.7 %shard_map.106 = (bf16[4,512,512]{2,1,0:T(8,128)(2,1)S(1)}, bf16[768,512]{1,0:T(8,128)(2,1)S(1)}) custom-call(bf16[512,1280]{1,0:T(8,128)(2,1)S(1)} %get-tuple-element.54.proj), custom_call_target="tpu_custom_call" | custom-call | flops 8589934592 | bytes 65536 | tf_op jit(solution)/shard_map/pallas_call | solution.py:428
  35.3 2.4 %shard_map.107 = (bf16[512,768]{1,0:T(8,128)(2,1)S(1)}, f32[192,768]{1,0:T(8,128)S(1)}, bf16[192,768]{1,0:T(8,128)(2,1)S(1)}, f32[192,128]{1,0:T(8,128)S(1)}) custom-call(bf16[128,768]{1,0:T(8,128)(2,1)S(1)} %bitcast.8, bf16[128,768]{1,0:T(8,128)(2,1)S(1)} %collective-permute-done.ca, bf16[128,768]{1,0:T(8,128)(2,1)S(1)} %collective-permute-done.4.cb, ...), custom_call_target="tpu_custom_call" | custom-call | flops 536870912 | bytes 65536 | tf_op jit(solution)/shard_map/pallas_call | solution.py:428
  37.9 1.6 %shard_map.108 = (bf16[128,512]{1,0:T(8,128)(2,1)S(1)}, bf16[512,128]{1,0:T(8,128)(2,1)S(1)}) custom-call(bf16[512,768]{1,0:T(8,128)(2,1)S(1)} %get-tuple-element.59.grad, bf16[512,1280]{1,0:T(8,128)(2,1)S(1)} %get-tuple-element.54.proj, bf16[4,512,512]{2,1,0:T(8,128)(2,1)S(1)} %get-tuple-element.55.probs_t), custom_call_target="tpu_custom_call" | custom-call | flops 16777216 | bytes 65536 | tf_op jit(solution)/shard_map/pallas_call | solution.py:428
  40.0 1.8 %shard_map.110 = (f32[208,256]{1,0:T(8,128)S(1)}, bf16[96,256]{1,0:T(8,128)(2,1)S(1)}, bf16[112,256]{1,0:T(8,128)(2,1)S(1)}) custom-call(bf16[512,768]{1,0:T(8,128)(2,1)S(1)} %get-tuple-element.59.grad, bf16[512,1280]{1,0:T(8,128)(2,1)S(1)} %get-tuple-element.54.proj, bf16[4,512,512]{2,1,0:T(8,128)(2,1)S(1)} %get-tuple-element.55.probs_t, ...), custom_call_target="tpu_custom_call" | custom-call | flops 8589934592 | bytes 65536 | tf_op jit(solution)/shard_map/pallas_call | solution.py:428
  42.4 1.3 %shard_map.109 = f32[128,768]{1,0:T(8,128)} custom-call(bf16[2,512,384]{2,1,0:T(8,128)(2,1)S(1)} %get-tuple-element.62.hid, bf16[768,512]{1,0:T(8,128)(2,1)S(1)} %get-tuple-element.56.att_t, bf16[768,768]{1,0:T(8,128)(2,1)S(1)} %copy-done), custom_call_target="tpu_custom_call" | custom-call | flops 65536 | bytes 65536 | tf_op jit(solution)/shard_map/pallas_call | solution.py:428
  43.7 1.8 %collective-permute-start.13 = (bf16[208,256]{1,0:T(8,128)(2,1)S(1)}, bf16[208,256]{1,0:T(8,128)(2,1)S(1)}, u32[]{:S(2)}, u32[]{:S(2)}) collective-permute-start(bf16[208,256]{1,0:T(8,128)(2,1)S(1)} %add_convert_fusion.3), channel_id=1, source_target_pairs={{0,2},{1,3},{2,0},{3,1},{4,6},{5,7},{6,4},{7,5},{8,10},{9,11},{10,... | collective-permute-start | bytes 319496 | tf_op jit(solution)/shard_map/ppermute | solution.py:195
  45.5 4.0 %collective-permute-done.10 = bf16[192,768]{1,0:T(8,128)(2,1)S(1)} collective-permute-done((bf16[192,768]{1,0:T(8,128)(2,1)S(1)}, bf16[192,768]{1,0:T(8,128)(2,1)S(1)}, u32[]{:S(2)}, u32[]{:S(2)}) %collective-permute-start.10) | collective-permute-done | bytes 294944 | tf_op jit(solution)/shard_map/ppermute | solution.py:195
  49.7 1.6 %collective-permute-done.13 = bf16[208,256]{1,0:T(8,128)(2,1)S(1)} collective-permute-done((bf16[208,256]{1,0:T(8,128)(2,1)S(1)}, bf16[208,256]{1,0:T(8,128)(2,1)S(1)}, u32[]{:S(2)}, u32[]{:S(2)}) %collective-permute-start.13) | collective-permute-done | bytes 106528 | tf_op jit(solution)/shard_map/ppermute | solution.py:195
  51.4 1.3 %collective-permute-done.15.other_k = bf16[208,256]{1,0:T(8,128)(2,1)S(1)} collective-permute-done((bf16[208,256]{1,0:T(8,128)(2,1)S(1)}, bf16[208,256]{1,0:T(8,128)(2,1)S(1)}, u32[]{:S(2)}, u32[]{:S(2)}) %collective-permute-start.15) | collective-permute-done | bytes 106528 | tf_op jit(solution)/shard_map/ppermute | solution.py:195
  52.7 1.2 %shard_map.111 = (f32[192,1280]{1,0:T(8,128)}, f32[192,768]{1,0:T(8,128)}, f32[192]{0:T(256)}) custom-call(bf16[192,768]{1,0:T(8,128)(2,1)S(1)} %add_convert_fusion.whole_v, bf16[208,256]{1,0:T(8,128)(2,1)S(1)} %add_convert_fusion.2.whole_k, bf16[192,768]{1,0:T(8,128)(2,1)S(1)} %collective-permute-done.14.other_v, ...), custom_call_target="tpu_custom_call" | custom-call | flops 2147483648 | bytes 65536 | tf_op jit(solution)/shard_map/pallas_call | solution.py:428
  (34 shorter events, 1.7 us)
Async XLA Ops:
  0.6 6.9 %collective-permute-start.2 = (bf16[960,384]{1,0:T(8,128)(2,1)}, bf16[960,384]{1,0:T(8,128)(2,1)S(1)}, u32[]{:S(2)}, u32[]{:S(2)}) collective-permute-start(bf16[960,384]{1,0:T(8,128)(2,1)} %bitcast.13), channel_id=1, source_target_pairs={{0,1},{1,0},{2,3},{3,2},{4,5},{5,4},{6,7},{7,6},{8,9},{9,8},{10,11... | collective-permute-start | bytes 2211848 | tf_op jit(solution)/shard_map/ppermute | solution.py:195
  1.1 24.6 %collective-permute-start.6 = (bf16[960,384]{1,0:T(8,128)(2,1)}, bf16[960,384]{1,0:T(8,128)(2,1)S(1)}, u32[]{:S(2)}, u32[]{:S(2)}) collective-permute-start(bf16[960,384]{1,0:T(8,128)(2,1)} %bitcast.14), channel_id=1, source_target_pairs={{0,2},{1,3},{2,0},{3,1},{4,6},{5,7},{6,4},{7,5},{8,10},{9,11},{10,... | collective-permute-start | bytes 2211848 | tf_op jit(solution)/shard_map/ppermute | solution.py:195
  3.7 9.8 %collective-permute-start.1 = (bf16[256,384]{1,0:T(8,128)(2,1)}, bf16[256,384]{1,0:T(8,128)(2,1)S(1)}, u32[]{:S(2)}, u32[]{:S(2)}) collective-permute-start(bf16[256,384]{1,0:T(8,128)(2,1)} %bitcast.9), channel_id=1, source_target_pairs={{0,4},{4,8},{8,12},{12,0},{1,5},{5,9},{9,13},{13,1},{2,6},{6,10},{... | collective-permute-start | bytes 589832 | tf_op jit(solution)/shard_map/ppermute | solution.py:191
  5.3 11.2 %collective-permute-start.3 = (bf16[256,384]{1,0:T(8,128)(2,1)}, bf16[256,384]{1,0:T(8,128)(2,1)S(1)}, u32[]{:S(2)}, u32[]{:S(2)}) collective-permute-start(bf16[256,384]{1,0:T(8,128)(2,1)} %bitcast.10), channel_id=1, source_target_pairs={{0,12},{4,0},{8,4},{12,8},{1,13},{5,1},{9,5},{13,9},{2,14},{6,2},{... | collective-permute-start | bytes 589832 | tf_op jit(solution)/shard_map/ppermute | solution.py:191
  7.5 10.7 %copy-start.3 = (bf16[1,256,384]{2,1,0:T(8,128)(2,1)S(1)}, bf16[1,256,384]{2,1,0:T(8,128)(2,1)}, u32[]{:S(2)}) copy-start(bf16[1,256,384]{2,1,0:T(8,128)(2,1)} %param.7) | copy-start | bytes 589828
  7.5 10.7 %copy-start.4 = (f32[768]{0:T(1024)S(1)}, f32[768]{0:T(1024)}, u32[]{:S(2)}) copy-start(f32[768]{0:T(1024)} %bias.5) | copy-start | bytes 9220
  7.5 14.4 %collective-permute-start = (bf16[128,768]{1,0:T(8,128)(2,1)}, bf16[128,768]{1,0:T(8,128)(2,1)S(1)}, u32[]{:S(2)}, u32[]{:S(2)}) collective-permute-start(bf16[128,768]{1,0:T(8,128)(2,1)} %bitcast.6), channel_id=1, source_target_pairs={{0,4},{4,8},{8,12},{12,0},{1,5},{5,9},{9,13},{13,1},{2,6},{6,10},{... | collective-permute-start | bytes 589832 | tf_op jit(solution)/shard_map/ppermute | solution.py:191
  8.9 13.1 %copy-start.2 = (bf16[1,128,768]{2,1,0:T(8,128)(2,1)S(1)}, bf16[1,128,768]{2,1,0:T(8,128)(2,1)}, u32[]{:S(2)}) copy-start(bf16[1,128,768]{2,1,0:T(8,128)(2,1)} %param.13) | copy-start | bytes 589828
  16.5 9.4 %collective-permute-start.7 = (bf16[256,384]{1,0:T(8,128)(2,1)S(1)}, bf16[256,384]{1,0:T(8,128)(2,1)S(1)}, u32[]{:S(2)}, u32[]{:S(2)}) collective-permute-start(bf16[256,384]{1,0:T(8,128)(2,1)S(1)} %collective-permute-done.1.fa), channel_id=1, source_target_pairs={{0,4},{4,8},{8,12},{12,0},{1,5},{5,9},{9,13},{13,1},{2,6},{6,10},{... | collective-permute-start | bytes 589832 | tf_op jit(solution)/shard_map/ppermute | solution.py:191
  21.9 13.4 %collective-permute-start.5 = (bf16[128,768]{1,0:T(8,128)(2,1)S(1)}, bf16[128,768]{1,0:T(8,128)(2,1)S(1)}, u32[]{:S(2)}, u32[]{:S(2)}) collective-permute-start(bf16[128,768]{1,0:T(8,128)(2,1)S(1)} %collective-permute-done.ca), channel_id=1, source_target_pairs={{0,4},{4,8},{8,12},{12,0},{1,5},{5,9},{9,13},{13,1},{2,6},{6,10},{... | collective-permute-start | bytes 589832 | tf_op jit(solution)/shard_map/ppermute | solution.py:191
  21.9 13.4 %collective-permute-start.4 = (bf16[128,768]{1,0:T(8,128)(2,1)S(1)}, bf16[128,768]{1,0:T(8,128)(2,1)S(1)}, u32[]{:S(2)}, u32[]{:S(2)}) collective-permute-start(bf16[128,768]{1,0:T(8,128)(2,1)S(1)} %bitcast.7), channel_id=1, source_target_pairs={{0,12},{4,0},{8,4},{12,8},{1,13},{5,1},{9,5},{13,9},{2,14},{6,2},{... | collective-permute-start | bytes 589832 | tf_op jit(solution)/shard_map/ppermute | solution.py:191
  25.9 2.2 %collective-permute-start.8 = (bf16[960,384]{1,0:T(8,128)(2,1)S(1)}, bf16[960,384]{1,0:T(8,128)(2,1)S(1)}, u32[]{:S(2)}, u32[]{:S(2)}) collective-permute-start(bf16[960,384]{1,0:T(8,128)(2,1)S(1)} %collective-permute-done.6.w2), channel_id=1, source_target_pairs={{0,1},{1,0},{2,3},{3,2},{4,5},{5,4},{6,7},{7,6},{8,9},{9,8},{10,11... | collective-permute-start | bytes 2211848 | tf_op jit(solution)/shard_map/ppermute | solution.py:195
  25.9 2.2 %copy-start.1 = (bf16[768,1280]{1,0:T(8,128)(2,1)S(1)}, bf16[768,1280]{1,0:T(8,128)(2,1)}, u32[]{:S(2)}) copy-start(bf16[768,1280]{1,0:T(8,128)(2,1)} %aw.5) | copy-start | bytes 5898244
  25.9 2.2 %copy-start.5 = (f32[768]{0:T(1024)S(1)}, f32[768]{0:T(1024)}, u32[]{:S(2)}) copy-start(f32[768]{0:T(1024)} %gain.3) | copy-start | bytes 9220
  32.6 2.8 %copy-start = (bf16[768,768]{1,0:T(8,128)(2,1)S(1)}, bf16[768,768]{1,0:T(8,128)(2,1)}, u32[]{:S(2)}) copy-start(bf16[768,768]{1,0:T(8,128)(2,1)} %ow.3) | copy-start | bytes 3538948
  37.7 1.8 %collective-permute-start.9 = (bf16[192,768]{1,0:T(8,128)(2,1)S(1)}, bf16[192,768]{1,0:T(8,128)(2,1)S(1)}, u32[]{:S(2)}, u32[]{:S(2)}) collective-permute-start(bf16[192,768]{1,0:T(8,128)(2,1)S(1)} %get-tuple-element.58), channel_id=1, source_target_pairs={{0,1},{1,0},{2,3},{3,2},{4,5},{5,4},{6,7},{7,6},{8,9},{9,8},{10,11... | collective-permute-start | bytes 884744 | tf_op jit(solution)/shard_map/ppermute | solution.py:195
  39.6 9.9 %collective-permute-start.10 = (bf16[192,768]{1,0:T(8,128)(2,1)S(1)}, bf16[192,768]{1,0:T(8,128)(2,1)S(1)}, u32[]{:S(2)}, u32[]{:S(2)}) collective-permute-start(bf16[192,768]{1,0:T(8,128)(2,1)S(1)} %add_convert_fusion.1), channel_id=1, source_target_pairs={{0,2},{1,3},{2,0},{3,1},{4,6},{5,7},{6,4},{7,5},{8,10},{9,11},{10,... | collective-permute-start | bytes 884744 | tf_op jit(solution)/shard_map/ppermute | solution.py:195
  41.8 1.8 %collective-permute-start.12 = (bf16[112,256]{1,0:T(8,128)(2,1)S(1)}, bf16[112,256]{1,0:T(8,128)(2,1)S(1)}, u32[]{:S(2)}, u32[]{:S(2)}) collective-permute-start(bf16[112,256]{1,0:T(8,128)(2,1)S(1)} %get-tuple-element.70), channel_id=1, source_target_pairs={{0,1},{1,0},{2,3},{3,2},{4,5},{5,4},{6,7},{7,6},{8,9},{9,8},{10,11... | collective-permute-start | bytes 172040 | tf_op jit(solution)/shard_map/ppermute | solution.py:195
  42.0 1.7 %collective-permute-start.11 = (bf16[96,256]{1,0:T(8,128)(2,1)S(1)}, bf16[96,256]{1,0:T(8,128)(2,1)S(1)}, u32[]{:S(2)}, u32[]{:S(2)}) collective-permute-start(bf16[96,256]{1,0:T(8,128)(2,1)S(1)} %get-tuple-element.69), channel_id=1, source_target_pairs={{0,1},{1,0},{2,3},{3,2},{4,5},{5,4},{6,7},{7,6},{8,9},{9,8},{10,11... | collective-permute-start | bytes 147464 | tf_op jit(solution)/shard_map/ppermute | solution.py:195
  43.7 7.6 %collective-permute-start.13 = (bf16[208,256]{1,0:T(8,128)(2,1)S(1)}, bf16[208,256]{1,0:T(8,128)(2,1)S(1)}, u32[]{:S(2)}, u32[]{:S(2)}) collective-permute-start(bf16[208,256]{1,0:T(8,128)(2,1)S(1)} %add_convert_fusion.3), channel_id=1, source_target_pairs={{0,2},{1,3},{2,0},{3,1},{4,6},{5,7},{6,4},{7,5},{8,10},{9,11},{10,... | collective-permute-start | bytes 319496 | tf_op jit(solution)/shard_map/ppermute | solution.py:195
  49.6 3.1 %collective-permute-start.14 = (bf16[192,768]{1,0:T(8,128)(2,1)S(1)}, bf16[192,768]{1,0:T(8,128)(2,1)S(1)}, u32[]{:S(2)}, u32[]{:S(2)}) collective-permute-start(bf16[192,768]{1,0:T(8,128)(2,1)S(1)} %add_convert_fusion.whole_v), channel_id=1, source_target_pairs={{0,1},{1,0},{2,3},{3,2},{4,5},{5,4},{6,7},{7,6},{8,9},{9,8},{10,11... | collective-permute-start | bytes 884744 | tf_op jit(solution)/shard_map/ppermute | solution.py:195
  51.3 1.4 %collective-permute-start.15 = (bf16[208,256]{1,0:T(8,128)(2,1)S(1)}, bf16[208,256]{1,0:T(8,128)(2,1)S(1)}, u32[]{:S(2)}, u32[]{:S(2)}) collective-permute-start(bf16[208,256]{1,0:T(8,128)(2,1)S(1)} %add_convert_fusion.2.whole_k), channel_id=1, source_target_pairs={{0,1},{1,0},{2,3},{3,2},{4,5},{5,4},{6,7},{7,6},{8,9},{9,8},{10,11... | collective-permute-start | bytes 319496 | tf_op jit(solution)/shard_map/ppermute | solution.py:195

commit v5 on v4

--- a/solution.py
+++ b/solution.py
@@ -173,6 +173,7 @@
 QW, VW = HEADS * KEY_DIM, HEADS * VAL_DIM
 PROJ = 2 * QW + VW
 SCALE = KEY_DIM**-0.5
+LOG2E = 1.4426950408889634
 NN = (((1,), (0,)), ((), ()))
 NT = (((1,), (1,)), ((), ()))
 TN = (((0,), (0,)), ((), ()))
@@ -201,6 +202,19 @@
         rows = slice(tap * SHARD, (tap + 1) * SHARD)
         taps[pl.ds(core * SHARD, SHARD), lanes] = mine[rows, :]
         taps[pl.ds((1 - core) * SHARD, SHARD), lanes] = other[rows, :]
+
+
+def put_shard(taps, shard):
+    for tap in range(5):
+        taps[:, tap * CIN : (tap + 1) * CIN] = shard[tap * SHARD : (tap + 1) * SHARD, :]
+
+
+def shard_of(bias, index):
+    every = bias[...].reshape(1, WIDTH)
+    mine = every[:, :SHARD]
+    for at in range(1, DP):
+        mine = jnp.where(index == at, every[:, at * SHARD : (at + 1) * SHARD], mine)
+    return mine
 
 
 def half_of(bias, side):
@@ -250,7 +264,9 @@
     return jnp.where(lane == row + z * ROWS, 1.0, 0.0).astype(BF16)
 
 
-def mend_kernel(fa, fb, fc, windows_in, hid_in, taps, bias, windows, hid, positions):
+def mend_kernel(
+    fa, fb, fc, windows_in, hid_in, taps, w2, bias, windows, hid, hid_two, positions, two
+):
     z, d = lax.axis_index("seq"), lax.axis_index("dp")
     fill_positions(positions, z, ((fa, 3), (fb, 1), (fc, 2)))
     windows[...] = windows_in[...]
@@ -264,14 +280,20 @@
             spots = pl.ds(2 * first + (6 + k), TOK + 2 * EDGE, stride=2)
             windows[fresh, at : at + 128] = positions[g, spots, :].astype(BF16)
     hid[fresh, :] = filtered_half(windows[fresh, :], taps, half_of(bias, d // 2))
-
-
-def project_kernel(windows, hid_near, w2, w3, bias, gain, aw, hid, normed, proj, normed_t, taps):
+    put_shard(two, w2)
+    hid_two[...] = filtered_half(windows, two, shard_of(bias, lax.rem(d + 2, DP)))
+
+
+def project_kernel(
+    windows, hid_near, hid_two, w3, bias, gain, aw, hid, normed, proj, normed_t, three, far
+):
     z, d = lax.axis_index("seq"), lax.axis_index("dp")
-    side, half = d // 2, WIDTH // 2
-    put_shards(taps, w2, w3, lax.rem(d, 2))
+    side, core, half = d // 2, lax.rem(d, 2), WIDTH // 2
+    put_shard(three, w3)
     hid[side] = hid_near[...]
-    hid[1 - side] = filtered_half(windows, taps, half_of(bias, 1 - side))
+    far[core] = hid_two[...]
+    far[1 - core] = filtered_half(windows, three, shard_of(bias, 2 * (1 - side) + 1 - core))
+    hid[1 - side] = jnp.concatenate([far[0], far[1]], axis=1)
     low, high = hid[0].astype(F32), hid[1].astype(F32)
     square = jnp.sum(low * low, axis=1, keepdims=True) + jnp.sum(high * high, axis=1, keepdims=True)
     inv = lax.rsqrt(square * (1.0 / WIDTH) + 1e-06)
@@ -292,9 +314,9 @@
 def attend_kernel(proj, probs_t, att_t):
     for h in range(HEADS):
         q, k, v = heads_of(proj, h)
-        scores = mm(k, q, NT) * SCALE
+        scores = mm(k, q, NT) * (SCALE * LOG2E)
         top = jnp.max(scores, axis=0, keepdims=True)
-        weight = jnp.exp(scores - top)
+        weight = jnp.exp2(scores - top)
         total = jnp.sum(weight, axis=0, keepdims=True)
         probs = (weight * (1.0 / total)).astype(BF16)
         probs_t[h] = probs
@@ -401,20 +423,24 @@
             rest[cut:, :ROWS] = gain_rows.astype(BF16)
 
 
-def finish_kernel(whole_v, whole_k, other_v, other_k, grad_attend, grad_output, grad_gain):
+def finish_output_kernel(whole_v, other_v, grad_output):
     half = VW // 2
-
-    def place(source, side):
-        lanes = slice(side * half, (side + 1) * half)
-        grad_attend[:, 2 * QW + side * half : 2 * QW + (side + 1) * half] = source[:, :half].astype(F32)
-        grad_output[:, lanes] = source[:, half:].astype(F32)
-
     for at in range(2):
 
         @pl.when(lax.rem(lax.axis_index("dp"), 2) == at)
         def _():
-            place(whole_v, at)
-            place(other_v, 1 - at)
+            grad_output[:, at * half : (at + 1) * half] = whole_v[:, half:].astype(F32)
+            grad_output[:, (1 - at) * half : (2 - at) * half] = other_v[:, half:].astype(F32)
+
+
+def finish_attend_kernel(whole_v, other_v, whole_k, other_k, grad_attend, grad_gain):
+    half, base = VW // 2, 2 * QW
+    for at in range(2):
+
+        @pl.when(lax.rem(lax.axis_index("dp"), 2) == at)
+        def _():
+            grad_attend[:, base + at * half : base + (at + 1) * half] = whole_v[:, :half].astype(F32)
+            grad_attend[:, base + (1 - at) * half : base + (2 - at) * half] = other_v[:, :half].astype(F32)
             low, high = (whole_k, other_k) if at == 0 else (other_k, whole_k)
             grad_attend[:, :QW] = low[:ROWS, :].astype(F32)
             grad_attend[:, QW : 2 * QW] = high[:ROWS, :].astype(F32)
@@ -452,7 +478,7 @@
         taps_kernel,
         [((2 * SHARD, 5 * CIN), BF16)],
         [((5 * SHARD, CIN), BF16)],
-        1 << 31,
+        1 << 24,
         pltpu.with_memory_space_constraint(w0, pltpu.HBM), w1,
         far=(0,),
     )
@@ -464,49 +490,49 @@
         near_kernel,
         [((LEN, 6 * CIN), BF16), ((LEN, half), BF16)],
         [((CIN // 128, 16 + 2 * LEN, 128), F32)],
-        1 << 24,
+        1 << 33,
         f0, fa, fb, taps, filter_bias,
     )
     ca, windows = lax.optimization_barrier((ca, windows))
     cb, cc = ring(to_left, SEQ - 1), ring(ca, 1)
     w2, fc, windows = lax.optimization_barrier((w2, fc, windows))
     w3 = swap(w2, 1)
-    windows, hid_near = kernel_call(
+    windows, hid_near, hid_two = kernel_call(
         mend_kernel,
-        [((LEN, 6 * CIN), BF16), ((LEN, half), BF16)],
-        [((CIN // 128, 16 + 2 * LEN, 128), F32)],
+        [((LEN, 6 * CIN), BF16), ((LEN, half), BF16), ((LEN, SHARD), BF16)],
+        [((CIN // 128, 16 + 2 * LEN, 128), F32), ((SHARD, 5 * CIN), BF16)],
         1 << 33,
-        fa, fb, fc, windows, hid_near, taps, filter_bias,
+        fa, fb, fc, windows, hid_near, taps, w2, filter_bias,
     )
     hid, normed, proj, normed_t = kernel_call(
         project_kernel,
         [((2, LEN, half), BF16), ((LEN, WIDTH), BF16), ((LEN, PROJ), BF16), ((ROWS, LEN), BF16)],
-        [((2 * SHARD, 5 * CIN), BF16)],
-        1 << 33,
-        windows, hid_near, w2, w3, filter_bias, norm_gain, attend_weight,
+        [((SHARD, 5 * CIN), BF16), ((2, LEN, SHARD), BF16)],
+        1 << 24,
+        windows, hid_near, hid_two, w3, filter_bias, norm_gain, attend_weight,
     )
     probs_t, att_t = kernel_call(
         attend_kernel,
         [((HEADS, LEN, LEN), BF16), ((VW, LEN), BF16)],
         [],
-        1 << 33,
+        1 << 29,
         proj,
     )
     (outputs,) = kernel_call(
-        outputs_kernel, [((TOK, WIDTH), F32)], [], 1 << 16, hid, att_t, output_weight
+        outputs_kernel, [((TOK, WIDTH), F32)], [], 1 << 33, hid, att_t, output_weight
     )
     grad, keep_v, send_v, mixed = kernel_call(
         value_kernel,
         [((LEN, VW), BF16), ((ROWS, VW), F32), ((ROWS, VW), BF16), ((ROWS, 128), F32)],
         [((LEN, WIDTH), BF16), ((ROWS, LEN), BF16), ((LEN, VW), BF16)],
-        1 << 29,
+        1 << 31,
         c0, ca, cb, cc, normed_t, probs_t, att_t, attend_weight, output_weight,
     )
     query_early, key_early = kernel_call(
         early_key_kernel,
         [((QW // 2, LEN), BF16), ((LEN, QW // 2), BF16)],
         [],
-        1 << 24,
+        1 << 33,
         grad, proj, probs_t,
     )
     part_v = combined(keep_v, swap(send_v, 1))
@@ -515,7 +541,7 @@
         late_key_kernel,
         [((ROWS + 16, QW), F32), ((ROWS // 2, QW), BF16), ((ROWS // 2 + 16, QW), BF16)],
         [((QW // 2, LEN), BF16), ((LEN, QW // 2), BF16)],
-        1 << 33,
+        1 << 16,
         grad, proj, probs_t, query_early, key_early, normed_t, mixed, norm_gain, attend_weight,
     )
     arrived_v = swap(part_v, 2)
@@ -524,12 +550,15 @@
     arrived_k = swap(part_k, 2)
     whole_v, whole_k = combined(part_v, arrived_v), combined(part_k, arrived_k)
     other_v, other_k = swap(whole_v, 1), swap(whole_k, 1)
-    grad_attend, grad_output, grad_gain = kernel_call(
-        finish_kernel,
-        [((ROWS, PROJ), F32), ((ROWS, WIDTH), F32), ((ROWS,), F32)],
+    (grad_output,) = kernel_call(
+        finish_output_kernel, [((ROWS, WIDTH), F32)], [], 1 << 33, whole_v, other_v
+    )
+    grad_attend, grad_gain = kernel_call(
+        finish_attend_kernel,
+        [((ROWS, PROJ), F32), ((ROWS,), F32)],
         [],
-        1 << 31,
-        whole_v, whole_k, other_v, other_k,
+        1 << 16,
+        whole_v, other_v, whole_k, other_k,
     )
     return outputs[None], grad_attend, grad_output, grad_gain
 

time: 54 us -> 52.5 us (0.972)
  waiting for transfers between devices: 16.6 us -> 13.7 us
  Pallas kernels: 20.8 us -> 22.2 us
    ppermute x6, waiting for transfers between devices: 8.89 us -> 7.43 us  [ring(): lax.ppermute(value, 'seq', [(i, (i + step) % SEQ) for i in range(SEQ)])]
    ppermute x10, waiting for transfers between devices: 7.71 us -> 6.26 us  [swap(): return lax.ppermute(value, 'dp', [(i, i ^ bit) for i in range(DP)])]
    pallas_call x10 -> x11, Pallas kernels: 20.8 us -> 22.2 us  [kernel_call(): pl.pallas_call(body, in_specs=[away if i in far else whole for i in range...]
    ppermute x10, starting transfers between devices: 6.14 us -> 5.51 us  [swap(): return lax.ppermute(value, 'dp', [(i, i ^ bit) for i in range(DP)])]
    ppermute x6, starting transfers between devices: 9.34 us -> 9.9 us  [ring(): lax.ppermute(value, 'seq', [(i, (i + step) % SEQ) for i in range(SEQ)])]
  transfers between devices with their start and end apart: 16 -> 16, of which waited for: 8 -> 8; matrix products, arithmetic and copies ran while one was open for 0% -> 0% of each run, Pallas kernels for 32% -> 36%
where the time goes in v5:
time: 52.5 us; the launch traced here: 52.4 us
  Pallas kernels  22.2 us (42%)
  starting transfers between devices  15.4 us (29%)
  waiting for transfers between devices  13.7 us (26%)
  between operations  0.82 us (2%)
    pallas_call x11, Pallas kernels, kernel_call(): pl.pallas_call(body, in_specs=[away if i in far else whole for i in range...  22.2 us
    ppermute x6, starting transfers between devices, ring(): lax.ppermute(value, 'seq', [(i, (i + step) % SEQ) for i in range(SEQ)])  9.9 us
    ppermute x6, waiting for transfers between devices, ring(): lax.ppermute(value, 'seq', [(i, (i + step) % SEQ) for i in range(SEQ)])  7.43 us
    ppermute x10, waiting for transfers between devices, swap(): return lax.ppermute(value, 'dp', [(i, i ^ bit) for i in range(DP)])  6.26 us
    ppermute x10, starting transfers between devices, swap(): return lax.ppermute(value, 'dp', [(i, i ^ bit) for i in range(DP)])  5.51 us
  transfers between devices with their start and end apart: 16, of which 8 were waited for; matrix products, arithmetic and copies ran while one was open for 0% of the time, Pallas kernels for 36%

profile of v5, /device:TPU:0, one launch (start us, length us, event | category | flops | bytes accessed | tf_op | source)
XLA Modules:
  0.0 52.4 jit_solution(1736768526190725286)
XLA Ops:
  1.2 2.6 %collective-permute-start.1 = (bf16[256,384]{1,0:T(8,128)(2,1)}, bf16[256,384]{1,0:T(8,128)(2,1)S(1)}, u32[]{:S(2)}, u32[]{:S(2)}) collective-permute-start(bf16[256,384]{1,0:T(8,128)(2,1)} %bitcast.6), channel_id=1, source_target_pairs={{0,4},{4,8},{8,12},{12,0},{1,5},{5,9},{9,13},{13,1},{2,6},{6,10},{... | collective-permute-start | bytes 589832 | tf_op jit(solution)/shard_map/ppermute | solution.py:192
  3.8 2.1 %collective-permute-start.3 = (bf16[256,384]{1,0:T(8,128)(2,1)}, bf16[256,384]{1,0:T(8,128)(2,1)S(1)}, u32[]{:S(2)}, u32[]{:S(2)}) collective-permute-start(bf16[256,384]{1,0:T(8,128)(2,1)} %bitcast.7), channel_id=1, source_target_pairs={{0,12},{4,0},{8,4},{12,8},{1,13},{5,1},{9,5},{13,9},{2,14},{6,2},{... | collective-permute-start | bytes 589832 | tf_op jit(solution)/shard_map/ppermute | solution.py:192
  5.9 1.6 %collective-permute-start.6 = (bf16[960,384]{1,0:T(8,128)(2,1)}, bf16[960,384]{1,0:T(8,128)(2,1)S(1)}, u32[]{:S(2)}, u32[]{:S(2)}) collective-permute-start(bf16[960,384]{1,0:T(8,128)(2,1)} %bitcast.13), channel_id=1, source_target_pairs={{0,2},{1,3},{2,0},{3,1},{4,6},{5,7},{6,4},{7,5},{8,10},{9,11},{10,... | collective-permute-start | bytes 2211848 | tf_op jit(solution)/shard_map/ppermute | solution.py:196
  7.6 1.3 %shard_map.102.taps = bf16[384,1920]{1,0:T(8,128)(2,1)S(1)} custom-call(bf16[960,384]{1,0:T(8,128)(2,1)} %bitcast.14, bf16[960,384]{1,0:T(8,128)(2,1)S(1)} %collective-permute-done.2.w1), custom_call_target="tpu_custom_call" | custom-call | flops 16777216 | bytes 65536 | tf_op jit(solution)/shard_map/pallas_call | solution.py:454
  8.9 3.0 %collective-permute-done.1.fa = bf16[256,384]{1,0:T(8,128)(2,1)S(1)} collective-permute-done((bf16[256,384]{1,0:T(8,128)(2,1)}, bf16[256,384]{1,0:T(8,128)(2,1)S(1)}, u32[]{:S(2)}, u32[]{:S(2)}) %collective-permute-start.1) | collective-permute-done | bytes 196640 | tf_op jit(solution)/shard_map/ppermute | solution.py:192
  11.8 3.4 %collective-permute-done.3.fb = bf16[256,384]{1,0:T(8,128)(2,1)S(1)} collective-permute-done((bf16[256,384]{1,0:T(8,128)(2,1)}, bf16[256,384]{1,0:T(8,128)(2,1)S(1)}, u32[]{:S(2)}, u32[]{:S(2)}) %collective-permute-start.3) | collective-permute-done | bytes 196640 | tf_op jit(solution)/shard_map/ppermute | solution.py:192
  15.2 1.3 %collective-permute-start.7 = (bf16[256,384]{1,0:T(8,128)(2,1)S(1)}, bf16[256,384]{1,0:T(8,128)(2,1)S(1)}, u32[]{:S(2)}, u32[]{:S(2)}) collective-permute-start(bf16[256,384]{1,0:T(8,128)(2,1)S(1)} %collective-permute-done.1.fa), channel_id=1, source_target_pairs={{0,4},{4,8},{8,12},{12,0},{1,5},{5,9},{9,13},{13,1},{2,6},{6,10},{... | collective-permute-start | bytes 589832 | tf_op jit(solution)/shard_map/ppermute | solution.py:192
  16.5 2.6 %shard_map.103 = (bf16[512,2304]{1,0:T(8,128)(2,1)S(1)}, bf16[512,384]{1,0:T(8,128)(2,1)S(1)}) custom-call(bf16[256,384]{1,0:T(8,128)(2,1)S(1)} %bitcast.8, bf16[256,384]{1,0:T(8,128)(2,1)S(1)} %collective-permute-done.1.fa, bf16[256,384]{1,0:T(8,128)(2,1)S(1)} %collective-permute-done.3.fb, bf16[384,1920]{1,0:T(8,128)(2,1)S(1)} %shard_map.102.taps, ...), custom_call_target="tpu_custom_call" | custom-call | flops 8589934592 | bytes 65536 | tf_op jit(solution)/shard_map/pallas_call | solution.py:454
  19.2 1.1 %collective-permute-done.ca = bf16[128,768]{1,0:T(8,128)(2,1)S(1)} collective-permute-done((bf16[128,768]{1,0:T(8,128)(2,1)}, bf16[128,768]{1,0:T(8,128)(2,1)S(1)}, u32[]{:S(2)}, u32[]{:S(2)}) %collective-permute-start) | collective-permute-done | bytes 196640 | tf_op jit(solution)/shard_map/ppermute | solution.py:192
  20.3 3.8 %collective-permute-start.4 = (bf16[128,768]{1,0:T(8,128)(2,1)S(1)}, bf16[128,768]{1,0:T(8,128)(2,1)S(1)}, u32[]{:S(2)}, u32[]{:S(2)}) collective-permute-start(bf16[128,768]{1,0:T(8,128)(2,1)S(1)} %bitcast.10), channel_id=1, source_target_pairs={{0,12},{4,0},{8,4},{12,8},{1,13},{5,1},{9,5},{13,9},{2,14},{6,2},{... | collective-permute-start | bytes 589832 | tf_op jit(solution)/shard_map/ppermute | solution.py:192
  24.6 2.8 %shard_map.104 = (bf16[512,2304]{1,0:T(8,128)(2,1)S(1)}, bf16[512,384]{1,0:T(8,128)(2,1)S(1)}, bf16[512,192]{1,0:T(8,128)(2,1)S(1)}) custom-call(bf16[256,384]{1,0:T(8,128)(2,1)S(1)} %collective-permute-done.1.fa, bf16[256,384]{1,0:T(8,128)(2,1)S(1)} %collective-permute-done.3.fb, bf16[256,384]{1,0:T(8,128)(2,1)S(1)} %collective-permute-done.7.fc, ...), custom_call_target="tpu_custom_call" | custom-call | flops 8589934592 | bytes 65536 | tf_op jit(solution)/shard_map/pallas_call | solution.py:454
  27.5 3.8 %shard_map.105 = (bf16[2,512,384]{2,1,0:T(8,128)(2,1)S(1)}, bf16[512,768]{1,0:T(8,128)(2,1)}, bf16[512,1280]{1,0:T(8,128)(2,1)S(1)}, bf16[192,512]{1,0:T(8,128)(2,1)S(1)}) custom-call(bf16[512,2304]{1,0:T(8,128)(2,1)S(1)} %get-tuple-element.51.windows, bf16[512,384]{1,0:T(8,128)(2,1)S(1)} %get-tuple-element.52.hid_near, ...), custom_call_target="tpu_custom_call" | custom-call | flops 16777216 | bytes 65536 | tf_op jit(solution)/shard_map/pallas_call | solution.py:454
  31.3 2.7 %shard_map.106 = (bf16[4,512,512]{2,1,0:T(8,128)(2,1)S(1)}, bf16[768,512]{1,0:T(8,128)(2,1)S(1)}) custom-call(bf16[512,1280]{1,0:T(8,128)(2,1)S(1)} %get-tuple-element.55.proj), custom_call_target="tpu_custom_call" | custom-call | flops 536870912 | bytes 65536 | tf_op jit(solution)/shard_map/pallas_call | solution.py:454
  34.0 2.4 %shard_map.107 = (bf16[512,768]{1,0:T(8,128)(2,1)S(1)}, f32[192,768]{1,0:T(8,128)S(1)}, bf16[192,768]{1,0:T(8,128)(2,1)S(1)}, f32[192,128]{1,0:T(8,128)S(1)}) custom-call(bf16[128,768]{1,0:T(8,128)(2,1)S(1)} %bitcast.11, bf16[128,768]{1,0:T(8,128)(2,1)S(1)} %collective-permute-done.ca, bf16[128,768]{1,0:T(8,128)(2,1)S(1)} %collective-permute-done.4.cb, ...), custom_call_target="tpu_custom_call" | custom-call | flops 2147483648 | bytes 65536 | tf_op jit(solution)/shard_map/pallas_call | solution.py:454
  36.4 0.5 %collective-permute-start.9 = (bf16[192,768]{1,0:T(8,128)(2,1)S(1)}, bf16[192,768]{1,0:T(8,128)(2,1)S(1)}, u32[]{:S(2)}, u32[]{:S(2)}) collective-permute-start(bf16[192,768]{1,0:T(8,128)(2,1)S(1)} %get-tuple-element.59), channel_id=1, source_target_pairs={{0,1},{1,0},{2,3},{3,2},{4,5},{5,4},{6,7},{7,6},{8,9},{9,8},{10,11... | collective-permute-start | bytes 884744 | tf_op jit(solution)/shard_map/ppermute | solution.py:196
  36.9 1.6 %shard_map.108 = (bf16[128,512]{1,0:T(8,128)(2,1)S(1)}, bf16[512,128]{1,0:T(8,128)(2,1)S(1)}) custom-call(bf16[512,768]{1,0:T(8,128)(2,1)S(1)} %get-tuple-element.60.grad, bf16[512,1280]{1,0:T(8,128)(2,1)S(1)} %get-tuple-element.55.proj, bf16[4,512,512]{2,1,0:T(8,128)(2,1)S(1)} %get-tuple-element.56.probs_t), custom_call_target="tpu_custom_call" | custom-call | flops 8589934592 | bytes 65536 | tf_op jit(solution)/shard_map/pallas_call | solution.py:454
  38.6 1.6 %collective-permute-start.10 = (bf16[192,768]{1,0:T(8,128)(2,1)S(1)}, bf16[192,768]{1,0:T(8,128)(2,1)S(1)}, u32[]{:S(2)}, u32[]{:S(2)}) collective-permute-start(bf16[192,768]{1,0:T(8,128)(2,1)S(1)} %add_convert_fusion.1), channel_id=1, source_target_pairs={{0,2},{1,3},{2,0},{3,1},{4,6},{5,7},{6,4},{7,5},{8,10},{9,11},{10,... | collective-permute-start | bytes 884744 | tf_op jit(solution)/shard_map/ppermute | solution.py:196
  40.2 1.8 %shard_map.110 = (f32[208,256]{1,0:T(8,128)S(1)}, bf16[96,256]{1,0:T(8,128)(2,1)S(1)}, bf16[112,256]{1,0:T(8,128)(2,1)S(1)}) custom-call(bf16[512,768]{1,0:T(8,128)(2,1)S(1)} %get-tuple-element.60.grad, bf16[512,1280]{1,0:T(8,128)(2,1)S(1)} %get-tuple-element.55.proj, bf16[4,512,512]{2,1,0:T(8,128)(2,1)S(1)} %get-tuple-element.56.probs_t, ...), custom_call_target="tpu_custom_call" | custom-call | flops 65536 | bytes 65536 | tf_op jit(solution)/shard_map/pallas_call | solution.py:454
  42.6 1.3 %shard_map.109 = f32[128,768]{1,0:T(8,128)} custom-call(bf16[2,512,384]{2,1,0:T(8,128)(2,1)S(1)} %get-tuple-element.63.hid, bf16[768,512]{1,0:T(8,128)(2,1)S(1)} %get-tuple-element.57.att_t, bf16[768,768]{1,0:T(8,128)(2,1)S(1)} %copy-done.3), custom_call_target="tpu_custom_call" | custom-call | flops 8589934592 | bytes 65536 | tf_op jit(solution)/shard_map/pallas_call | solution.py:454
  43.9 0.6 %collective-permute-start.14 = (bf16[208,256]{1,0:T(8,128)(2,1)S(1)}, bf16[208,256]{1,0:T(8,128)(2,1)S(1)}, u32[]{:S(2)}, u32[]{:S(2)}) collective-permute-start(bf16[208,256]{1,0:T(8,128)(2,1)S(1)} %add_convert_fusion.3), channel_id=1, source_target_pairs={{0,2},{1,3},{2,0},{3,1},{4,6},{5,7},{6,4},{7,5},{8,10},{9,11},{10,... | collective-permute-start | bytes 319496 | tf_op jit(solution)/shard_map/ppermute | solution.py:196
  44.5 4.1 %collective-permute-done.10 = bf16[192,768]{1,0:T(8,128)(2,1)S(1)} collective-permute-done((bf16[192,768]{1,0:T(8,128)(2,1)S(1)}, bf16[192,768]{1,0:T(8,128)(2,1)S(1)}, u32[]{:S(2)}, u32[]{:S(2)}) %collective-permute-start.10) | collective-permute-done | bytes 294944 | tf_op jit(solution)/shard_map/ppermute | solution.py:196
  48.7 1.2 %collective-permute-done.14 = bf16[208,256]{1,0:T(8,128)(2,1)S(1)} collective-permute-done((bf16[208,256]{1,0:T(8,128)(2,1)S(1)}, bf16[208,256]{1,0:T(8,128)(2,1)S(1)}, u32[]{:S(2)}, u32[]{:S(2)}) %collective-permute-start.14) | collective-permute-done | bytes 106528 | tf_op jit(solution)/shard_map/ppermute | solution.py:196
  50.3 0.9 %shard_map.112 = f32[192,768]{1,0:T(8,128)} custom-call(bf16[192,768]{1,0:T(8,128)(2,1)S(1)} %add_convert_fusion.whole_v, bf16[192,768]{1,0:T(8,128)(2,1)S(1)} %collective-permute-done.11.other_v), custom_call_target="tpu_custom_call" | custom-call | flops 8589934592 | bytes 65536 | tf_op jit(solution)/shard_map/pallas_call | solution.py:454
  51.3 1.0 %shard_map.111 = (f32[192,1280]{1,0:T(8,128)}, f32[192]{0:T(256)}) custom-call(bf16[192,768]{1,0:T(8,128)(2,1)S(1)} %add_convert_fusion.whole_v, bf16[192,768]{1,0:T(8,128)(2,1)S(1)} %collective-permute-done.11.other_v, bf16[208,256]{1,0:T(8,128)(2,1)S(1)} %add_convert_fusion.2.whole_k, bf16[208,256]{1,0:T(8,128)(2,1)S(1)} %collective-permute-done.15.other_k), custom_call_target="tpu_custom_call" | custom-call | flops 65536 | bytes 65536 | tf_op jit(solution)/shard_map/pallas_call | solution.py:454
  (35 shorter events, 2.4 us)
Async XLA Ops:
  0.6 15.9 %copy-start.4 = (bf16[1,256,384]{2,1,0:T(8,128)(2,1)S(1)}, bf16[1,256,384]{2,1,0:T(8,128)(2,1)}, u32[]{:S(2)}) copy-start(bf16[1,256,384]{2,1,0:T(8,128)(2,1)} %param.7) | copy-start | bytes 589828
  0.6 15.9 %copy-start.2 = (f32[768]{0:T(1024)S(1)}, f32[768]{0:T(1024)}, u32[]{:S(2)}) copy-start(f32[768]{0:T(1024)} %bias.5) | copy-start | bytes 9220
  0.7 6.9 %collective-permute-start.2 = (bf16[960,384]{1,0:T(8,128)(2,1)}, bf16[960,384]{1,0:T(8,128)(2,1)S(1)}, u32[]{:S(2)}, u32[]{:S(2)}) collective-permute-start(bf16[960,384]{1,0:T(8,128)(2,1)} %bitcast.12), channel_id=1, source_target_pairs={{0,1},{1,0},{2,3},{3,2},{4,5},{5,4},{6,7},{7,6},{8,9},{9,8},{10,11... | collective-permute-start | bytes 2211848 | tf_op jit(solution)/shard_map/ppermute | solution.py:196
  1.2 10.7 %collective-permute-start.1 = (bf16[256,384]{1,0:T(8,128)(2,1)}, bf16[256,384]{1,0:T(8,128)(2,1)S(1)}, u32[]{:S(2)}, u32[]{:S(2)}) collective-permute-start(bf16[256,384]{1,0:T(8,128)(2,1)} %bitcast.6), channel_id=1, source_target_pairs={{0,4},{4,8},{8,12},{12,0},{1,5},{5,9},{9,13},{13,1},{2,6},{6,10},{... | collective-permute-start | bytes 589832 | tf_op jit(solution)/shard_map/ppermute | solution.py:192
  3.8 11.4 %collective-permute-start.3 = (bf16[256,384]{1,0:T(8,128)(2,1)}, bf16[256,384]{1,0:T(8,128)(2,1)S(1)}, u32[]{:S(2)}, u32[]{:S(2)}) collective-permute-start(bf16[256,384]{1,0:T(8,128)(2,1)} %bitcast.7), channel_id=1, source_target_pairs={{0,12},{4,0},{8,4},{12,8},{1,13},{5,1},{9,5},{13,9},{2,14},{6,2},{... | collective-permute-start | bytes 589832 | tf_op jit(solution)/shard_map/ppermute | solution.py:192
  5.9 18.7 %collective-permute-start.6 = (bf16[960,384]{1,0:T(8,128)(2,1)}, bf16[960,384]{1,0:T(8,128)(2,1)S(1)}, u32[]{:S(2)}, u32[]{:S(2)}) collective-permute-start(bf16[960,384]{1,0:T(8,128)(2,1)} %bitcast.13), channel_id=1, source_target_pairs={{0,2},{1,3},{2,0},{3,1},{4,6},{5,7},{6,4},{7,5},{8,10},{9,11},{10,... | collective-permute-start | bytes 2211848 | tf_op jit(solution)/shard_map/ppermute | solution.py:196
  7.5 12.7 %collective-permute-start = (bf16[128,768]{1,0:T(8,128)(2,1)}, bf16[128,768]{1,0:T(8,128)(2,1)S(1)}, u32[]{:S(2)}, u32[]{:S(2)}) collective-permute-start(bf16[128,768]{1,0:T(8,128)(2,1)} %bitcast.9), channel_id=1, source_target_pairs={{0,4},{4,8},{8,12},{12,0},{1,5},{5,9},{9,13},{13,1},{2,6},{6,10},{... | collective-permute-start | bytes 589832 | tf_op jit(solution)/shard_map/ppermute | solution.py:192
  8.8 11.4 %copy-start.5 = (bf16[1,128,768]{2,1,0:T(8,128)(2,1)S(1)}, bf16[1,128,768]{2,1,0:T(8,128)(2,1)}, u32[]{:S(2)}) copy-start(bf16[1,128,768]{2,1,0:T(8,128)(2,1)} %param.13) | copy-start | bytes 589828
  15.2 9.4 %collective-permute-start.7 = (bf16[256,384]{1,0:T(8,128)(2,1)S(1)}, bf16[256,384]{1,0:T(8,128)(2,1)S(1)}, u32[]{:S(2)}, u32[]{:S(2)}) collective-permute-start(bf16[256,384]{1,0:T(8,128)(2,1)S(1)} %collective-permute-done.1.fa), channel_id=1, source_target_pairs={{0,4},{4,8},{8,12},{12,0},{1,5},{5,9},{9,13},{13,1},{2,6},{6,10},{... | collective-permute-start | bytes 589832 | tf_op jit(solution)/shard_map/ppermute | solution.py:192
  20.3 13.7 %collective-permute-start.5 = (bf16[128,768]{1,0:T(8,128)(2,1)S(1)}, bf16[128,768]{1,0:T(8,128)(2,1)S(1)}, u32[]{:S(2)}, u32[]{:S(2)}) collective-permute-start(bf16[128,768]{1,0:T(8,128)(2,1)S(1)} %collective-permute-done.ca), channel_id=1, source_target_pairs={{0,4},{4,8},{8,12},{12,0},{1,5},{5,9},{9,13},{13,1},{2,6},{6,10},{... | collective-permute-start | bytes 589832 | tf_op jit(solution)/shard_map/ppermute | solution.py:192
  20.3 13.7 %collective-permute-start.4 = (bf16[128,768]{1,0:T(8,128)(2,1)S(1)}, bf16[128,768]{1,0:T(8,128)(2,1)S(1)}, u32[]{:S(2)}, u32[]{:S(2)}) collective-permute-start(bf16[128,768]{1,0:T(8,128)(2,1)S(1)} %bitcast.10), channel_id=1, source_target_pairs={{0,12},{4,0},{8,4},{12,8},{1,13},{5,1},{9,5},{13,9},{2,14},{6,2},{... | collective-permute-start | bytes 589832 | tf_op jit(solution)/shard_map/ppermute | solution.py:192
  24.6 2.8 %collective-permute-start.8 = (bf16[960,384]{1,0:T(8,128)(2,1)S(1)}, bf16[960,384]{1,0:T(8,128)(2,1)S(1)}, u32[]{:S(2)}, u32[]{:S(2)}) collective-permute-start(bf16[960,384]{1,0:T(8,128)(2,1)S(1)} %collective-permute-done.6.w2), channel_id=1, source_target_pairs={{0,1},{1,0},{2,3},{3,2},{4,5},{5,4},{6,7},{7,6},{8,9},{9,8},{10,11... | collective-permute-start | bytes 2211848 | tf_op jit(solution)/shard_map/ppermute | solution.py:196
  24.6 2.9 %copy-start = (bf16[768,1280]{1,0:T(8,128)(2,1)S(1)}, bf16[768,1280]{1,0:T(8,128)(2,1)}, u32[]{:S(2)}) copy-start(bf16[768,1280]{1,0:T(8,128)(2,1)} %aw.5) | copy-start | bytes 5898244
  24.6 2.9 %copy-start.1 = (f32[768]{0:T(1024)S(1)}, f32[768]{0:T(1024)}, u32[]{:S(2)}) copy-start(f32[768]{0:T(1024)} %gain.3) | copy-start | bytes 9220
  31.3 2.7 %copy-start.3 = (bf16[768,768]{1,0:T(8,128)(2,1)S(1)}, bf16[768,768]{1,0:T(8,128)(2,1)}, u32[]{:S(2)}) copy-start(bf16[768,768]{1,0:T(8,128)(2,1)} %ow.3) | copy-start | bytes 3538948
  36.4 2.1 %collective-permute-start.9 = (bf16[192,768]{1,0:T(8,128)(2,1)S(1)}, bf16[192,768]{1,0:T(8,128)(2,1)S(1)}, u32[]{:S(2)}, u32[]{:S(2)}) collective-permute-start(bf16[192,768]{1,0:T(8,128)(2,1)S(1)} %get-tuple-element.59), channel_id=1, source_target_pairs={{0,1},{1,0},{2,3},{3,2},{4,5},{5,4},{6,7},{7,6},{8,9},{9,8},{10,11... | collective-permute-start | bytes 884744 | tf_op jit(solution)/shard_map/ppermute | solution.py:196
  38.6 9.9 %collective-permute-start.10 = (bf16[192,768]{1,0:T(8,128)(2,1)S(1)}, bf16[192,768]{1,0:T(8,128)(2,1)S(1)}, u32[]{:S(2)}, u32[]{:S(2)}) collective-permute-start(bf16[192,768]{1,0:T(8,128)(2,1)S(1)} %add_convert_fusion.1), channel_id=1, source_target_pairs={{0,2},{1,3},{2,0},{3,1},{4,6},{5,7},{6,4},{7,5},{8,10},{9,11},{10,... | collective-permute-start | bytes 884744 | tf_op jit(solution)/shard_map/ppermute | solution.py:196
  42.0 1.8 %collective-permute-start.13 = (bf16[112,256]{1,0:T(8,128)(2,1)S(1)}, bf16[112,256]{1,0:T(8,128)(2,1)S(1)}, u32[]{:S(2)}, u32[]{:S(2)}) collective-permute-start(bf16[112,256]{1,0:T(8,128)(2,1)S(1)} %get-tuple-element.71), channel_id=1, source_target_pairs={{0,1},{1,0},{2,3},{3,2},{4,5},{5,4},{6,7},{7,6},{8,9},{9,8},{10,11... | collective-permute-start | bytes 172040 | tf_op jit(solution)/shard_map/ppermute | solution.py:196
  42.1 1.8 %collective-permute-start.12 = (bf16[96,256]{1,0:T(8,128)(2,1)S(1)}, bf16[96,256]{1,0:T(8,128)(2,1)S(1)}, u32[]{:S(2)}, u32[]{:S(2)}) collective-permute-start(bf16[96,256]{1,0:T(8,128)(2,1)S(1)} %get-tuple-element.70), channel_id=1, source_target_pairs={{0,1},{1,0},{2,3},{3,2},{4,5},{5,4},{6,7},{7,6},{8,9},{9,8},{10,11... | collective-permute-start | bytes 147464 | tf_op jit(solution)/shard_map/ppermute | solution.py:196
  43.9 6.0 %collective-permute-start.14 = (bf16[208,256]{1,0:T(8,128)(2,1)S(1)}, bf16[208,256]{1,0:T(8,128)(2,1)S(1)}, u32[]{:S(2)}, u32[]{:S(2)}) collective-permute-start(bf16[208,256]{1,0:T(8,128)(2,1)S(1)} %add_convert_fusion.3), channel_id=1, source_target_pairs={{0,2},{1,3},{2,0},{3,1},{4,6},{5,7},{6,4},{7,5},{8,10},{9,11},{10,... | collective-permute-start | bytes 319496 | tf_op jit(solution)/shard_map/ppermute | solution.py:196
  48.6 1.6 %collective-permute-start.11 = (bf16[192,768]{1,0:T(8,128)(2,1)S(1)}, bf16[192,768]{1,0:T(8,128)(2,1)S(1)}, u32[]{:S(2)}, u32[]{:S(2)}) collective-permute-start(bf16[192,768]{1,0:T(8,128)(2,1)S(1)} %add_convert_fusion.whole_v), channel_id=1, source_target_pairs={{0,1},{1,0},{2,3},{3,2},{4,5},{5,4},{6,7},{7,6},{8,9},{9,8},{10,11... | collective-permute-start | bytes 884744 | tf_op jit(solution)/shard_map/ppermute | solution.py:196
  50.0 1.4 %collective-permute-start.15 = (bf16[208,256]{1,0:T(8,128)(2,1)S(1)}, bf16[208,256]{1,0:T(8,128)(2,1)S(1)}, u32[]{:S(2)}, u32[]{:S(2)}) collective-permute-start(bf16[208,256]{1,0:T(8,128)(2,1)S(1)} %add_convert_fusion.2.whole_k), channel_id=1, source_target_pairs={{0,1},{1,0},{2,3},{3,2},{4,5},{5,4},{6,7},{7,6},{8,9},{9,8},{10,11... | collective-permute-start | bytes 319496 | tf_op jit(solution)/shard_map/ppermute | solution.py:196

commit v6 on v5

--- a/solution.py
+++ b/solution.py
@@ -345,13 +345,24 @@
             write(send, 1 - at)
 
 
-def value_kernel(c0, ca, cb, cc, normed_t, probs_t, att_t, aw, ow, grad, keep, send, mixed, cot, cot_t, d_value):
+def early_grad_kernel(c0, ca, ow, early):
+    early[0] = mm(c0[...], ow[...]).astype(BF16)
+    early[1] = mm(ca[...], ow[...]).astype(BF16)
+
+
+def value_kernel(early, c0, ca, cb, cc, normed_t, probs_t, att_t, aw, ow, grad, keep, send, mixed, cot, cot_t, d_value):
     z, d = lax.axis_index("seq"), lax.axis_index("dp")
     for ref, off in ((c0, 0), (ca, 3), (cb, 1), (cc, 2)):
         start = pl.multiple_of(lax.rem(z + off, SEQ) * TOK, TOK)
         cot[pl.ds(start, TOK), :] = ref[...]
     cot_t[...] = mm(row_picker(z), cot[...], NT).astype(BF16)
-    grad[...] = mm(cot[...], ow[...]).astype(BF16)
+    for index, off in ((0, 0), (1, 3)):
+        start = pl.multiple_of(lax.rem(z + off, SEQ) * TOK, TOK)
+        grad[pl.ds(start, TOK), :] = early[index]
+    late = mm(jnp.concatenate([cb[...], cc[...]], axis=0), ow[...]).astype(BF16)
+    for index, off in ((0, 1), (1, 2)):
+        start = pl.multiple_of(lax.rem(z + off, SEQ) * TOK, TOK)
+        grad[pl.ds(start, TOK), :] = late[index * TOK : (index + 1) * TOK, :]
     out_part = mm(cot_t[...], att_t[...], NT)
     for h in range(HEADS):
         lanes = slice(h * VAL_DIM, (h + 1) * VAL_DIM)
@@ -495,7 +506,10 @@
     )
     ca, windows = lax.optimization_barrier((ca, windows))
     cb, cc = ring(to_left, SEQ - 1), ring(ca, 1)
-    w2, fc, windows = lax.optimization_barrier((w2, fc, windows))
+    (early,) = kernel_call(
+        early_grad_kernel, [((2, TOK, WIDTH), BF16)], [], 1 << 24, c0, ca, output_weight
+    )
+    w2, fc, windows, early = lax.optimization_barrier((w2, fc, windows, early))
     w3 = swap(w2, 1)
     windows, hid_near, hid_two = kernel_call(
         mend_kernel,
@@ -526,7 +540,7 @@
         [((LEN, VW), BF16), ((ROWS, VW), F32), ((ROWS, VW), BF16), ((ROWS, 128), F32)],
         [((LEN, WIDTH), BF16), ((ROWS, LEN), BF16), ((LEN, VW), BF16)],
         1 << 31,
-        c0, ca, cb, cc, normed_t, probs_t, att_t, attend_weight, output_weight,
+        early, c0, ca, cb, cc, normed_t, probs_t, att_t, attend_weight, output_weight,
     )
     query_early, key_early = kernel_call(
         early_key_kernel,

time: 52.5 us -> 52.2 us (level)
    pallas_call x11 -> x12, Pallas kernels: 22.2 us -> 22.3 us  [kernel_call(): pl.pallas_call(body, in_specs=[away if i in far else whole for i in range...]
  transfers between devices with their start and end apart: 16 -> 16, of which waited for: 8 -> 7; matrix products, arithmetic and copies ran while one was open for 0% -> 0% of each run, Pallas kernels for 36% -> 37%
where the time goes in v6:
time: 52.2 us; the launch traced here: 52 us
  Pallas kernels  22.3 us (43%)
  starting transfers between devices  15.5 us (30%)
  waiting for transfers between devices  13.2 us (25%)
  between operations  0.84 us (2%)
    pallas_call x12, Pallas kernels, kernel_call(): pl.pallas_call(body, in_specs=[away if i in far else whole for i in range...  22.3 us
    ppermute x6, starting transfers between devices, ring(): lax.ppermute(value, 'seq', [(i, (i + step) % SEQ) for i in range(SEQ)])  9.9 us
    ppermute x6, waiting for transfers between devices, ring(): lax.ppermute(value, 'seq', [(i, (i + step) % SEQ) for i in range(SEQ)])  7.38 us
    ppermute x10, waiting for transfers between devices, swap(): return lax.ppermute(value, 'dp', [(i, i ^ bit) for i in range(DP)])  5.81 us
    ppermute x10, starting transfers between devices, swap(): return lax.ppermute(value, 'dp', [(i, i ^ bit) for i in range(DP)])  5.57 us
  transfers between devices with their start and end apart: 16, of which 7 were waited for; matrix products, arithmetic and copies ran while one was open for 0% of the time, Pallas kernels for 37%

profile of v6, /device:TPU:0, one launch (start us, length us, event | category | flops | bytes accessed | tf_op | source)
XLA Modules:
  0.0 52.0 jit_solution(10788586553554325352)
XLA Ops:
  0.7 0.5 collective-permute-start.2
  1.2 2.6 %collective-permute-start.1 = (bf16[256,384]{1,0:T(8,128)(2,1)}, bf16[256,384]{1,0:T(8,128)(2,1)S(1)}, u32[]{:S(2)}, u32[]{:S(2)}) collective-permute-start(bf16[256,384]{1,0:T(8,128)(2,1)} %bitcast.10), channel_id=1, source_target_pairs={{0,4},{4,8},{8,12},{12,0},{1,5},{5,9},{9,13},{13,1},{2,6},{6,10},{... | collective-permute-start | bytes 589832 | tf_op jit(solution)/shard_map/ppermute | solution.py:192
  3.8 2.1 %collective-permute-start.3 = (bf16[256,384]{1,0:T(8,128)(2,1)}, bf16[256,384]{1,0:T(8,128)(2,1)S(1)}, u32[]{:S(2)}, u32[]{:S(2)}) collective-permute-start(bf16[256,384]{1,0:T(8,128)(2,1)} %bitcast.11), channel_id=1, source_target_pairs={{0,12},{4,0},{8,4},{12,8},{1,13},{5,1},{9,5},{13,9},{2,14},{6,2},{... | collective-permute-start | bytes 589832 | tf_op jit(solution)/shard_map/ppermute | solution.py:192
  5.9 1.6 %collective-permute-start = (bf16[960,384]{1,0:T(8,128)(2,1)}, bf16[960,384]{1,0:T(8,128)(2,1)S(1)}, u32[]{:S(2)}, u32[]{:S(2)}) collective-permute-start(bf16[960,384]{1,0:T(8,128)(2,1)} %bitcast.14), channel_id=1, source_target_pairs={{0,2},{1,3},{2,0},{3,1},{4,6},{5,7},{6,4},{7,5},{8,10},{9,11},{10,... | collective-permute-start | bytes 2211848 | tf_op jit(solution)/shard_map/ppermute | solution.py:196
  7.6 1.3 %shard_map.102.taps = bf16[384,1920]{1,0:T(8,128)(2,1)S(1)} custom-call(bf16[960,384]{1,0:T(8,128)(2,1)} %bitcast.15, bf16[960,384]{1,0:T(8,128)(2,1)S(1)} %collective-permute-done.2.w1), custom_call_target="tpu_custom_call" | custom-call | flops 16777216 | bytes 65536 | tf_op jit(solution)/shard_map/pallas_call | solution.py:465
  8.9 3.0 %collective-permute-done.1.fa = bf16[256,384]{1,0:T(8,128)(2,1)S(1)} collective-permute-done((bf16[256,384]{1,0:T(8,128)(2,1)}, bf16[256,384]{1,0:T(8,128)(2,1)S(1)}, u32[]{:S(2)}, u32[]{:S(2)}) %collective-permute-start.1) | collective-permute-done | bytes 196640 | tf_op jit(solution)/shard_map/ppermute | solution.py:192
  11.8 3.4 %collective-permute-done.3.fb = bf16[256,384]{1,0:T(8,128)(2,1)S(1)} collective-permute-done((bf16[256,384]{1,0:T(8,128)(2,1)}, bf16[256,384]{1,0:T(8,128)(2,1)S(1)}, u32[]{:S(2)}, u32[]{:S(2)}) %collective-permute-start.3) | collective-permute-done | bytes 196640 | tf_op jit(solution)/shard_map/ppermute | solution.py:192
  15.2 1.3 %collective-permute-start.4 = (bf16[256,384]{1,0:T(8,128)(2,1)S(1)}, bf16[256,384]{1,0:T(8,128)(2,1)S(1)}, u32[]{:S(2)}, u32[]{:S(2)}) collective-permute-start(bf16[256,384]{1,0:T(8,128)(2,1)S(1)} %collective-permute-done.1.fa), channel_id=1, source_target_pairs={{0,4},{4,8},{8,12},{12,0},{1,5},{5,9},{9,13},{13,1},{2,6},{6,10},{... | collective-permute-start | bytes 589832 | tf_op jit(solution)/shard_map/ppermute | solution.py:192
  16.5 2.7 %shard_map.103 = (bf16[512,2304]{1,0:T(8,128)(2,1)S(1)}, bf16[512,384]{1,0:T(8,128)(2,1)S(1)}) custom-call(bf16[256,384]{1,0:T(8,128)(2,1)S(1)} %bitcast.12, bf16[256,384]{1,0:T(8,128)(2,1)S(1)} %collective-permute-done.1.fa, bf16[256,384]{1,0:T(8,128)(2,1)S(1)} %collective-permute-done.3.fb, bf16[384,1920]{1,0:T(8,128)(2,1)S(1)} %shard_map.102.taps, ...), custom_call_target="tpu_custom_call" | custom-call | flops 8589934592 | bytes 65536 | tf_op jit(solution)/shard_map/pallas_call | solution.py:465
  19.2 1.0 %collective-permute-done.5.ca = bf16[128,768]{1,0:T(8,128)(2,1)S(1)} collective-permute-done((bf16[128,768]{1,0:T(8,128)(2,1)}, bf16[128,768]{1,0:T(8,128)(2,1)S(1)}, u32[]{:S(2)}, u32[]{:S(2)}) %collective-permute-start.5) | collective-permute-done | bytes 196640 | tf_op jit(solution)/shard_map/ppermute | solution.py:192
  20.3 3.8 %collective-permute-start.6 = (bf16[128,768]{1,0:T(8,128)(2,1)S(1)}, bf16[128,768]{1,0:T(8,128)(2,1)S(1)}, u32[]{:S(2)}, u32[]{:S(2)}) collective-permute-start(bf16[128,768]{1,0:T(8,128)(2,1)S(1)} %bitcast.7), channel_id=1, source_target_pairs={{0,12},{4,0},{8,4},{12,8},{1,13},{5,1},{9,5},{13,9},{2,14},{6,2},{... | collective-permute-start | bytes 589832 | tf_op jit(solution)/shard_map/ppermute | solution.py:192
  24.7 2.8 %shard_map.105 = (bf16[512,2304]{1,0:T(8,128)(2,1)S(1)}, bf16[512,384]{1,0:T(8,128)(2,1)S(1)}, bf16[512,192]{1,0:T(8,128)(2,1)S(1)}) custom-call(bf16[256,384]{1,0:T(8,128)(2,1)S(1)} %collective-permute-done.1.fa, bf16[256,384]{1,0:T(8,128)(2,1)S(1)} %collective-permute-done.3.fb, bf16[256,384]{1,0:T(8,128)(2,1)S(1)} %collective-permute-done.4.fc, ...), custom_call_target="tpu_custom_call" | custom-call | flops 8589934592 | bytes 65536 | tf_op jit(solution)/shard_map/pallas_call | solution.py:465
  27.5 3.8 %shard_map.106 = (bf16[2,512,384]{2,1,0:T(8,128)(2,1)S(1)}, bf16[512,768]{1,0:T(8,128)(2,1)}, bf16[512,1280]{1,0:T(8,128)(2,1)S(1)}, bf16[192,512]{1,0:T(8,128)(2,1)S(1)}) custom-call(bf16[512,2304]{1,0:T(8,128)(2,1)S(1)} %get-tuple-element.53.windows, bf16[512,384]{1,0:T(8,128)(2,1)S(1)} %get-tuple-element.54.hid_near, ...), custom_call_target="tpu_custom_call" | custom-call | flops 16777216 | bytes 65536 | tf_op jit(solution)/shard_map/pallas_call | solution.py:465
  31.3 2.7 %shard_map.107 = (bf16[4,512,512]{2,1,0:T(8,128)(2,1)S(1)}, bf16[768,512]{1,0:T(8,128)(2,1)S(1)}) custom-call(bf16[512,1280]{1,0:T(8,128)(2,1)S(1)} %get-tuple-element.57.proj), custom_call_target="tpu_custom_call" | custom-call | flops 536870912 | bytes 65536 | tf_op jit(solution)/shard_map/pallas_call | solution.py:465
  34.0 2.1 %shard_map.108 = (bf16[512,768]{1,0:T(8,128)(2,1)S(1)}, f32[192,768]{1,0:T(8,128)S(1)}, bf16[192,768]{1,0:T(8,128)(2,1)S(1)}, f32[192,128]{1,0:T(8,128)S(1)}) custom-call(bf16[2,128,768]{2,1,0:T(8,128)(2,1)S(1)} %shard_map.104.early, bf16[128,768]{1,0:T(8,128)(2,1)S(1)} %bitcast.9, bf16[128,768]{1,0:T(8,128)(2,1)S(1)} %collective-permute-done.5.ca, ...), custom_call_target="tpu_custom_call" | custom-call | flops 2147483648 | bytes 65536 | tf_op jit(solution)/shard_map/pallas_call | solution.py:465
  36.1 0.5 collective-permute-start.9
  36.6 1.6 %shard_map.109 = (bf16[128,512]{1,0:T(8,128)(2,1)S(1)}, bf16[512,128]{1,0:T(8,128)(2,1)S(1)}) custom-call(bf16[512,768]{1,0:T(8,128)(2,1)S(1)} %get-tuple-element.62.grad, bf16[512,1280]{1,0:T(8,128)(2,1)S(1)} %get-tuple-element.57.proj, bf16[4,512,512]{2,1,0:T(8,128)(2,1)S(1)} %get-tuple-element.58.probs_t), custom_call_target="tpu_custom_call" | custom-call | flops 8589934592 | bytes 65536 | tf_op jit(solution)/shard_map/pallas_call | solution.py:465
  38.3 1.7 %collective-permute-start.10 = (bf16[192,768]{1,0:T(8,128)(2,1)S(1)}, bf16[192,768]{1,0:T(8,128)(2,1)S(1)}, u32[]{:S(2)}, u32[]{:S(2)}) collective-permute-start(bf16[192,768]{1,0:T(8,128)(2,1)S(1)} %add_convert_fusion.1), channel_id=1, source_target_pairs={{0,2},{1,3},{2,0},{3,1},{4,6},{5,7},{6,4},{7,5},{8,10},{9,11},{10,... | collective-permute-start | bytes 884744 | tf_op jit(solution)/shard_map/ppermute | solution.py:196
  40.0 1.8 %shard_map.111 = (f32[208,256]{1,0:T(8,128)S(1)}, bf16[96,256]{1,0:T(8,128)(2,1)S(1)}, bf16[112,256]{1,0:T(8,128)(2,1)S(1)}) custom-call(bf16[512,768]{1,0:T(8,128)(2,1)S(1)} %get-tuple-element.62.grad, bf16[512,1280]{1,0:T(8,128)(2,1)S(1)} %get-tuple-element.57.proj, bf16[4,512,512]{2,1,0:T(8,128)(2,1)S(1)} %get-tuple-element.58.probs_t, ...), custom_call_target="tpu_custom_call" | custom-call | flops 65536 | bytes 65536 | tf_op jit(solution)/shard_map/pallas_call | solution.py:465
  42.4 1.3 %shard_map.110 = f32[128,768]{1,0:T(8,128)} custom-call(bf16[2,512,384]{2,1,0:T(8,128)(2,1)S(1)} %get-tuple-element.65.hid, bf16[768,512]{1,0:T(8,128)(2,1)S(1)} %get-tuple-element.59.att_t, bf16[768,768]{1,0:T(8,128)(2,1)S(1)} %copy-done.1), custom_call_target="tpu_custom_call" | custom-call | flops 8589934592 | bytes 65536 | tf_op jit(solution)/shard_map/pallas_call | solution.py:465
  44.1 4.1 %collective-permute-done.10 = bf16[192,768]{1,0:T(8,128)(2,1)S(1)} collective-permute-done((bf16[192,768]{1,0:T(8,128)(2,1)S(1)}, bf16[192,768]{1,0:T(8,128)(2,1)S(1)}, u32[]{:S(2)}, u32[]{:S(2)}) %collective-permute-start.10) | collective-permute-done | bytes 294944 | tf_op jit(solution)/shard_map/ppermute | solution.py:196
  48.4 1.2 %collective-permute-done.14 = bf16[208,256]{1,0:T(8,128)(2,1)S(1)} collective-permute-done((bf16[208,256]{1,0:T(8,128)(2,1)S(1)}, bf16[208,256]{1,0:T(8,128)(2,1)S(1)}, u32[]{:S(2)}, u32[]{:S(2)}) %collective-permute-start.14) | collective-permute-done | bytes 106528 | tf_op jit(solution)/shard_map/ppermute | solution.py:196
  49.9 0.9 %shard_map.113 = f32[192,768]{1,0:T(8,128)} custom-call(bf16[192,768]{1,0:T(8,128)(2,1)S(1)} %add_convert_fusion.whole_v, bf16[192,768]{1,0:T(8,128)(2,1)S(1)} %collective-permute-done.11.other_v), custom_call_target="tpu_custom_call" | custom-call | flops 8589934592 | bytes 65536 | tf_op jit(solution)/shard_map/pallas_call | solution.py:465
  51.0 1.0 %shard_map.112 = (f32[192,1280]{1,0:T(8,128)}, f32[192]{0:T(256)}) custom-call(bf16[192,768]{1,0:T(8,128)(2,1)S(1)} %add_convert_fusion.whole_v, bf16[192,768]{1,0:T(8,128)(2,1)S(1)} %collective-permute-done.11.other_v, bf16[208,256]{1,0:T(8,128)(2,1)S(1)} %add_convert_fusion.2.whole_k, bf16[208,256]{1,0:T(8,128)(2,1)S(1)} %collective-permute-done.15.other_k), custom_call_target="tpu_custom_call" | custom-call | flops 65536 | bytes 65536 | tf_op jit(solution)/shard_map/pallas_call | solution.py:465
  (36 shorter events, 2.4 us)
Async XLA Ops:
  0.6 15.9 %copy-start.5 = (bf16[1,256,384]{2,1,0:T(8,128)(2,1)S(1)}, bf16[1,256,384]{2,1,0:T(8,128)(2,1)}, u32[]{:S(2)}) copy-start(bf16[1,256,384]{2,1,0:T(8,128)(2,1)} %param.7) | copy-start | bytes 589828
  0.6 15.9 %copy-start.4 = (f32[768]{0:T(1024)S(1)}, f32[768]{0:T(1024)}, u32[]{:S(2)}) copy-start(f32[768]{0:T(1024)} %bias.5) | copy-start | bytes 9220
  0.7 6.9 %collective-permute-start.2 = (bf16[960,384]{1,0:T(8,128)(2,1)}, bf16[960,384]{1,0:T(8,128)(2,1)S(1)}, u32[]{:S(2)}, u32[]{:S(2)}) collective-permute-start(bf16[960,384]{1,0:T(8,128)(2,1)} %bitcast.13), channel_id=1, source_target_pairs={{0,1},{1,0},{2,3},{3,2},{4,5},{5,4},{6,7},{7,6},{8,9},{9,8},{10,11... | collective-permute-start | bytes 2211848 | tf_op jit(solution)/shard_map/ppermute | solution.py:196
  1.2 10.7 %collective-permute-start.1 = (bf16[256,384]{1,0:T(8,128)(2,1)}, bf16[256,384]{1,0:T(8,128)(2,1)S(1)}, u32[]{:S(2)}, u32[]{:S(2)}) collective-permute-start(bf16[256,384]{1,0:T(8,128)(2,1)} %bitcast.10), channel_id=1, source_target_pairs={{0,4},{4,8},{8,12},{12,0},{1,5},{5,9},{9,13},{13,1},{2,6},{6,10},{... | collective-permute-start | bytes 589832 | tf_op jit(solution)/shard_map/ppermute | solution.py:192
  3.8 11.4 %collective-permute-start.3 = (bf16[256,384]{1,0:T(8,128)(2,1)}, bf16[256,384]{1,0:T(8,128)(2,1)S(1)}, u32[]{:S(2)}, u32[]{:S(2)}) collective-permute-start(bf16[256,384]{1,0:T(8,128)(2,1)} %bitcast.11), channel_id=1, source_target_pairs={{0,12},{4,0},{8,4},{12,8},{1,13},{5,1},{9,5},{13,9},{2,14},{6,2},{... | collective-permute-start | bytes 589832 | tf_op jit(solution)/shard_map/ppermute | solution.py:192
  5.9 18.7 %collective-permute-start = (bf16[960,384]{1,0:T(8,128)(2,1)}, bf16[960,384]{1,0:T(8,128)(2,1)S(1)}, u32[]{:S(2)}, u32[]{:S(2)}) collective-permute-start(bf16[960,384]{1,0:T(8,128)(2,1)} %bitcast.14), channel_id=1, source_target_pairs={{0,2},{1,3},{2,0},{3,1},{4,6},{5,7},{6,4},{7,5},{8,10},{9,11},{10,... | collective-permute-start | bytes 2211848 | tf_op jit(solution)/shard_map/ppermute | solution.py:196
  7.5 12.7 %collective-permute-start.5 = (bf16[128,768]{1,0:T(8,128)(2,1)}, bf16[128,768]{1,0:T(8,128)(2,1)S(1)}, u32[]{:S(2)}, u32[]{:S(2)}) collective-permute-start(bf16[128,768]{1,0:T(8,128)(2,1)} %bitcast.6), channel_id=1, source_target_pairs={{0,4},{4,8},{8,12},{12,0},{1,5},{5,9},{9,13},{13,1},{2,6},{6,10},{... | collective-permute-start | bytes 589832 | tf_op jit(solution)/shard_map/ppermute | solution.py:192
  8.8 11.4 %copy-start.2 = (bf16[1,128,768]{2,1,0:T(8,128)(2,1)S(1)}, bf16[1,128,768]{2,1,0:T(8,128)(2,1)}, u32[]{:S(2)}) copy-start(bf16[1,128,768]{2,1,0:T(8,128)(2,1)} %param.13) | copy-start | bytes 589828
  8.9 15.2 %copy-start.1 = (bf16[768,768]{1,0:T(8,128)(2,1)S(1)}, bf16[768,768]{1,0:T(8,128)(2,1)}, u32[]{:S(2)}) copy-start(bf16[768,768]{1,0:T(8,128)(2,1)} %ow.5) | copy-start | bytes 3538948
  15.2 9.4 %collective-permute-start.4 = (bf16[256,384]{1,0:T(8,128)(2,1)S(1)}, bf16[256,384]{1,0:T(8,128)(2,1)S(1)}, u32[]{:S(2)}, u32[]{:S(2)}) collective-permute-start(bf16[256,384]{1,0:T(8,128)(2,1)S(1)} %collective-permute-done.1.fa), channel_id=1, source_target_pairs={{0,4},{4,8},{8,12},{12,0},{1,5},{5,9},{9,13},{13,1},{2,6},{6,10},{... | collective-permute-start | bytes 589832 | tf_op jit(solution)/shard_map/ppermute | solution.py:192
  20.3 13.7 %collective-permute-start.7 = (bf16[128,768]{1,0:T(8,128)(2,1)S(1)}, bf16[128,768]{1,0:T(8,128)(2,1)S(1)}, u32[]{:S(2)}, u32[]{:S(2)}) collective-permute-start(bf16[128,768]{1,0:T(8,128)(2,1)S(1)} %collective-permute-done.5.ca), channel_id=1, source_target_pairs={{0,4},{4,8},{8,12},{12,0},{1,5},{5,9},{9,13},{13,1},{2,6},{6,10},{... | collective-permute-start | bytes 589832 | tf_op jit(solution)/shard_map/ppermute | solution.py:192
  20.3 13.7 %collective-permute-start.6 = (bf16[128,768]{1,0:T(8,128)(2,1)S(1)}, bf16[128,768]{1,0:T(8,128)(2,1)S(1)}, u32[]{:S(2)}, u32[]{:S(2)}) collective-permute-start(bf16[128,768]{1,0:T(8,128)(2,1)S(1)} %bitcast.7), channel_id=1, source_target_pairs={{0,12},{4,0},{8,4},{12,8},{1,13},{5,1},{9,5},{13,9},{2,14},{6,2},{... | collective-permute-start | bytes 589832 | tf_op jit(solution)/shard_map/ppermute | solution.py:192
  24.6 2.9 %collective-permute-start.8 = (bf16[960,384]{1,0:T(8,128)(2,1)S(1)}, bf16[960,384]{1,0:T(8,128)(2,1)S(1)}, u32[]{:S(2)}, u32[]{:S(2)}) collective-permute-start(bf16[960,384]{1,0:T(8,128)(2,1)S(1)} %collective-permute-done.w2), channel_id=1, source_target_pairs={{0,1},{1,0},{2,3},{3,2},{4,5},{5,4},{6,7},{7,6},{8,9},{9,8},{10,11... | collective-permute-start | bytes 2211848 | tf_op jit(solution)/shard_map/ppermute | solution.py:196
  24.7 2.8 %copy-start = (bf16[768,1280]{1,0:T(8,128)(2,1)S(1)}, bf16[768,1280]{1,0:T(8,128)(2,1)}, u32[]{:S(2)}) copy-start(bf16[768,1280]{1,0:T(8,128)(2,1)} %aw.5) | copy-start | bytes 5898244
  24.7 2.8 %copy-start.3 = (f32[768]{0:T(1024)S(1)}, f32[768]{0:T(1024)}, u32[]{:S(2)}) copy-start(f32[768]{0:T(1024)} %gain.3) | copy-start | bytes 9220
  36.1 2.1 %collective-permute-start.9 = (bf16[192,768]{1,0:T(8,128)(2,1)S(1)}, bf16[192,768]{1,0:T(8,128)(2,1)S(1)}, u32[]{:S(2)}, u32[]{:S(2)}) collective-permute-start(bf16[192,768]{1,0:T(8,128)(2,1)S(1)} %get-tuple-element.61), channel_id=1, source_target_pairs={{0,1},{1,0},{2,3},{3,2},{4,5},{5,4},{6,7},{7,6},{8,9},{9,8},{10,11... | collective-permute-start | bytes 884744 | tf_op jit(solution)/shard_map/ppermute | solution.py:196
  38.3 9.9 %collective-permute-start.10 = (bf16[192,768]{1,0:T(8,128)(2,1)S(1)}, bf16[192,768]{1,0:T(8,128)(2,1)S(1)}, u32[]{:S(2)}, u32[]{:S(2)}) collective-permute-start(bf16[192,768]{1,0:T(8,128)(2,1)S(1)} %add_convert_fusion.1), channel_id=1, source_target_pairs={{0,2},{1,3},{2,0},{3,1},{4,6},{5,7},{6,4},{7,5},{8,10},{9,11},{10,... | collective-permute-start | bytes 884744 | tf_op jit(solution)/shard_map/ppermute | solution.py:196
  41.8 1.8 %collective-permute-start.13 = (bf16[112,256]{1,0:T(8,128)(2,1)S(1)}, bf16[112,256]{1,0:T(8,128)(2,1)S(1)}, u32[]{:S(2)}, u32[]{:S(2)}) collective-permute-start(bf16[112,256]{1,0:T(8,128)(2,1)S(1)} %get-tuple-element.73), channel_id=1, source_target_pairs={{0,1},{1,0},{2,3},{3,2},{4,5},{5,4},{6,7},{7,6},{8,9},{9,8},{10,11... | collective-permute-start | bytes 172040 | tf_op jit(solution)/shard_map/ppermute | solution.py:196
  41.9 1.8 %collective-permute-start.12 = (bf16[96,256]{1,0:T(8,128)(2,1)S(1)}, bf16[96,256]{1,0:T(8,128)(2,1)S(1)}, u32[]{:S(2)}, u32[]{:S(2)}) collective-permute-start(bf16[96,256]{1,0:T(8,128)(2,1)S(1)} %get-tuple-element.72), channel_id=1, source_target_pairs={{0,1},{1,0},{2,3},{3,2},{4,5},{5,4},{6,7},{7,6},{8,9},{9,8},{10,11... | collective-permute-start | bytes 147464 | tf_op jit(solution)/shard_map/ppermute | solution.py:196
  43.7 5.9 %collective-permute-start.14 = (bf16[208,256]{1,0:T(8,128)(2,1)S(1)}, bf16[208,256]{1,0:T(8,128)(2,1)S(1)}, u32[]{:S(2)}, u32[]{:S(2)}) collective-permute-start(bf16[208,256]{1,0:T(8,128)(2,1)S(1)} %add_convert_fusion.3), channel_id=1, source_target_pairs={{0,2},{1,3},{2,0},{3,1},{4,6},{5,7},{6,4},{7,5},{8,10},{9,11},{10,... | collective-permute-start | bytes 319496 | tf_op jit(solution)/shard_map/ppermute | solution.py:196
  48.3 1.6 %collective-permute-start.11 = (bf16[192,768]{1,0:T(8,128)(2,1)S(1)}, bf16[192,768]{1,0:T(8,128)(2,1)S(1)}, u32[]{:S(2)}, u32[]{:S(2)}) collective-permute-start(bf16[192,768]{1,0:T(8,128)(2,1)S(1)} %add_convert_fusion.whole_v), channel_id=1, source_target_pairs={{0,1},{1,0},{2,3},{3,2},{4,5},{5,4},{6,7},{7,6},{8,9},{9,8},{10,11... | collective-permute-start | bytes 884744 | tf_op jit(solution)/shard_map/ppermute | solution.py:196
  49.6 1.4 %collective-permute-start.15 = (bf16[208,256]{1,0:T(8,128)(2,1)S(1)}, bf16[208,256]{1,0:T(8,128)(2,1)S(1)}, u32[]{:S(2)}, u32[]{:S(2)}) collective-permute-start(bf16[208,256]{1,0:T(8,128)(2,1)S(1)} %add_convert_fusion.2.whole_k), channel_id=1, source_target_pairs={{0,1},{1,0},{2,3},{3,2},{4,5},{5,4},{6,7},{7,6},{8,9},{9,8},{10,11... | collective-permute-start | bytes 319496 | tf_op jit(solution)/shard_map/ppermute | solution.py:196

commit v7 on v6

--- a/solution.py
+++ b/solution.py
@@ -537,7 +537,7 @@
     )
     grad, keep_v, send_v, mixed = kernel_call(
         value_kernel,
-        [((LEN, VW), BF16), ((ROWS, VW), F32), ((ROWS, VW), BF16), ((ROWS, 128), F32)],
+        [((LEN, VW), BF16), ((ROWS, VW), BF16), ((ROWS, VW), BF16), ((ROWS, 128), F32)],
         [((LEN, WIDTH), BF16), ((ROWS, LEN), BF16), ((LEN, VW), BF16)],
         1 << 31,
         early, c0, ca, cb, cc, normed_t, probs_t, att_t, attend_weight, output_weight,

time: 52.2 us -> 52.2 us (level)
  no operation moved by 1% of the time
where the time goes in v7:
time: 52.2 us; the launch traced here: 52.1 us
  Pallas kernels  22.3 us (43%)
  starting transfers between devices  15.4 us (30%)
  waiting for transfers between devices  13.2 us (25%)
  between operations  0.84 us (2%)
    pallas_call x12, Pallas kernels, kernel_call(): pl.pallas_call(body, in_specs=[away if i in far else whole for i in range...  22.3 us
    ppermute x6, starting transfers between devices, ring(): lax.ppermute(value, 'seq', [(i, (i + step) % SEQ) for i in range(SEQ)])  9.9 us
    ppermute x6, waiting for transfers between devices, ring(): lax.ppermute(value, 'seq', [(i, (i + step) % SEQ) for i in range(SEQ)])  7.38 us
    ppermute x10, waiting for transfers between devices, swap(): return lax.ppermute(value, 'dp', [(i, i ^ bit) for i in range(DP)])  5.84 us
    ppermute x10, starting transfers between devices, swap(): return lax.ppermute(value, 'dp', [(i, i ^ bit) for i in range(DP)])  5.54 us
  transfers between devices with their start and end apart: 16, of which 7 were waited for; matrix products, arithmetic and copies ran while one was open for 0% of the time, Pallas kernels for 37%

profile of v7, /device:TPU:0, one launch (start us, length us, event | category | flops | bytes accessed | tf_op | source)
XLA Modules:
  0.0 52.1 jit_solution(14105778913155433270)
XLA Ops:
  0.7 0.5 collective-permute-start.2
  1.2 2.6 %collective-permute-start.1 = (bf16[256,384]{1,0:T(8,128)(2,1)}, bf16[256,384]{1,0:T(8,128)(2,1)S(1)}, u32[]{:S(2)}, u32[]{:S(2)}) collective-permute-start(bf16[256,384]{1,0:T(8,128)(2,1)} %bitcast.10), channel_id=1, source_target_pairs={{0,4},{4,8},{8,12},{12,0},{1,5},{5,9},{9,13},{13,1},{2,6},{6,10},{... | collective-permute-start | bytes 589832 | tf_op jit(solution)/shard_map/ppermute | solution.py:192
  3.8 2.1 %collective-permute-start.3 = (bf16[256,384]{1,0:T(8,128)(2,1)}, bf16[256,384]{1,0:T(8,128)(2,1)S(1)}, u32[]{:S(2)}, u32[]{:S(2)}) collective-permute-start(bf16[256,384]{1,0:T(8,128)(2,1)} %bitcast.11), channel_id=1, source_target_pairs={{0,12},{4,0},{8,4},{12,8},{1,13},{5,1},{9,5},{13,9},{2,14},{6,2},{... | collective-permute-start | bytes 589832 | tf_op jit(solution)/shard_map/ppermute | solution.py:192
  5.9 1.6 %collective-permute-start = (bf16[960,384]{1,0:T(8,128)(2,1)}, bf16[960,384]{1,0:T(8,128)(2,1)S(1)}, u32[]{:S(2)}, u32[]{:S(2)}) collective-permute-start(bf16[960,384]{1,0:T(8,128)(2,1)} %bitcast.14), channel_id=1, source_target_pairs={{0,2},{1,3},{2,0},{3,1},{4,6},{5,7},{6,4},{7,5},{8,10},{9,11},{10,... | collective-permute-start | bytes 2211848 | tf_op jit(solution)/shard_map/ppermute | solution.py:196
  7.6 1.3 %shard_map.102.taps = bf16[384,1920]{1,0:T(8,128)(2,1)S(1)} custom-call(bf16[960,384]{1,0:T(8,128)(2,1)} %bitcast.15, bf16[960,384]{1,0:T(8,128)(2,1)S(1)} %collective-permute-done.2.w1), custom_call_target="tpu_custom_call" | custom-call | flops 16777216 | bytes 65536 | tf_op jit(solution)/shard_map/pallas_call | solution.py:465
  8.9 3.0 %collective-permute-done.1.fa = bf16[256,384]{1,0:T(8,128)(2,1)S(1)} collective-permute-done((bf16[256,384]{1,0:T(8,128)(2,1)}, bf16[256,384]{1,0:T(8,128)(2,1)S(1)}, u32[]{:S(2)}, u32[]{:S(2)}) %collective-permute-start.1) | collective-permute-done | bytes 196640 | tf_op jit(solution)/shard_map/ppermute | solution.py:192
  11.8 3.4 %collective-permute-done.3.fb = bf16[256,384]{1,0:T(8,128)(2,1)S(1)} collective-permute-done((bf16[256,384]{1,0:T(8,128)(2,1)}, bf16[256,384]{1,0:T(8,128)(2,1)S(1)}, u32[]{:S(2)}, u32[]{:S(2)}) %collective-permute-start.3) | collective-permute-done | bytes 196640 | tf_op jit(solution)/shard_map/ppermute | solution.py:192
  15.2 1.3 %collective-permute-start.4 = (bf16[256,384]{1,0:T(8,128)(2,1)S(1)}, bf16[256,384]{1,0:T(8,128)(2,1)S(1)}, u32[]{:S(2)}, u32[]{:S(2)}) collective-permute-start(bf16[256,384]{1,0:T(8,128)(2,1)S(1)} %collective-permute-done.1.fa), channel_id=1, source_target_pairs={{0,4},{4,8},{8,12},{12,0},{1,5},{5,9},{9,13},{13,1},{2,6},{6,10},{... | collective-permute-start | bytes 589832 | tf_op jit(solution)/shard_map/ppermute | solution.py:192
  16.5 2.7 %shard_map.103 = (bf16[512,2304]{1,0:T(8,128)(2,1)S(1)}, bf16[512,384]{1,0:T(8,128)(2,1)S(1)}) custom-call(bf16[256,384]{1,0:T(8,128)(2,1)S(1)} %bitcast.12, bf16[256,384]{1,0:T(8,128)(2,1)S(1)} %collective-permute-done.1.fa, bf16[256,384]{1,0:T(8,128)(2,1)S(1)} %collective-permute-done.3.fb, bf16[384,1920]{1,0:T(8,128)(2,1)S(1)} %shard_map.102.taps, ...), custom_call_target="tpu_custom_call" | custom-call | flops 8589934592 | bytes 65536 | tf_op jit(solution)/shard_map/pallas_call | solution.py:465
  19.2 1.0 %collective-permute-done.5.ca = bf16[128,768]{1,0:T(8,128)(2,1)S(1)} collective-permute-done((bf16[128,768]{1,0:T(8,128)(2,1)}, bf16[128,768]{1,0:T(8,128)(2,1)S(1)}, u32[]{:S(2)}, u32[]{:S(2)}) %collective-permute-start.5) | collective-permute-done | bytes 196640 | tf_op jit(solution)/shard_map/ppermute | solution.py:192
  20.3 3.8 %collective-permute-start.6 = (bf16[128,768]{1,0:T(8,128)(2,1)S(1)}, bf16[128,768]{1,0:T(8,128)(2,1)S(1)}, u32[]{:S(2)}, u32[]{:S(2)}) collective-permute-start(bf16[128,768]{1,0:T(8,128)(2,1)S(1)} %bitcast.7), channel_id=1, source_target_pairs={{0,12},{4,0},{8,4},{12,8},{1,13},{5,1},{9,5},{13,9},{2,14},{6,2},{... | collective-permute-start | bytes 589832 | tf_op jit(solution)/shard_map/ppermute | solution.py:192
  24.7 2.8 %shard_map.105 = (bf16[512,2304]{1,0:T(8,128)(2,1)S(1)}, bf16[512,384]{1,0:T(8,128)(2,1)S(1)}, bf16[512,192]{1,0:T(8,128)(2,1)S(1)}) custom-call(bf16[256,384]{1,0:T(8,128)(2,1)S(1)} %collective-permute-done.1.fa, bf16[256,384]{1,0:T(8,128)(2,1)S(1)} %collective-permute-done.3.fb, bf16[256,384]{1,0:T(8,128)(2,1)S(1)} %collective-permute-done.4.fc, ...), custom_call_target="tpu_custom_call" | custom-call | flops 8589934592 | bytes 65536 | tf_op jit(solution)/shard_map/pallas_call | solution.py:465
  27.5 3.8 %shard_map.106 = (bf16[2,512,384]{2,1,0:T(8,128)(2,1)S(1)}, bf16[512,768]{1,0:T(8,128)(2,1)}, bf16[512,1280]{1,0:T(8,128)(2,1)S(1)}, bf16[192,512]{1,0:T(8,128)(2,1)S(1)}) custom-call(bf16[512,2304]{1,0:T(8,128)(2,1)S(1)} %get-tuple-element.53.windows, bf16[512,384]{1,0:T(8,128)(2,1)S(1)} %get-tuple-element.54.hid_near, ...), custom_call_target="tpu_custom_call" | custom-call | flops 16777216 | bytes 65536 | tf_op jit(solution)/shard_map/pallas_call | solution.py:465
  31.3 2.7 %shard_map.107 = (bf16[4,512,512]{2,1,0:T(8,128)(2,1)S(1)}, bf16[768,512]{1,0:T(8,128)(2,1)S(1)}) custom-call(bf16[512,1280]{1,0:T(8,128)(2,1)S(1)} %get-tuple-element.57.proj), custom_call_target="tpu_custom_call" | custom-call | flops 536870912 | bytes 65536 | tf_op jit(solution)/shard_map/pallas_call | solution.py:465
  34.0 2.1 %shard_map.108 = (bf16[512,768]{1,0:T(8,128)(2,1)S(1)}, bf16[192,768]{1,0:T(8,128)(2,1)S(1)}, bf16[192,768]{1,0:T(8,128)(2,1)S(1)}, f32[192,128]{1,0:T(8,128)S(1)}) custom-call(bf16[2,128,768]{2,1,0:T(8,128)(2,1)S(1)} %shard_map.104.early, bf16[128,768]{1,0:T(8,128)(2,1)S(1)} %bitcast.9, bf16[128,768]{1,0:T(8,128)(2,1)S(1)} %collective-permute-done.5.ca, ...), custom_call_target="tpu_custom_call" | custom-call | flops 2147483648 | bytes 65536 | tf_op jit(solution)/shard_map/pallas_call | solution.py:465
  36.6 1.6 %shard_map.109 = (bf16[128,512]{1,0:T(8,128)(2,1)S(1)}, bf16[512,128]{1,0:T(8,128)(2,1)S(1)}) custom-call(bf16[512,768]{1,0:T(8,128)(2,1)S(1)} %get-tuple-element.62.grad, bf16[512,1280]{1,0:T(8,128)(2,1)S(1)} %get-tuple-element.57.proj, bf16[4,512,512]{2,1,0:T(8,128)(2,1)S(1)} %get-tuple-element.58.probs_t), custom_call_target="tpu_custom_call" | custom-call | flops 8589934592 | bytes 65536 | tf_op jit(solution)/shard_map/pallas_call | solution.py:465
  38.3 1.7 %collective-permute-start.10 = (bf16[192,768]{1,0:T(8,128)(2,1)S(1)}, bf16[192,768]{1,0:T(8,128)(2,1)S(1)}, u32[]{:S(2)}, u32[]{:S(2)}) collective-permute-start(bf16[192,768]{1,0:T(8,128)(2,1)S(1)} %add_convert_fusion.1), channel_id=1, source_target_pairs={{0,2},{1,3},{2,0},{3,1},{4,6},{5,7},{6,4},{7,5},{8,10},{9,11},{10,... | collective-permute-start | bytes 884744 | tf_op jit(solution)/shard_map/ppermute | solution.py:196
  40.0 1.8 %shard_map.111 = (f32[208,256]{1,0:T(8,128)S(1)}, bf16[96,256]{1,0:T(8,128)(2,1)S(1)}, bf16[112,256]{1,0:T(8,128)(2,1)S(1)}) custom-call(bf16[512,768]{1,0:T(8,128)(2,1)S(1)} %get-tuple-element.62.grad, bf16[512,1280]{1,0:T(8,128)(2,1)S(1)} %get-tuple-element.57.proj, bf16[4,512,512]{2,1,0:T(8,128)(2,1)S(1)} %get-tuple-element.58.probs_t, ...), custom_call_target="tpu_custom_call" | custom-call | flops 65536 | bytes 65536 | tf_op jit(solution)/shard_map/pallas_call | solution.py:465
  41.9 0.5 collective-permute-start.12
  42.4 1.3 %shard_map.110 = f32[128,768]{1,0:T(8,128)} custom-call(bf16[2,512,384]{2,1,0:T(8,128)(2,1)S(1)} %get-tuple-element.65.hid, bf16[768,512]{1,0:T(8,128)(2,1)S(1)} %get-tuple-element.59.att_t, bf16[768,768]{1,0:T(8,128)(2,1)S(1)} %copy-done.1), custom_call_target="tpu_custom_call" | custom-call | flops 8589934592 | bytes 65536 | tf_op jit(solution)/shard_map/pallas_call | solution.py:465
  44.1 4.1 %collective-permute-done.10 = bf16[192,768]{1,0:T(8,128)(2,1)S(1)} collective-permute-done((bf16[192,768]{1,0:T(8,128)(2,1)S(1)}, bf16[192,768]{1,0:T(8,128)(2,1)S(1)}, u32[]{:S(2)}, u32[]{:S(2)}) %collective-permute-start.10) | collective-permute-done | bytes 294944 | tf_op jit(solution)/shard_map/ppermute | solution.py:196
  48.4 1.3 %collective-permute-done.14 = bf16[208,256]{1,0:T(8,128)(2,1)S(1)} collective-permute-done((bf16[208,256]{1,0:T(8,128)(2,1)S(1)}, bf16[208,256]{1,0:T(8,128)(2,1)S(1)}, u32[]{:S(2)}, u32[]{:S(2)}) %collective-permute-start.14) | collective-permute-done | bytes 106528 | tf_op jit(solution)/shard_map/ppermute | solution.py:196
  50.0 0.9 %shard_map.113 = f32[192,768]{1,0:T(8,128)} custom-call(bf16[192,768]{1,0:T(8,128)(2,1)S(1)} %add_convert_fusion.whole_v, bf16[192,768]{1,0:T(8,128)(2,1)S(1)} %collective-permute-done.11.other_v), custom_call_target="tpu_custom_call" | custom-call | flops 8589934592 | bytes 65536 | tf_op jit(solution)/shard_map/pallas_call | solution.py:465
  51.1 1.0 %shard_map.112 = (f32[192,1280]{1,0:T(8,128)}, f32[192]{0:T(256)}) custom-call(bf16[192,768]{1,0:T(8,128)(2,1)S(1)} %add_convert_fusion.whole_v, bf16[192,768]{1,0:T(8,128)(2,1)S(1)} %collective-permute-done.11.other_v, bf16[208,256]{1,0:T(8,128)(2,1)S(1)} %add_convert_fusion.2.whole_k, bf16[208,256]{1,0:T(8,128)(2,1)S(1)} %collective-permute-done.15.other_k), custom_call_target="tpu_custom_call" | custom-call | flops 65536 | bytes 65536 | tf_op jit(solution)/shard_map/pallas_call | solution.py:465
  (36 shorter events, 2.4 us)
Async XLA Ops:
  0.6 15.9 %copy-start.5 = (bf16[1,256,384]{2,1,0:T(8,128)(2,1)S(1)}, bf16[1,256,384]{2,1,0:T(8,128)(2,1)}, u32[]{:S(2)}) copy-start(bf16[1,256,384]{2,1,0:T(8,128)(2,1)} %param.7) | copy-start | bytes 589828
  0.6 15.9 %copy-start.4 = (f32[768]{0:T(1024)S(1)}, f32[768]{0:T(1024)}, u32[]{:S(2)}) copy-start(f32[768]{0:T(1024)} %bias.5) | copy-start | bytes 9220
  0.7 6.9 %collective-permute-start.2 = (bf16[960,384]{1,0:T(8,128)(2,1)}, bf16[960,384]{1,0:T(8,128)(2,1)S(1)}, u32[]{:S(2)}, u32[]{:S(2)}) collective-permute-start(bf16[960,384]{1,0:T(8,128)(2,1)} %bitcast.13), channel_id=1, source_target_pairs={{0,1},{1,0},{2,3},{3,2},{4,5},{5,4},{6,7},{7,6},{8,9},{9,8},{10,11... | collective-permute-start | bytes 2211848 | tf_op jit(solution)/shard_map/ppermute | solution.py:196
  1.2 10.7 %collective-permute-start.1 = (bf16[256,384]{1,0:T(8,128)(2,1)}, bf16[256,384]{1,0:T(8,128)(2,1)S(1)}, u32[]{:S(2)}, u32[]{:S(2)}) collective-permute-start(bf16[256,384]{1,0:T(8,128)(2,1)} %bitcast.10), channel_id=1, source_target_pairs={{0,4},{4,8},{8,12},{12,0},{1,5},{5,9},{9,13},{13,1},{2,6},{6,10},{... | collective-permute-start | bytes 589832 | tf_op jit(solution)/shard_map/ppermute | solution.py:192
  3.8 11.4 %collective-permute-start.3 = (bf16[256,384]{1,0:T(8,128)(2,1)}, bf16[256,384]{1,0:T(8,128)(2,1)S(1)}, u32[]{:S(2)}, u32[]{:S(2)}) collective-permute-start(bf16[256,384]{1,0:T(8,128)(2,1)} %bitcast.11), channel_id=1, source_target_pairs={{0,12},{4,0},{8,4},{12,8},{1,13},{5,1},{9,5},{13,9},{2,14},{6,2},{... | collective-permute-start | bytes 589832 | tf_op jit(solution)/shard_map/ppermute | solution.py:192
  5.9 18.7 %collective-permute-start = (bf16[960,384]{1,0:T(8,128)(2,1)}, bf16[960,384]{1,0:T(8,128)(2,1)S(1)}, u32[]{:S(2)}, u32[]{:S(2)}) collective-permute-start(bf16[960,384]{1,0:T(8,128)(2,1)} %bitcast.14), channel_id=1, source_target_pairs={{0,2},{1,3},{2,0},{3,1},{4,6},{5,7},{6,4},{7,5},{8,10},{9,11},{10,... | collective-permute-start | bytes 2211848 | tf_op jit(solution)/shard_map/ppermute | solution.py:196
  7.5 12.7 %collective-permute-start.5 = (bf16[128,768]{1,0:T(8,128)(2,1)}, bf16[128,768]{1,0:T(8,128)(2,1)S(1)}, u32[]{:S(2)}, u32[]{:S(2)}) collective-permute-start(bf16[128,768]{1,0:T(8,128)(2,1)} %bitcast.6), channel_id=1, source_target_pairs={{0,4},{4,8},{8,12},{12,0},{1,5},{5,9},{9,13},{13,1},{2,6},{6,10},{... | collective-permute-start | bytes 589832 | tf_op jit(solution)/shard_map/ppermute | solution.py:192
  8.8 11.4 %copy-start.2 = (bf16[1,128,768]{2,1,0:T(8,128)(2,1)S(1)}, bf16[1,128,768]{2,1,0:T(8,128)(2,1)}, u32[]{:S(2)}) copy-start(bf16[1,128,768]{2,1,0:T(8,128)(2,1)} %param.13) | copy-start | bytes 589828
  8.9 15.2 %copy-start.1 = (bf16[768,768]{1,0:T(8,128)(2,1)S(1)}, bf16[768,768]{1,0:T(8,128)(2,1)}, u32[]{:S(2)}) copy-start(bf16[768,768]{1,0:T(8,128)(2,1)} %ow.5) | copy-start | bytes 3538948
  15.2 9.4 %collective-permute-start.4 = (bf16[256,384]{1,0:T(8,128)(2,1)S(1)}, bf16[256,384]{1,0:T(8,128)(2,1)S(1)}, u32[]{:S(2)}, u32[]{:S(2)}) collective-permute-start(bf16[256,384]{1,0:T(8,128)(2,1)S(1)} %collective-permute-done.1.fa), channel_id=1, source_target_pairs={{0,4},{4,8},{8,12},{12,0},{1,5},{5,9},{9,13},{13,1},{2,6},{6,10},{... | collective-permute-start | bytes 589832 | tf_op jit(solution)/shard_map/ppermute | solution.py:192
  20.3 13.7 %collective-permute-start.7 = (bf16[128,768]{1,0:T(8,128)(2,1)S(1)}, bf16[128,768]{1,0:T(8,128)(2,1)S(1)}, u32[]{:S(2)}, u32[]{:S(2)}) collective-permute-start(bf16[128,768]{1,0:T(8,128)(2,1)S(1)} %collective-permute-done.5.ca), channel_id=1, source_target_pairs={{0,4},{4,8},{8,12},{12,0},{1,5},{5,9},{9,13},{13,1},{2,6},{6,10},{... | collective-permute-start | bytes 589832 | tf_op jit(solution)/shard_map/ppermute | solution.py:192
  20.3 13.7 %collective-permute-start.6 = (bf16[128,768]{1,0:T(8,128)(2,1)S(1)}, bf16[128,768]{1,0:T(8,128)(2,1)S(1)}, u32[]{:S(2)}, u32[]{:S(2)}) collective-permute-start(bf16[128,768]{1,0:T(8,128)(2,1)S(1)} %bitcast.7), channel_id=1, source_target_pairs={{0,12},{4,0},{8,4},{12,8},{1,13},{5,1},{9,5},{13,9},{2,14},{6,2},{... | collective-permute-start | bytes 589832 | tf_op jit(solution)/shard_map/ppermute | solution.py:192
  24.6 2.9 %collective-permute-start.8 = (bf16[960,384]{1,0:T(8,128)(2,1)S(1)}, bf16[960,384]{1,0:T(8,128)(2,1)S(1)}, u32[]{:S(2)}, u32[]{:S(2)}) collective-permute-start(bf16[960,384]{1,0:T(8,128)(2,1)S(1)} %collective-permute-done.w2), channel_id=1, source_target_pairs={{0,1},{1,0},{2,3},{3,2},{4,5},{5,4},{6,7},{7,6},{8,9},{9,8},{10,11... | collective-permute-start | bytes 2211848 | tf_op jit(solution)/shard_map/ppermute | solution.py:196
  24.7 2.8 %copy-start = (bf16[768,1280]{1,0:T(8,128)(2,1)S(1)}, bf16[768,1280]{1,0:T(8,128)(2,1)}, u32[]{:S(2)}) copy-start(bf16[768,1280]{1,0:T(8,128)(2,1)} %aw.5) | copy-start | bytes 5898244
  24.7 2.8 %copy-start.3 = (f32[768]{0:T(1024)S(1)}, f32[768]{0:T(1024)}, u32[]{:S(2)}) copy-start(f32[768]{0:T(1024)} %gain.3) | copy-start | bytes 9220
  36.1 2.1 %collective-permute-start.9 = (bf16[192,768]{1,0:T(8,128)(2,1)S(1)}, bf16[192,768]{1,0:T(8,128)(2,1)S(1)}, u32[]{:S(2)}, u32[]{:S(2)}) collective-permute-start(bf16[192,768]{1,0:T(8,128)(2,1)S(1)} %get-tuple-element.61), channel_id=1, source_target_pairs={{0,1},{1,0},{2,3},{3,2},{4,5},{5,4},{6,7},{7,6},{8,9},{9,8},{10,11... | collective-permute-start | bytes 884744 | tf_op jit(solution)/shard_map/ppermute | solution.py:196
  38.3 9.9 %collective-permute-start.10 = (bf16[192,768]{1,0:T(8,128)(2,1)S(1)}, bf16[192,768]{1,0:T(8,128)(2,1)S(1)}, u32[]{:S(2)}, u32[]{:S(2)}) collective-permute-start(bf16[192,768]{1,0:T(8,128)(2,1)S(1)} %add_convert_fusion.1), channel_id=1, source_target_pairs={{0,2},{1,3},{2,0},{3,1},{4,6},{5,7},{6,4},{7,5},{8,10},{9,11},{10,... | collective-permute-start | bytes 884744 | tf_op jit(solution)/shard_map/ppermute | solution.py:196
  41.8 1.8 %collective-permute-start.13 = (bf16[112,256]{1,0:T(8,128)(2,1)S(1)}, bf16[112,256]{1,0:T(8,128)(2,1)S(1)}, u32[]{:S(2)}, u32[]{:S(2)}) collective-permute-start(bf16[112,256]{1,0:T(8,128)(2,1)S(1)} %get-tuple-element.73), channel_id=1, source_target_pairs={{0,1},{1,0},{2,3},{3,2},{4,5},{5,4},{6,7},{7,6},{8,9},{9,8},{10,11... | collective-permute-start | bytes 172040 | tf_op jit(solution)/shard_map/ppermute | solution.py:196
  41.9 1.8 %collective-permute-start.12 = (bf16[96,256]{1,0:T(8,128)(2,1)S(1)}, bf16[96,256]{1,0:T(8,128)(2,1)S(1)}, u32[]{:S(2)}, u32[]{:S(2)}) collective-permute-start(bf16[96,256]{1,0:T(8,128)(2,1)S(1)} %get-tuple-element.72), channel_id=1, source_target_pairs={{0,1},{1,0},{2,3},{3,2},{4,5},{5,4},{6,7},{7,6},{8,9},{9,8},{10,11... | collective-permute-start | bytes 147464 | tf_op jit(solution)/shard_map/ppermute | solution.py:196
  43.7 6.0 %collective-permute-start.14 = (bf16[208,256]{1,0:T(8,128)(2,1)S(1)}, bf16[208,256]{1,0:T(8,128)(2,1)S(1)}, u32[]{:S(2)}, u32[]{:S(2)}) collective-permute-start(bf16[208,256]{1,0:T(8,128)(2,1)S(1)} %add_convert_fusion.3), channel_id=1, source_target_pairs={{0,2},{1,3},{2,0},{3,1},{4,6},{5,7},{6,4},{7,5},{8,10},{9,11},{10,... | collective-permute-start | bytes 319496 | tf_op jit(solution)/shard_map/ppermute | solution.py:196
  48.3 1.6 %collective-permute-start.11 = (bf16[192,768]{1,0:T(8,128)(2,1)S(1)}, bf16[192,768]{1,0:T(8,128)(2,1)S(1)}, u32[]{:S(2)}, u32[]{:S(2)}) collective-permute-start(bf16[192,768]{1,0:T(8,128)(2,1)S(1)} %add_convert_fusion.whole_v), channel_id=1, source_target_pairs={{0,1},{1,0},{2,3},{3,2},{4,5},{5,4},{6,7},{7,6},{8,9},{9,8},{10,11... | collective-permute-start | bytes 884744 | tf_op jit(solution)/shard_map/ppermute | solution.py:196
  49.7 1.4 %collective-permute-start.15 = (bf16[208,256]{1,0:T(8,128)(2,1)S(1)}, bf16[208,256]{1,0:T(8,128)(2,1)S(1)}, u32[]{:S(2)}, u32[]{:S(2)}) collective-permute-start(bf16[208,256]{1,0:T(8,128)(2,1)S(1)} %add_convert_fusion.2.whole_k), channel_id=1, source_target_pairs={{0,1},{1,0},{2,3},{3,2},{4,5},{5,4},{6,7},{7,6},{8,9},{9,8},{10,11... | collective-permute-start | bytes 319496 | tf_op jit(solution)/shard_map/ppermute | solution.py:196

commit v8 on v6

--- a/solution.py
+++ b/solution.py
@@ -166,6 +166,7 @@
 SEQ, DP = 4, 4
 TOK = 128
 EDGE = 16
+REACH = 80
 LEN = SEQ * TOK
 CIN, WIDTH = 384, 768
 SHARD = WIDTH // DP
@@ -248,6 +249,14 @@
                 positions[g, pl.ds(start, chunk), :] = ref[:, g * 128 : (g + 1) * 128].astype(F32)
 
 
+def fill_edges(positions, z, parts):
+    for g in range(CIN // 128):
+        for ref, off, row in parts:
+            start = pl.multiple_of(lax.rem(z + off, SEQ) * 2 * TOK + (8 + row), 8)
+            piece = ref[row : row + REACH, g * 128 : (g + 1) * 128]
+            positions[g, pl.ds(start, REACH), :] = piece.astype(F32)
+
+
 def near_kernel(f0, fa, fb, taps, bias, windows, hid, positions):
     z, d = lax.axis_index("seq"), lax.axis_index("dp")
     fill_positions(positions, z, ((f0, 0), (fa, 3), (fb, 1), (None, 2)))
@@ -268,7 +277,8 @@
     fa, fb, fc, windows_in, hid_in, taps, w2, bias, windows, hid, hid_two, positions, two
 ):
     z, d = lax.axis_index("seq"), lax.axis_index("dp")
-    fill_positions(positions, z, ((fa, 3), (fb, 1), (fc, 2)))
+    fill_positions(positions, z, ((fc, 2),))
+    fill_edges(positions, z, ((fa, 3, 0), (fb, 1, 2 * TOK - REACH)))
     windows[...] = windows_in[...]
     hid[...] = hid_in[...]
     first = jnp.clip(lax.rem(z + 2, SEQ) * TOK - EDGE, 0, LEN - TOK - 2 * EDGE)

time: 52.2 us -> 52.1 us (level)
  no operation moved by 1% of the time
where the time goes in v8:
time: 52.1 us; the launch traced here: 52 us
  Pallas kernels  22.2 us (43%)
  starting transfers between devices  15.5 us (30%)
  waiting for transfers between devices  13.2 us (25%)
  between operations  0.84 us (2%)
    pallas_call x12, Pallas kernels, kernel_call(): pl.pallas_call(body, in_specs=[away if i in far else whole for i in range...  22.2 us
    ppermute x6, starting transfers between devices, ring(): lax.ppermute(value, 'seq', [(i, (i + step) % SEQ) for i in range(SEQ)])  9.9 us
    ppermute x6, waiting for transfers between devices, ring(): lax.ppermute(value, 'seq', [(i, (i + step) % SEQ) for i in range(SEQ)])  7.38 us
    ppermute x10, waiting for transfers between devices, swap(): return lax.ppermute(value, 'dp', [(i, i ^ bit) for i in range(DP)])  5.81 us
    ppermute x10, starting transfers between devices, swap(): return lax.ppermute(value, 'dp', [(i, i ^ bit) for i in range(DP)])  5.58 us
  transfers between devices with their start and end apart: 16, of which 7 were waited for; matrix products, arithmetic and copies ran while one was open for 0% of the time, Pallas kernels for 37%

profile of v8, /device:TPU:0, one launch (start us, length us, event | category | flops | bytes accessed | tf_op | source)
XLA Modules:
  0.0 52.0 jit_solution(10717744242265933528)
XLA Ops:
  0.7 0.5 collective-permute-start.2
  1.2 2.6 %collective-permute-start.1 = (bf16[256,384]{1,0:T(8,128)(2,1)}, bf16[256,384]{1,0:T(8,128)(2,1)S(1)}, u32[]{:S(2)}, u32[]{:S(2)}) collective-permute-start(bf16[256,384]{1,0:T(8,128)(2,1)} %bitcast.10), channel_id=1, source_target_pairs={{0,4},{4,8},{8,12},{12,0},{1,5},{5,9},{9,13},{13,1},{2,6},{6,10},{... | collective-permute-start | bytes 589832 | tf_op jit(solution)/shard_map/ppermute | solution.py:193
  3.8 2.1 %collective-permute-start.3 = (bf16[256,384]{1,0:T(8,128)(2,1)}, bf16[256,384]{1,0:T(8,128)(2,1)S(1)}, u32[]{:S(2)}, u32[]{:S(2)}) collective-permute-start(bf16[256,384]{1,0:T(8,128)(2,1)} %bitcast.11), channel_id=1, source_target_pairs={{0,12},{4,0},{8,4},{12,8},{1,13},{5,1},{9,5},{13,9},{2,14},{6,2},{... | collective-permute-start | bytes 589832 | tf_op jit(solution)/shard_map/ppermute | solution.py:193
  5.9 1.6 %collective-permute-start = (bf16[960,384]{1,0:T(8,128)(2,1)}, bf16[960,384]{1,0:T(8,128)(2,1)S(1)}, u32[]{:S(2)}, u32[]{:S(2)}) collective-permute-start(bf16[960,384]{1,0:T(8,128)(2,1)} %bitcast.14), channel_id=1, source_target_pairs={{0,2},{1,3},{2,0},{3,1},{4,6},{5,7},{6,4},{7,5},{8,10},{9,11},{10,... | collective-permute-start | bytes 2211848 | tf_op jit(solution)/shard_map/ppermute | solution.py:197
  7.6 1.3 %shard_map.102.taps = bf16[384,1920]{1,0:T(8,128)(2,1)S(1)} custom-call(bf16[960,384]{1,0:T(8,128)(2,1)} %bitcast.15, bf16[960,384]{1,0:T(8,128)(2,1)S(1)} %collective-permute-done.2.w1), custom_call_target="tpu_custom_call" | custom-call | flops 16777216 | bytes 65536 | tf_op jit(solution)/shard_map/pallas_call | solution.py:475
  8.9 3.0 %collective-permute-done.1.fa = bf16[256,384]{1,0:T(8,128)(2,1)S(1)} collective-permute-done((bf16[256,384]{1,0:T(8,128)(2,1)}, bf16[256,384]{1,0:T(8,128)(2,1)S(1)}, u32[]{:S(2)}, u32[]{:S(2)}) %collective-permute-start.1) | collective-permute-done | bytes 196640 | tf_op jit(solution)/shard_map/ppermute | solution.py:193
  11.8 3.4 %collective-permute-done.3.fb = bf16[256,384]{1,0:T(8,128)(2,1)S(1)} collective-permute-done((bf16[256,384]{1,0:T(8,128)(2,1)}, bf16[256,384]{1,0:T(8,128)(2,1)S(1)}, u32[]{:S(2)}, u32[]{:S(2)}) %collective-permute-start.3) | collective-permute-done | bytes 196640 | tf_op jit(solution)/shard_map/ppermute | solution.py:193
  15.2 1.3 %collective-permute-start.4 = (bf16[256,384]{1,0:T(8,128)(2,1)S(1)}, bf16[256,384]{1,0:T(8,128)(2,1)S(1)}, u32[]{:S(2)}, u32[]{:S(2)}) collective-permute-start(bf16[256,384]{1,0:T(8,128)(2,1)S(1)} %collective-permute-done.1.fa), channel_id=1, source_target_pairs={{0,4},{4,8},{8,12},{12,0},{1,5},{5,9},{9,13},{13,1},{2,6},{6,10},{... | collective-permute-start | bytes 589832 | tf_op jit(solution)/shard_map/ppermute | solution.py:193
  16.5 2.7 %shard_map.103 = (bf16[512,2304]{1,0:T(8,128)(2,1)S(1)}, bf16[512,384]{1,0:T(8,128)(2,1)S(1)}) custom-call(bf16[256,384]{1,0:T(8,128)(2,1)S(1)} %bitcast.12, bf16[256,384]{1,0:T(8,128)(2,1)S(1)} %collective-permute-done.1.fa, bf16[256,384]{1,0:T(8,128)(2,1)S(1)} %collective-permute-done.3.fb, bf16[384,1920]{1,0:T(8,128)(2,1)S(1)} %shard_map.102.taps, ...), custom_call_target="tpu_custom_call" | custom-call | flops 8589934592 | bytes 65536 | tf_op jit(solution)/shard_map/pallas_call | solution.py:475
  19.2 1.0 %collective-permute-done.5.ca = bf16[128,768]{1,0:T(8,128)(2,1)S(1)} collective-permute-done((bf16[128,768]{1,0:T(8,128)(2,1)}, bf16[128,768]{1,0:T(8,128)(2,1)S(1)}, u32[]{:S(2)}, u32[]{:S(2)}) %collective-permute-start.5) | collective-permute-done | bytes 196640 | tf_op jit(solution)/shard_map/ppermute | solution.py:193
  20.3 3.8 %collective-permute-start.6 = (bf16[128,768]{1,0:T(8,128)(2,1)S(1)}, bf16[128,768]{1,0:T(8,128)(2,1)S(1)}, u32[]{:S(2)}, u32[]{:S(2)}) collective-permute-start(bf16[128,768]{1,0:T(8,128)(2,1)S(1)} %bitcast.7), channel_id=1, source_target_pairs={{0,12},{4,0},{8,4},{12,8},{1,13},{5,1},{9,5},{13,9},{2,14},{6,2},{... | collective-permute-start | bytes 589832 | tf_op jit(solution)/shard_map/ppermute | solution.py:193
  24.7 2.7 %shard_map.105 = (bf16[512,2304]{1,0:T(8,128)(2,1)S(1)}, bf16[512,384]{1,0:T(8,128)(2,1)S(1)}, bf16[512,192]{1,0:T(8,128)(2,1)S(1)}) custom-call(bf16[256,384]{1,0:T(8,128)(2,1)S(1)} %collective-permute-done.1.fa, bf16[256,384]{1,0:T(8,128)(2,1)S(1)} %collective-permute-done.3.fb, bf16[256,384]{1,0:T(8,128)(2,1)S(1)} %collective-permute-done.4.fc, ...), custom_call_target="tpu_custom_call" | custom-call | flops 8589934592 | bytes 65536 | tf_op jit(solution)/shard_map/pallas_call | solution.py:475
  27.5 3.8 %shard_map.106 = (bf16[2,512,384]{2,1,0:T(8,128)(2,1)S(1)}, bf16[512,768]{1,0:T(8,128)(2,1)}, bf16[512,1280]{1,0:T(8,128)(2,1)S(1)}, bf16[192,512]{1,0:T(8,128)(2,1)S(1)}) custom-call(bf16[512,2304]{1,0:T(8,128)(2,1)S(1)} %get-tuple-element.53.windows, bf16[512,384]{1,0:T(8,128)(2,1)S(1)} %get-tuple-element.54.hid_near, ...), custom_call_target="tpu_custom_call" | custom-call | flops 16777216 | bytes 65536 | tf_op jit(solution)/shard_map/pallas_call | solution.py:475
  31.2 2.6 %shard_map.107 = (bf16[4,512,512]{2,1,0:T(8,128)(2,1)S(1)}, bf16[768,512]{1,0:T(8,128)(2,1)S(1)}) custom-call(bf16[512,1280]{1,0:T(8,128)(2,1)S(1)} %get-tuple-element.57.proj), custom_call_target="tpu_custom_call" | custom-call | flops 536870912 | bytes 65536 | tf_op jit(solution)/shard_map/pallas_call | solution.py:475
  33.9 2.1 %shard_map.108 = (bf16[512,768]{1,0:T(8,128)(2,1)S(1)}, f32[192,768]{1,0:T(8,128)S(1)}, bf16[192,768]{1,0:T(8,128)(2,1)S(1)}, f32[192,128]{1,0:T(8,128)S(1)}) custom-call(bf16[2,128,768]{2,1,0:T(8,128)(2,1)S(1)} %shard_map.104.early, bf16[128,768]{1,0:T(8,128)(2,1)S(1)} %bitcast.9, bf16[128,768]{1,0:T(8,128)(2,1)S(1)} %collective-permute-done.5.ca, ...), custom_call_target="tpu_custom_call" | custom-call | flops 2147483648 | bytes 65536 | tf_op jit(solution)/shard_map/pallas_call | solution.py:475
  36.0 0.5 %collective-permute-start.9 = (bf16[192,768]{1,0:T(8,128)(2,1)S(1)}, bf16[192,768]{1,0:T(8,128)(2,1)S(1)}, u32[]{:S(2)}, u32[]{:S(2)}) collective-permute-start(bf16[192,768]{1,0:T(8,128)(2,1)S(1)} %get-tuple-element.61), channel_id=1, source_target_pairs={{0,1},{1,0},{2,3},{3,2},{4,5},{5,4},{6,7},{7,6},{8,9},{9,8},{10,11... | collective-permute-start | bytes 884744 | tf_op jit(solution)/shard_map/ppermute | solution.py:197
  36.6 1.6 %shard_map.109 = (bf16[128,512]{1,0:T(8,128)(2,1)S(1)}, bf16[512,128]{1,0:T(8,128)(2,1)S(1)}) custom-call(bf16[512,768]{1,0:T(8,128)(2,1)S(1)} %get-tuple-element.62.grad, bf16[512,1280]{1,0:T(8,128)(2,1)S(1)} %get-tuple-element.57.proj, bf16[4,512,512]{2,1,0:T(8,128)(2,1)S(1)} %get-tuple-element.58.probs_t), custom_call_target="tpu_custom_call" | custom-call | flops 8589934592 | bytes 65536 | tf_op jit(solution)/shard_map/pallas_call | solution.py:475
  38.2 1.7 %collective-permute-start.10 = (bf16[192,768]{1,0:T(8,128)(2,1)S(1)}, bf16[192,768]{1,0:T(8,128)(2,1)S(1)}, u32[]{:S(2)}, u32[]{:S(2)}) collective-permute-start(bf16[192,768]{1,0:T(8,128)(2,1)S(1)} %add_convert_fusion.1), channel_id=1, source_target_pairs={{0,2},{1,3},{2,0},{3,1},{4,6},{5,7},{6,4},{7,5},{8,10},{9,11},{10,... | collective-permute-start | bytes 884744 | tf_op jit(solution)/shard_map/ppermute | solution.py:197
  39.9 1.8 %shard_map.111 = (f32[208,256]{1,0:T(8,128)S(1)}, bf16[96,256]{1,0:T(8,128)(2,1)S(1)}, bf16[112,256]{1,0:T(8,128)(2,1)S(1)}) custom-call(bf16[512,768]{1,0:T(8,128)(2,1)S(1)} %get-tuple-element.62.grad, bf16[512,1280]{1,0:T(8,128)(2,1)S(1)} %get-tuple-element.57.proj, bf16[4,512,512]{2,1,0:T(8,128)(2,1)S(1)} %get-tuple-element.58.probs_t, ...), custom_call_target="tpu_custom_call" | custom-call | flops 65536 | bytes 65536 | tf_op jit(solution)/shard_map/pallas_call | solution.py:475
  42.3 1.3 %shard_map.110 = f32[128,768]{1,0:T(8,128)} custom-call(bf16[2,512,384]{2,1,0:T(8,128)(2,1)S(1)} %get-tuple-element.65.hid, bf16[768,512]{1,0:T(8,128)(2,1)S(1)} %get-tuple-element.59.att_t, bf16[768,768]{1,0:T(8,128)(2,1)S(1)} %copy-done.1), custom_call_target="tpu_custom_call" | custom-call | flops 8589934592 | bytes 65536 | tf_op jit(solution)/shard_map/pallas_call | solution.py:475
  44.1 4.1 %collective-permute-done.10 = bf16[192,768]{1,0:T(8,128)(2,1)S(1)} collective-permute-done((bf16[192,768]{1,0:T(8,128)(2,1)S(1)}, bf16[192,768]{1,0:T(8,128)(2,1)S(1)}, u32[]{:S(2)}, u32[]{:S(2)}) %collective-permute-start.10) | collective-permute-done | bytes 294944 | tf_op jit(solution)/shard_map/ppermute | solution.py:197
  48.3 1.2 %collective-permute-done.14 = bf16[208,256]{1,0:T(8,128)(2,1)S(1)} collective-permute-done((bf16[208,256]{1,0:T(8,128)(2,1)S(1)}, bf16[208,256]{1,0:T(8,128)(2,1)S(1)}, u32[]{:S(2)}, u32[]{:S(2)}) %collective-permute-start.14) | collective-permute-done | bytes 106528 | tf_op jit(solution)/shard_map/ppermute | solution.py:197
  49.9 0.9 %shard_map.113 = f32[192,768]{1,0:T(8,128)} custom-call(bf16[192,768]{1,0:T(8,128)(2,1)S(1)} %add_convert_fusion.whole_v, bf16[192,768]{1,0:T(8,128)(2,1)S(1)} %collective-permute-done.11.other_v), custom_call_target="tpu_custom_call" | custom-call | flops 8589934592 | bytes 65536 | tf_op jit(solution)/shard_map/pallas_call | solution.py:475
  50.9 1.0 %shard_map.112 = (f32[192,1280]{1,0:T(8,128)}, f32[192]{0:T(256)}) custom-call(bf16[192,768]{1,0:T(8,128)(2,1)S(1)} %add_convert_fusion.whole_v, bf16[192,768]{1,0:T(8,128)(2,1)S(1)} %collective-permute-done.11.other_v, bf16[208,256]{1,0:T(8,128)(2,1)S(1)} %add_convert_fusion.2.whole_k, bf16[208,256]{1,0:T(8,128)(2,1)S(1)} %collective-permute-done.15.other_k), custom_call_target="tpu_custom_call" | custom-call | flops 65536 | bytes 65536 | tf_op jit(solution)/shard_map/pallas_call | solution.py:475
  (36 shorter events, 2.4 us)
Async XLA Ops:
  0.6 15.9 %copy-start.5 = (bf16[1,256,384]{2,1,0:T(8,128)(2,1)S(1)}, bf16[1,256,384]{2,1,0:T(8,128)(2,1)}, u32[]{:S(2)}) copy-start(bf16[1,256,384]{2,1,0:T(8,128)(2,1)} %param.7) | copy-start | bytes 589828
  0.6 15.9 %copy-start.4 = (f32[768]{0:T(1024)S(1)}, f32[768]{0:T(1024)}, u32[]{:S(2)}) copy-start(f32[768]{0:T(1024)} %bias.5) | copy-start | bytes 9220
  0.7 6.9 %collective-permute-start.2 = (bf16[960,384]{1,0:T(8,128)(2,1)}, bf16[960,384]{1,0:T(8,128)(2,1)S(1)}, u32[]{:S(2)}, u32[]{:S(2)}) collective-permute-start(bf16[960,384]{1,0:T(8,128)(2,1)} %bitcast.13), channel_id=1, source_target_pairs={{0,1},{1,0},{2,3},{3,2},{4,5},{5,4},{6,7},{7,6},{8,9},{9,8},{10,11... | collective-permute-start | bytes 2211848 | tf_op jit(solution)/shard_map/ppermute | solution.py:197
  1.2 10.7 %collective-permute-start.1 = (bf16[256,384]{1,0:T(8,128)(2,1)}, bf16[256,384]{1,0:T(8,128)(2,1)S(1)}, u32[]{:S(2)}, u32[]{:S(2)}) collective-permute-start(bf16[256,384]{1,0:T(8,128)(2,1)} %bitcast.10), channel_id=1, source_target_pairs={{0,4},{4,8},{8,12},{12,0},{1,5},{5,9},{9,13},{13,1},{2,6},{6,10},{... | collective-permute-start | bytes 589832 | tf_op jit(solution)/shard_map/ppermute | solution.py:193
  3.8 11.4 %collective-permute-start.3 = (bf16[256,384]{1,0:T(8,128)(2,1)}, bf16[256,384]{1,0:T(8,128)(2,1)S(1)}, u32[]{:S(2)}, u32[]{:S(2)}) collective-permute-start(bf16[256,384]{1,0:T(8,128)(2,1)} %bitcast.11), channel_id=1, source_target_pairs={{0,12},{4,0},{8,4},{12,8},{1,13},{5,1},{9,5},{13,9},{2,14},{6,2},{... | collective-permute-start | bytes 589832 | tf_op jit(solution)/shard_map/ppermute | solution.py:193
  5.9 18.7 %collective-permute-start = (bf16[960,384]{1,0:T(8,128)(2,1)}, bf16[960,384]{1,0:T(8,128)(2,1)S(1)}, u32[]{:S(2)}, u32[]{:S(2)}) collective-permute-start(bf16[960,384]{1,0:T(8,128)(2,1)} %bitcast.14), channel_id=1, source_target_pairs={{0,2},{1,3},{2,0},{3,1},{4,6},{5,7},{6,4},{7,5},{8,10},{9,11},{10,... | collective-permute-start | bytes 2211848 | tf_op jit(solution)/shard_map/ppermute | solution.py:197
  7.5 12.7 %collective-permute-start.5 = (bf16[128,768]{1,0:T(8,128)(2,1)}, bf16[128,768]{1,0:T(8,128)(2,1)S(1)}, u32[]{:S(2)}, u32[]{:S(2)}) collective-permute-start(bf16[128,768]{1,0:T(8,128)(2,1)} %bitcast.6), channel_id=1, source_target_pairs={{0,4},{4,8},{8,12},{12,0},{1,5},{5,9},{9,13},{13,1},{2,6},{6,10},{... | collective-permute-start | bytes 589832 | tf_op jit(solution)/shard_map/ppermute | solution.py:193
  8.8 11.4 %copy-start.2 = (bf16[1,128,768]{2,1,0:T(8,128)(2,1)S(1)}, bf16[1,128,768]{2,1,0:T(8,128)(2,1)}, u32[]{:S(2)}) copy-start(bf16[1,128,768]{2,1,0:T(8,128)(2,1)} %param.13) | copy-start | bytes 589828
  8.9 15.2 %copy-start.1 = (bf16[768,768]{1,0:T(8,128)(2,1)S(1)}, bf16[768,768]{1,0:T(8,128)(2,1)}, u32[]{:S(2)}) copy-start(bf16[768,768]{1,0:T(8,128)(2,1)} %ow.5) | copy-start | bytes 3538948
  15.2 9.4 %collective-permute-start.4 = (bf16[256,384]{1,0:T(8,128)(2,1)S(1)}, bf16[256,384]{1,0:T(8,128)(2,1)S(1)}, u32[]{:S(2)}, u32[]{:S(2)}) collective-permute-start(bf16[256,384]{1,0:T(8,128)(2,1)S(1)} %collective-permute-done.1.fa), channel_id=1, source_target_pairs={{0,4},{4,8},{8,12},{12,0},{1,5},{5,9},{9,13},{13,1},{2,6},{6,10},{... | collective-permute-start | bytes 589832 | tf_op jit(solution)/shard_map/ppermute | solution.py:193
  20.3 13.6 %collective-permute-start.7 = (bf16[128,768]{1,0:T(8,128)(2,1)S(1)}, bf16[128,768]{1,0:T(8,128)(2,1)S(1)}, u32[]{:S(2)}, u32[]{:S(2)}) collective-permute-start(bf16[128,768]{1,0:T(8,128)(2,1)S(1)} %collective-permute-done.5.ca), channel_id=1, source_target_pairs={{0,4},{4,8},{8,12},{12,0},{1,5},{5,9},{9,13},{13,1},{2,6},{6,10},{... | collective-permute-start | bytes 589832 | tf_op jit(solution)/shard_map/ppermute | solution.py:193
  20.3 13.6 %collective-permute-start.6 = (bf16[128,768]{1,0:T(8,128)(2,1)S(1)}, bf16[128,768]{1,0:T(8,128)(2,1)S(1)}, u32[]{:S(2)}, u32[]{:S(2)}) collective-permute-start(bf16[128,768]{1,0:T(8,128)(2,1)S(1)} %bitcast.7), channel_id=1, source_target_pairs={{0,12},{4,0},{8,4},{12,8},{1,13},{5,1},{9,5},{13,9},{2,14},{6,2},{... | collective-permute-start | bytes 589832 | tf_op jit(solution)/shard_map/ppermute | solution.py:193
  24.6 2.8 %collective-permute-start.8 = (bf16[960,384]{1,0:T(8,128)(2,1)S(1)}, bf16[960,384]{1,0:T(8,128)(2,1)S(1)}, u32[]{:S(2)}, u32[]{:S(2)}) collective-permute-start(bf16[960,384]{1,0:T(8,128)(2,1)S(1)} %collective-permute-done.w2), channel_id=1, source_target_pairs={{0,1},{1,0},{2,3},{3,2},{4,5},{5,4},{6,7},{7,6},{8,9},{9,8},{10,11... | collective-permute-start | bytes 2211848 | tf_op jit(solution)/shard_map/ppermute | solution.py:197
  24.7 2.8 %copy-start = (bf16[768,1280]{1,0:T(8,128)(2,1)S(1)}, bf16[768,1280]{1,0:T(8,128)(2,1)}, u32[]{:S(2)}) copy-start(bf16[768,1280]{1,0:T(8,128)(2,1)} %aw.5) | copy-start | bytes 5898244
  24.7 2.8 %copy-start.3 = (f32[768]{0:T(1024)S(1)}, f32[768]{0:T(1024)}, u32[]{:S(2)}) copy-start(f32[768]{0:T(1024)} %gain.3) | copy-start | bytes 9220
  36.0 2.1 %collective-permute-start.9 = (bf16[192,768]{1,0:T(8,128)(2,1)S(1)}, bf16[192,768]{1,0:T(8,128)(2,1)S(1)}, u32[]{:S(2)}, u32[]{:S(2)}) collective-permute-start(bf16[192,768]{1,0:T(8,128)(2,1)S(1)} %get-tuple-element.61), channel_id=1, source_target_pairs={{0,1},{1,0},{2,3},{3,2},{4,5},{5,4},{6,7},{7,6},{8,9},{9,8},{10,11... | collective-permute-start | bytes 884744 | tf_op jit(solution)/shard_map/ppermute | solution.py:197
  38.2 9.9 %collective-permute-start.10 = (bf16[192,768]{1,0:T(8,128)(2,1)S(1)}, bf16[192,768]{1,0:T(8,128)(2,1)S(1)}, u32[]{:S(2)}, u32[]{:S(2)}) collective-permute-start(bf16[192,768]{1,0:T(8,128)(2,1)S(1)} %add_convert_fusion.1), channel_id=1, source_target_pairs={{0,2},{1,3},{2,0},{3,1},{4,6},{5,7},{6,4},{7,5},{8,10},{9,11},{10,... | collective-permute-start | bytes 884744 | tf_op jit(solution)/shard_map/ppermute | solution.py:197
  41.7 1.8 %collective-permute-start.13 = (bf16[112,256]{1,0:T(8,128)(2,1)S(1)}, bf16[112,256]{1,0:T(8,128)(2,1)S(1)}, u32[]{:S(2)}, u32[]{:S(2)}) collective-permute-start(bf16[112,256]{1,0:T(8,128)(2,1)S(1)} %get-tuple-element.73), channel_id=1, source_target_pairs={{0,1},{1,0},{2,3},{3,2},{4,5},{5,4},{6,7},{7,6},{8,9},{9,8},{10,11... | collective-permute-start | bytes 172040 | tf_op jit(solution)/shard_map/ppermute | solution.py:197
  41.8 1.8 %collective-permute-start.12 = (bf16[96,256]{1,0:T(8,128)(2,1)S(1)}, bf16[96,256]{1,0:T(8,128)(2,1)S(1)}, u32[]{:S(2)}, u32[]{:S(2)}) collective-permute-start(bf16[96,256]{1,0:T(8,128)(2,1)S(1)} %get-tuple-element.72), channel_id=1, source_target_pairs={{0,1},{1,0},{2,3},{3,2},{4,5},{5,4},{6,7},{7,6},{8,9},{9,8},{10,11... | collective-permute-start | bytes 147464 | tf_op jit(solution)/shard_map/ppermute | solution.py:197
  43.6 5.9 %collective-permute-start.14 = (bf16[208,256]{1,0:T(8,128)(2,1)S(1)}, bf16[208,256]{1,0:T(8,128)(2,1)S(1)}, u32[]{:S(2)}, u32[]{:S(2)}) collective-permute-start(bf16[208,256]{1,0:T(8,128)(2,1)S(1)} %add_convert_fusion.3), channel_id=1, source_target_pairs={{0,2},{1,3},{2,0},{3,1},{4,6},{5,7},{6,4},{7,5},{8,10},{9,11},{10,... | collective-permute-start | bytes 319496 | tf_op jit(solution)/shard_map/ppermute | solution.py:197
  48.2 1.6 %collective-permute-start.11 = (bf16[192,768]{1,0:T(8,128)(2,1)S(1)}, bf16[192,768]{1,0:T(8,128)(2,1)S(1)}, u32[]{:S(2)}, u32[]{:S(2)}) collective-permute-start(bf16[192,768]{1,0:T(8,128)(2,1)S(1)} %add_convert_fusion.whole_v), channel_id=1, source_target_pairs={{0,1},{1,0},{2,3},{3,2},{4,5},{5,4},{6,7},{7,6},{8,9},{9,8},{10,11... | collective-permute-start | bytes 884744 | tf_op jit(solution)/shard_map/ppermute | solution.py:197
  49.6 1.4 %collective-permute-start.15 = (bf16[208,256]{1,0:T(8,128)(2,1)S(1)}, bf16[208,256]{1,0:T(8,128)(2,1)S(1)}, u32[]{:S(2)}, u32[]{:S(2)}) collective-permute-start(bf16[208,256]{1,0:T(8,128)(2,1)S(1)} %add_convert_fusion.2.whole_k), channel_id=1, source_target_pairs={{0,1},{1,0},{2,3},{3,2},{4,5},{5,4},{6,7},{7,6},{8,9},{9,8},{10,11... | collective-permute-start | bytes 319496 | tf_op jit(solution)/shard_map/ppermute | solution.py:197
